TPU v7x, 32 devices: a whole 2x2x4 slice. The times are simulated.
32 devices in a mesh: dp: 16 (over z, y, x), kv: 2 (over core).
Axes of the slice: x: 2, y: 2, z: 4, core: 2. Of those that a mesh axis runs over, the one named last changes fastest.
Arguments:
- tokens: bfloat16 [256, 64, 768], P(('dp', 'kv')), may hold values from -6 to 6
- images: bfloat16 [256, 576, 768], P('dp', 'kv'), may hold values from -6 to 6
- image_counts: int32 [256], P('dp'), may hold values from 196 to 576, as said below
- cotangent: bfloat16 [256, 64, 768], P(('dp', 'kv')), may hold values from -6 to 6
- norm1_gain: float32 [768], replicated, may hold values from 0.5 to 1.5
- norm1_shift: float32 [768], replicated, may hold values from -3 to 3
- self_qkv: bfloat16 [768, 2304], replicated, may hold values from -0.21875 to 0.21875
- self_out: bfloat16 [768, 768], replicated, may hold values from -0.875 to 0.875
- norm2_gain: float32 [768], replicated, may hold values from 0.5 to 1.5
- norm2_shift: float32 [768], replicated, may hold values from -3 to 3
- cross_q: bfloat16 [768, 768], replicated, may hold values from -0.21875 to 0.21875
- cross_kv: bfloat16 [768, 1536], replicated, may hold values from -0.21875 to 0.21875
- cross_out: bfloat16 [768, 768], replicated, may hold values from -1.75 to 1.75
- norm3_gain: float32 [768], replicated, may hold values from 0.5 to 1.5
- norm3_shift: float32 [768], replicated, may hold values from -3 to 3
- w_up: bfloat16 [768, 3072], replicated, may hold values from -0.21875 to 0.21875
- w_down: bfloat16 [3072, 768], replicated, may hold values from -0.109375 to 0.109375
Outputs:
- layer_out: bfloat16 [256, 64, 768], P(('dp', 'kv'))
- tokens_grad: bfloat16 [256, 64, 768], P(('dp', 'kv'))
- images_grad: bfloat16 [256, 576, 768], P('dp', 'kv')
- norm1_gain_grad: float32 [768], P('kv')
- norm1_shift_grad: float32 [768], P('kv')
- self_qkv_grad: float32 [768, 2304], P('dp', 'kv')
- self_out_grad: float32 [768, 768], P('dp', 'kv')
- norm2_gain_grad: float32 [768], P('kv')
- norm2_shift_grad: float32 [768], P('kv')
- cross_q_grad: float32 [768, 768], P('dp', 'kv')
- cross_kv_grad: float32 [768, 1536], P('dp', 'kv')
- cross_out_grad: float32 [768, 768], P('dp', 'kv')
- norm3_gain_grad: float32 [768], P('kv')
- norm3_shift_grad: float32 [768], P('kv')
- w_up_grad: float32 [768, 3072], P('dp', 'kv')
- down_weight_gradient: float32 [3072, 768], P('dp', 'kv')
Inputs may be any that keep to these rules, and one draw needn't show every extreme that they name: `image_counts`: each caption's image fills its first 196 or all 576 patch slots.
All inputs are finite; a program needn't handle non-finite values.
Results may differ from a plain program's by a relative error of at most 0.02.
Values may be sent and summed in bfloat16 or wider, within the bound.
A program may use at most 256 MiB of HBM per device.

v0:
```python
import jax
import jax.numpy as jnp
from jax import lax
from jax.sharding import PartitionSpec as P

HEADS = 12
HEAD_DIM = 64


def combined_all(part, axis, combine):
    gathered = jax.tree.map(lambda a: lax.all_gather(a, axis), part)

    def take(source):
        return jax.tree.map(lambda a: lax.dynamic_index_in_dim(a, source, 0, False), gathered)

    return lax.fori_loop(
        1, lax.axis_size(axis), lambda source, state: combine(state, take(source)), take(0)
    )


def layer_norm(values, gain, shift):
    centered = values - jnp.mean(values, axis=-1, keepdims=True)
    variance = jnp.mean(centered * centered, axis=-1, keepdims=True)
    return centered * lax.rsqrt(variance + 1e-05) * gain + shift


def exact_gelu_activation(values):
    return 0.5 * values * (1.0 + jax.scipy.special.erf(values * 0.7071067811865476))


def softmax_rows(scores):
    peak = jnp.max(scores, axis=-1, keepdims=True)
    exponent = jnp.exp(scores - peak)
    return exponent / jnp.sum(exponent, axis=-1, keepdims=True)


def cross_partial(queries, keys, values, valid, score_scale):
    scores = (
        jnp.einsum("cqhd,cphd->cqhp", queries, keys, preferred_element_type=jnp.float32)
        * score_scale
    )
    mask_wide = valid[:, None, None, :]
    masked = jnp.where(mask_wide, scores, -1e30)
    row_peak = jnp.max(masked, axis=-1)
    weights = jnp.where(mask_wide, jnp.exp(masked - row_peak[..., None]), 0.0)
    row_total = jnp.sum(weights, axis=-1)
    numerator = jnp.einsum(
        "cqhp,cphd->cqhd", weights, values.astype(jnp.float32), precision=lax.Precision.HIGHEST
    )
    return (row_peak, row_total, numerator.reshape(numerator.shape[0], numerator.shape[1], -1))


def combine_parts(first, second):
    peak_one, total_one, numer_one = first
    peak_two, total_two, numer_two = second
    peak_both = jnp.maximum(peak_one, peak_two)
    factor_one = jnp.exp(peak_one - peak_both)
    factor_two = jnp.exp(peak_two - peak_both)
    head_width = numer_one.shape[-1] // peak_one.shape[-1]
    split_shape = peak_one.shape + (head_width,)
    numerator = (
        numer_one.reshape(split_shape) * factor_one[..., None]
        + numer_two.reshape(split_shape) * factor_two[..., None]
    ).reshape(numer_one.shape)
    return (peak_both, total_one * factor_one + total_two * factor_two, numerator)


def cross_back(queries, keys, values, valid, log_total, delta, grad_att, score_scale):
    scores = (
        jnp.einsum("cqhd,cphd->cqhp", queries, keys, preferred_element_type=jnp.float32)
        * score_scale
    )
    probs = jnp.where(valid[:, None, None, :], jnp.exp(scores - log_total[..., None]), 0.0)
    grad_probs = jnp.einsum("cqhd,cphd->cqhp", grad_att, values, preferred_element_type=jnp.float32)
    grad_scores = (probs * (grad_probs - delta[..., None])).astype(jnp.bfloat16)
    grad_queries = (
        jnp.einsum("cqhp,cphd->cqhd", grad_scores, keys, preferred_element_type=jnp.float32)
        * score_scale
    )
    grad_keys = (
        jnp.einsum("cqhp,cqhd->cphd", grad_scores, queries, preferred_element_type=jnp.float32)
        * score_scale
    )
    grad_values = jnp.einsum(
        "cqhp,cqhd->cphd", probs, grad_att.astype(jnp.float32), precision=lax.Precision.HIGHEST
    )
    return (grad_queries, grad_keys, grad_values)


def body(
    tokens,
    images,
    image_counts,
    cotangent,
    norm1_gain,
    norm1_shift,
    self_qkv,
    self_out,
    norm2_gain,
    norm2_shift,
    cross_q,
    cross_kv,
    cross_out,
    norm3_gain,
    norm3_shift,
    w_up,
    w_down,
):
    captions, seq_len, model_width = tokens.shape
    head_count = HEADS
    head_width = HEAD_DIM
    score_scale = head_width ** (-0.5)
    row_count = captions * seq_len
    kv_index = lax.axis_index("kv")
    group_caps, slot_count, _ = images.shape
    hidden_input_rows = tokens.astype(jnp.float32).reshape(row_count, model_width)
    normed_one = layer_norm(hidden_input_rows, norm1_gain, norm1_shift).astype(jnp.bfloat16)
    qkv_all = jnp.dot(normed_one, self_qkv, preferred_element_type=jnp.float32).astype(jnp.bfloat16)
    qkv_all = qkv_all.reshape(captions, seq_len, 3, head_count, head_width)
    self_query = qkv_all[:, :, 0]
    self_key = qkv_all[:, :, 1]
    self_value = qkv_all[:, :, 2]
    raw_self = (
        jnp.einsum("bqhd,bkhd->bhqk", self_query, self_key, preferred_element_type=jnp.float32)
        * score_scale
    )
    causal = lax.broadcasted_iota(jnp.int32, (seq_len, seq_len), 0) >= lax.broadcasted_iota(
        jnp.int32, (seq_len, seq_len), 1
    )
    self_probs = softmax_rows(jnp.where(causal, raw_self, -1e30))
    probs_low = self_probs.astype(jnp.bfloat16)
    self_att = jnp.einsum(
        "bhqk,bkhd->bqhd", probs_low, self_value, preferred_element_type=jnp.float32
    )
    self_att = self_att.astype(jnp.bfloat16).reshape(row_count, model_width)
    hidden_one = hidden_input_rows + jnp.dot(self_att, self_out, preferred_element_type=jnp.float32)
    normed_two = layer_norm(hidden_one, norm2_gain, norm2_shift).astype(jnp.bfloat16)
    cross_query = jnp.dot(normed_two, cross_q, preferred_element_type=jnp.float32).astype(
        jnp.bfloat16
    )
    gathered = lax.all_gather(cross_query, "kv", axis=0, tiled=True)
    att_queries = gathered.reshape(group_caps, seq_len, head_count, head_width)
    positions = kv_index * slot_count + lax.broadcasted_iota(jnp.int32, (group_caps, slot_count), 1)
    valid = positions < image_counts[:, None]
    picture_count, picture_slots, _ = images.shape
    image_kv = jnp.dot(
        images.reshape(picture_count * picture_slots, model_width),
        cross_kv,
        preferred_element_type=jnp.float32,
    ).astype(jnp.bfloat16)
    image_kv = image_kv.reshape(picture_count, picture_slots, 2, head_count, head_width)
    image_keys = image_kv[:, :, 0]
    image_values = image_kv[:, :, 1]
    row_peak, row_total, numerator = cross_partial(
        att_queries, image_keys, image_values, valid, score_scale
    )
    row_peak, row_total, numerator = combined_all(
        (row_peak, row_total, numerator), "kv", combine_parts
    )
    row_peak = lax.dynamic_slice_in_dim(row_peak, kv_index * captions, captions, 0)
    row_total = lax.dynamic_slice_in_dim(row_total, kv_index * captions, captions, 0)
    numerator = lax.dynamic_slice_in_dim(numerator, kv_index * captions, captions, 0)
    cross_att = numerator.reshape(captions, seq_len, head_count, head_width) / row_total[..., None]
    log_total = row_peak + jnp.log(row_total)
    cross_low = cross_att.reshape(row_count, model_width).astype(jnp.bfloat16)
    hidden_two = hidden_one + jnp.dot(cross_low, cross_out, preferred_element_type=jnp.float32)
    normed_three = layer_norm(hidden_two, norm3_gain, norm3_shift).astype(jnp.bfloat16)
    up_pre = jnp.dot(normed_three, w_up, preferred_element_type=jnp.float32)
    activated_f32, gelu_pullback = jax.vjp(exact_gelu_activation, up_pre)
    activated = activated_f32.astype(jnp.bfloat16)
    layer_out = hidden_two + jnp.dot(activated, w_down, preferred_element_type=jnp.float32)
    layer_out = layer_out.astype(jnp.bfloat16).reshape(captions, seq_len, model_width)
    grad_low = cotangent.reshape(row_count, model_width)
    grad_out = grad_low.astype(jnp.float32)
    down_weight_gradient = jnp.einsum(
        "rk,rn->kn", activated, grad_low, preferred_element_type=jnp.float32
    )
    grad_act = jnp.einsum("rn,kn->rk", grad_low, w_down, preferred_element_type=jnp.float32)
    grad_up = gelu_pullback(grad_act)[0].astype(jnp.bfloat16)
    w_up_grad = jnp.einsum("rd,rf->df", normed_three, grad_up, preferred_element_type=jnp.float32)
    grad_normed3 = jnp.einsum("rf,df->rd", grad_up, w_up, preferred_element_type=jnp.float32)
    _, norm_three_back = jax.vjp(layer_norm, hidden_two, norm3_gain, norm3_shift)
    input_part3, norm3_gain_grad, norm3_shift_grad = norm_three_back(grad_normed3)
    grad_two = grad_out + input_part3
    grad_branch2 = grad_two.astype(jnp.bfloat16)
    cross_out_grad = jnp.einsum(
        "rd,rn->dn", cross_low, grad_branch2, preferred_element_type=jnp.float32
    )
    grad_catt = jnp.einsum(
        "rn,dn->rd", grad_branch2, cross_out, preferred_element_type=jnp.float32
    ).astype(jnp.bfloat16)
    grad_catt = grad_catt.reshape(captions, seq_len, head_count, head_width)
    cross_delta = jnp.sum(grad_catt.astype(jnp.float32) * cross_att, axis=-1)
    grad_all = lax.all_gather(grad_catt, "kv", axis=0, tiled=True)
    log_all, delta_all = (
        lax.all_gather(log_total, "kv", axis=0, tiled=True),
        lax.all_gather(cross_delta, "kv", axis=0, tiled=True),
    )
    grad_queries, grad_keys, grad_values = cross_back(
        att_queries, image_keys, image_values, valid, log_all, delta_all, grad_all, score_scale
    )
    grad_cquery = lax.psum_scatter(
        grad_queries.reshape(group_caps * seq_len, model_width).astype(jnp.bfloat16),
        "kv",
        scatter_dimension=0,
        tiled=True,
    ).astype(jnp.float32)
    grad_ckv = jnp.stack([grad_keys, grad_values], axis=2).astype(jnp.bfloat16)
    grad_ckv = grad_ckv.reshape(picture_count * picture_slots, 2 * model_width)
    cross_kv_grad = jnp.einsum(
        "rd,rk->dk",
        images.reshape(picture_count * picture_slots, model_width),
        grad_ckv,
        preferred_element_type=jnp.float32,
    )
    images_grad = jnp.einsum("rk,dk->rd", grad_ckv, cross_kv, preferred_element_type=jnp.float32)
    images_grad = images_grad.astype(jnp.bfloat16).reshape(
        picture_count, picture_slots, model_width
    )
    grad_cquery = grad_cquery.astype(jnp.bfloat16)
    cross_q_grad = jnp.einsum(
        "rd,rn->dn", normed_two, grad_cquery, preferred_element_type=jnp.float32
    )
    grad_normed2 = jnp.einsum("rn,dn->rd", grad_cquery, cross_q, preferred_element_type=jnp.float32)
    _, norm_two_back = jax.vjp(layer_norm, hidden_one, norm2_gain, norm2_shift)
    input_part2, norm2_gain_grad, norm2_shift_grad = norm_two_back(grad_normed2)
    grad_one = grad_two + input_part2
    first_branch_gradient = grad_one.astype(jnp.bfloat16)
    self_out_grad = jnp.einsum(
        "rd,rn->dn", self_att, first_branch_gradient, preferred_element_type=jnp.float32
    )
    grad_satt = jnp.einsum(
        "rn,dn->rd", first_branch_gradient, self_out, preferred_element_type=jnp.float32
    ).astype(jnp.bfloat16)
    grad_satt = grad_satt.reshape(captions, seq_len, head_count, head_width)
    grad_sprobs = jnp.einsum(
        "bqhd,bkhd->bhqk", grad_satt, self_value, preferred_element_type=jnp.float32
    )
    grad_sscore = (
        self_probs * (grad_sprobs - jnp.sum(self_probs * grad_sprobs, axis=-1, keepdims=True))
    ).astype(jnp.bfloat16)
    self_attention_query_gradient = (
        jnp.einsum("bhqk,bkhd->bqhd", grad_sscore, self_key, preferred_element_type=jnp.float32)
        * score_scale
    )
    self_attention_key_gradient = (
        jnp.einsum("bhqk,bqhd->bkhd", grad_sscore, self_query, preferred_element_type=jnp.float32)
        * score_scale
    )
    self_attention_value_gradient = jnp.einsum(
        "bhqk,bqhd->bkhd", probs_low, grad_satt, preferred_element_type=jnp.float32
    )
    query_key_value_gradient = jnp.stack(
        [self_attention_query_gradient, self_attention_key_gradient, self_attention_value_gradient],
        axis=2,
    ).astype(jnp.bfloat16)
    query_key_value_gradient = query_key_value_gradient.reshape(row_count, 3 * model_width)
    self_qkv_grad = jnp.einsum(
        "rd,rk->dk", normed_one, query_key_value_gradient, preferred_element_type=jnp.float32
    )
    grad_normed1 = jnp.einsum(
        "rk,dk->rd", query_key_value_gradient, self_qkv, preferred_element_type=jnp.float32
    )
    _, norm_one_back = jax.vjp(layer_norm, hidden_input_rows, norm1_gain, norm1_shift)
    input_part1, norm1_gain_grad, norm1_shift_grad = norm_one_back(grad_normed1)
    tokens_grad = (
        (grad_one + input_part1).astype(jnp.bfloat16).reshape(captions, seq_len, model_width)
    )
    gain_terms = jnp.stack(
        [
            norm1_gain_grad,
            norm1_shift_grad,
            norm2_gain_grad,
            norm2_shift_grad,
            norm3_gain_grad,
            norm3_shift_grad,
        ],
        axis=0,
    )
    (
        self_qkv_grad,
        self_out_grad,
        cross_q_grad,
        cross_kv_grad,
        cross_out_grad,
        w_up_grad,
        down_weight_gradient,
        gain_terms,
    ) = (
        lax.psum_scatter(
            self_qkv_grad.astype(jnp.bfloat16), "kv", scatter_dimension=1, tiled=True
        ).astype(jnp.float32),
        lax.psum_scatter(
            self_out_grad.astype(jnp.bfloat16), "kv", scatter_dimension=1, tiled=True
        ).astype(jnp.float32),
        lax.psum_scatter(
            cross_q_grad.astype(jnp.bfloat16), "kv", scatter_dimension=1, tiled=True
        ).astype(jnp.float32),
        lax.psum_scatter(
            cross_kv_grad.astype(jnp.bfloat16), "kv", scatter_dimension=1, tiled=True
        ).astype(jnp.float32),
        lax.psum_scatter(
            cross_out_grad.astype(jnp.bfloat16), "kv", scatter_dimension=1, tiled=True
        ).astype(jnp.float32),
        lax.psum_scatter(
            w_up_grad.astype(jnp.bfloat16), "kv", scatter_dimension=1, tiled=True
        ).astype(jnp.float32),
        lax.psum_scatter(
            down_weight_gradient.astype(jnp.bfloat16), "kv", scatter_dimension=1, tiled=True
        ).astype(jnp.float32),
        lax.psum_scatter(
            gain_terms.astype(jnp.bfloat16), "kv", scatter_dimension=1, tiled=True
        ).astype(jnp.float32),
    )
    (
        self_qkv_grad,
        self_out_grad,
        cross_q_grad,
        cross_kv_grad,
        cross_out_grad,
        w_up_grad,
        down_weight_gradient,
    ) = (
        lax.psum_scatter(self_qkv_grad, "dp", scatter_dimension=0, tiled=True),
        lax.psum_scatter(self_out_grad, "dp", scatter_dimension=0, tiled=True),
        lax.psum_scatter(cross_q_grad, "dp", scatter_dimension=0, tiled=True),
        lax.psum_scatter(cross_kv_grad, "dp", scatter_dimension=0, tiled=True),
        lax.psum_scatter(cross_out_grad, "dp", scatter_dimension=0, tiled=True),
        lax.psum_scatter(w_up_grad, "dp", scatter_dimension=0, tiled=True),
        lax.psum_scatter(down_weight_gradient, "dp", scatter_dimension=0, tiled=True),
    )
    gain_terms = lax.psum(gain_terms, "dp")
    return (
        layer_out,
        tokens_grad,
        images_grad,
        gain_terms[0],
        gain_terms[1],
        self_qkv_grad,
        self_out_grad,
        gain_terms[2],
        gain_terms[3],
        cross_q_grad,
        cross_kv_grad,
        cross_out_grad,
        gain_terms[4],
        gain_terms[5],
        w_up_grad,
        down_weight_gradient,
    )


def solution(mesh):
    return jax.shard_map(
        body,
        mesh=mesh,
        in_specs=(
            P(("dp", "kv"), None, None),
            P("dp", "kv", None),
            P("dp"),
            P(("dp", "kv"), None, None),
            P(),
            P(),
            P(),
            P(),
            P(),
            P(),
            P(),
            P(),
            P(),
            P(),
            P(),
            P(),
            P(),
        ),
        out_specs=(
            P(("dp", "kv"), None, None),
            P(("dp", "kv"), None, None),
            P("dp", "kv", None),
            P("kv"),
            P("kv"),
            P("dp", "kv"),
            P("dp", "kv"),
            P("kv"),
            P("kv"),
            P("dp", "kv"),
            P("dp", "kv"),
            P("dp", "kv"),
            P("kv"),
            P("kv"),
            P("dp", "kv"),
            P("dp", "kv"),
        ),
        check_vma=False,
    )
```

profile of v0, /device:TPU:2, one launch (start us, length us, event | category | flops | bytes accessed | tf_op | source)
XLA Modules:
  0.0 1585.0 jit_solution(8560638861241691844)
XLA Ops:
  21.4 7.0 reshape.315
  56.9 17.0 %convolution_convert_fusion = bf16[4608,1536]{1,0:T(8,128)(2,1)} fusion(bf16[4608,768]{1,0:T(8,128)(2,1)} %bitcast.231, bf16[768,1536]{1,0:T(8,128)(2,1)} %param.28), kind=kOutput, calls=%fused_computation.2 | convolution fusion | flops 10878713856 | bytes 23592960 | tf_op jit(solution)/shard_map/dot_general | solution.py:146
  73.9 45.5 %reshape.360 = bf16[16,288,2,12,64]{4,3,2,1,0:T(8,128)(2,1)} reshape(bf16[4608,1536]{1,0:T(8,128)(2,1)} %convolution_convert_fusion) | data formatting | bytes 28311552 | tf_op jit(solution)/shard_map/reshape | solution.py:151
  119.4 25.6 %fusion.85 = (bf16[16,288,1,12,64]{4,3,2,1,0:T(8,128)(2,1)}, bf16[16,288,1,12,64]{4,3,2,1,0:T(8,128)(2,1)}) fusion(bf16[16,288,2,12,64]{4,3,2,1,0:T(8,128)(2,1)} %reshape.360), kind=kLoop, calls=%fused_computation.164 | loop fusion | bytes 28311552 | tf_op jit(solution)/shard_map/slice | solution.py:153
  145.0 24.5 %copy.241 = bf16[16,288,1,12,64]{1,4,3,0,2:T(8,128)(2,1)} copy(bf16[16,288,1,12,64]{4,3,2,1,0:T(8,128)(2,1)} %get-tuple-element.145) | data formatting | bytes 14155776
  169.5 24.5 %copy.240 = bf16[16,288,1,12,64]{1,4,3,0,2:T(8,128)(2,1)} copy(bf16[16,288,1,12,64]{4,3,2,1,0:T(8,128)(2,1)} %get-tuple-element.144) | data formatting | bytes 14155776
  206.4 16.0 %fusion.5 = (f32[16,64,12]{1,2,0:T(8,128)}, f32[16,12,288,64]{2,3,1,0:T(8,128)}) fusion(pred[16,288]{1,0:T(8,128)(4,1)S(1)} %broadcast_compare_fusion, bf16[16,64,12,64]{1,3,2,0:T(8,128)(2,1)} %copy.205, bf16[16,288,1,12,64]{1,4,3,0,2:T(8,128)(2,1)} %copy.241), kind=kOutput, calls=%fused_computation.12 | convolution fusion | flops 463589376 | bytes 22860288 | tf_op jit(solution)/shard_map/cqhd,cphd->cqhp/dot_general | solution.py:39
  222.4 22.2 %fusion.9 = f32[16,12,64,64]{3,2,1,0:T(8,128)} fusion(f32[16,12,288,64]{2,3,1,0:T(8,128)} %get-tuple-element.162, bf16[16,288,1,12,64]{1,4,3,0,2:T(8,128)(2,1)} %copy.240, f32[16,64,12]{1,2,0:T(8,128)} %get-tuple-element.161, pred[16,288]{1,0:T(8,128)(4,1)S(1)} %broadcast_compare_fusion), kind=kOutput, calls=%fused_computation.15 | convolution fusion | flops 2732064768 | bytes 24433152 | tf_op jit(solution)/shard_map/cqhp,cphd->cqhd/dot_general | solution.py:47
  263.6 7.1 mul.333
  278.5 7.2 mul.330
  285.8 9.1 fusion.8
  356.5 12.7 fusion.2
  369.2 10.5 fusion.31
  396.7 11.7 multiply_bitcast_fusion
  408.5 21.5 %fusion.28 = bf16[16,288,1,12,64]{1,4,3,0,2:T(8,128)(2,1)} fusion(bf16[16,64,12,64]{3,1,2,0:T(8,128)(2,1)} %all-gather.10.cloned.1.call-done, f32[16,12,288,64]{2,3,1,0:T(8,128)} %get-tuple-element.162, f32[16,64,12]{1,2,0:T(8,128)} %copy.186, pred[16,288]{1,0:T(8,128)(4,1)S(1)} %broadcast_compare_fusion), kind=kOutput, calls=%fused_computation.34 | convolution fusion | flops 2728525824 | bytes 22860288 | tf_op jit(solution)/shard_map/cqhp,cqhd->cphd/dot_general | solution.py:84
  436.2 11.4 maximum_convert_fusion
  447.6 14.6 copy.207
  462.3 29.4 %convert_element_type.196 = bf16[4608,1536]{0,1:T(8,128)(2,1)} reshape(bf16[16,288,2,12,64]{1,0,4,3,2:T(8,128)(2,1)} %copy.207) | data formatting | bytes 28311552 | tf_op jit(solution)/shard_map/convert_element_type | solution.py:208
  503.1 16.8 %fusion.32 = bf16[768,1536]{0,1:T(8,128)(2,1)} fusion(bf16[4608,1536]{0,1:T(8,128)(2,1)} %convert_element_type.196, bf16[4608,768]{1,0:T(8,128)(2,1)} %bitcast.232), kind=kOutput, calls=%fused_computation.54 | convolution fusion | flops 10872815616 | bytes 23592960 | tf_op jit(solution)/shard_map/rd,rk->dk/dot_general | solution.py:210
  546.7 7.0 copy.204
  553.7 7.4 convert_element_type.193
  573.3 7.9 convolution_convert_fusion.3
  644.9 7.4 add_convert_fusion.2
  652.3 16.5 %convolution_convert_fusion.1 = bf16[4608,768]{1,0:T(8,128)(2,1)} fusion(bf16[4608,1536]{0,1:T(8,128)(2,1)} %convert_element_type.196, bf16[768,1536]{1,0:T(8,128)(2,1)S(1)} %copy-done.69), kind=kOutput, calls=%fused_computation.33 | convolution fusion | flops 10875174912 | bytes 23592960 | tf_op jit(solution)/shard_map/rk,dk->rd/dot_general | solution.py:216
  671.9 71.8 %psum.7 = f32[6,384]{1,0:T(8,128)S(1)} all-reduce(bf16[6,384]{1,0:T(8,128)(2,1)} %copy.222), channel_id=1, replica_groups=mesh['dp'=16,'kv'=2] {'dp'}, use_global_device_ids=true, to_apply=%region_26.27 | all-reduce | flops 2304 | bytes 13824 | tf_op jit(solution)/shard_map/psum | solution.py:332
  744.3 16.2 %reduce-scatter.41.cloned.1.call-done = f32[48,384]{1,0:T(8,128)} async-done(((f32[768,384]{1,0:T(8,128)}), f32[48,384]{1,0:T(8,128)}) %reduce-scatter.41.cloned.1.call-update) | async-done | bytes 73744 | tf_op jit(solution)/shard_map/reduce_scatter | solution.py:328
  760.5 129.2 %reduce-scatter.37.cloned.1.call-done = f32[48,384]{1,0:T(8,128)} async-done(((f32[768,384]{1,0:T(8,128)}), f32[48,384]{1,0:T(8,128)}) %reduce-scatter.37.cloned.1.call-update) | async-done | bytes 73744 | tf_op jit(solution)/shard_map/reduce_scatter | solution.py:326
  889.7 129.2 %reduce-scatter.35.cloned.1.call-done = f32[48,384]{1,0:T(8,128)} async-done(((f32[768,384]{1,0:T(8,128)}), f32[48,384]{1,0:T(8,128)}) %reduce-scatter.35.cloned.1.call-update) | async-done | bytes 73744 | tf_op jit(solution)/shard_map/reduce_scatter | solution.py:325
  1018.9 133.4 %reduce-scatter.57.cloned.1.call-done = f32[48,768]{1,0:T(8,128)} async-done(((f32[768,768]{1,0:T(8,128)}), f32[48,768]{1,0:T(8,128)}) %reduce-scatter.57.cloned.1.call-update) | async-done | bytes 147472
  1152.2 139.2 %reduce-scatter.33.cloned.1.call-done = f32[48,1152]{1,0:T(8,128)} async-done(((f32[768,1152]{1,0:T(8,128)}), f32[48,1152]{1,0:T(8,128)}) %reduce-scatter.33.cloned.1.call-update) | async-done | bytes 221200 | tf_op jit(solution)/shard_map/reduce_scatter | solution.py:324
  1291.4 143.4 %reduce-scatter.45.cloned.1.call-done = f32[48,1536]{1,0:T(8,128)} async-done(((f32[768,1536]{1,0:T(8,128)}), f32[48,1536]{1,0:T(8,128)}) %reduce-scatter.45.cloned.1.call-update) | async-done | bytes 294928 | tf_op jit(solution)/shard_map/reduce_scatter | solution.py:329
  1434.8 143.5 %reduce-scatter.47.cloned.1.call-done = f32[192,384]{1,0:T(8,128)} async-done(((f32[3072,384]{1,0:T(8,128)}), f32[192,384]{1,0:T(8,128)}) %reduce-scatter.47.cloned.1.call-update) | async-done | bytes 294928 | tf_op jit(solution)/shard_map/reduce_scatter | solution.py:330
  (330 shorter events, 283.7 us)
Async XLA Ops:
  7.2 186.8 %all-gather.6.cloned.1.call-start = ((), (), s32[]{:S(2)}) async-start(), calls=%async_computation.16 | async-start | bytes 2359296 | tf_op jit(solution)/shard_map/all_gather | solution.py:141
  56.7 250.1 %all-gather.8.cloned.1.call-start = ((), (), s32[]{:S(2)}) async-start(), calls=%async_computation.17 | async-start | bytes 9437184 | tf_op jit(solution)/shard_map/all_gather | solution.py:11
  169.5 24.5 %copy-start.68 = (s32[16]{0:T(128)S(1)}, s32[16]{0:T(128)}, u32[]{:S(2)}) copy-start(s32[16]{0:T(128)} %param.19) | copy-start | bytes 196
  250.8 105.7 %all-gather.10.cloned.1.call-start = ((), (), s32[]{:S(2)}) async-start(), calls=%async_computation.18 | async-start | bytes 4718592 | tf_op jit(solution)/shard_map/all_gather | solution.py:194
  285.7 11.1 copy-start.30
  285.7 11.1 copy-start.31
  285.7 11.1 copy-start.33
  316.1 13.3 copy-start.6
  316.8 12.6 copy-start.55
  342.6 87.4 %reduce-scatter.31.cloned.1.call-start = ((), (), s32[]{:S(2)}) async-start(), calls=%async_computation.19 | async-start | bytes 2359296 | tf_op jit(solution)/shard_map/reduce_scatter | solution.py:202
  391.0 217.0 %reduce-scatter.59.cloned.1.call-start = ((), (), s32[]{:S(2)}) async-start(), calls=%async_computation.33 | async-start | bytes 1769472
  396.7 215.8 %reduce-scatter.55.cloned.1.call-start = ((), (), s32[]{:S(2)}) async-start(), calls=%async_computation.31 | async-start | bytes 1769472
  408.5 21.5 %copy-start.45 = (f32[512]{0:T(512)S(1)}, f32[512]{0:T(512)}, u32[]{:S(2)}) copy-start(f32[512]{0:T(512)} %copy-done.44) | copy-start | bytes 6148
  436.1 180.9 %reduce-scatter.53.cloned.1.call-start = ((), (), s32[]{:S(2)}) async-start(), calls=%async_computation.30 | async-start | bytes 1769472
  462.3 29.4 %copy-start.54 = (f32[512]{0:T(512)S(1)}, f32[512]{0:T(512)}, u32[]{:S(2)}) copy-start(f32[512]{0:T(512)} %copy-done.53) | copy-start | bytes 6148
  462.3 29.4 %copy-start.60 = (f32[768]{0:T(1024)S(1)}, f32[768]{0:T(1024)}, u32[]{:S(2)}) copy-start(f32[768]{0:T(1024)} %param.25) | copy-start | bytes 9220
  503.0 118.4 %reduce-scatter.39.cloned.1.call-start = ((), (), s32[]{:S(2)}) async-start(), calls=%async_computation.23 | async-start | bytes 3538944 | tf_op jit(solution)/shard_map/reduce_scatter | solution.py:299
  520.0 104.3 %reduce-scatter.51.cloned.1.call-start = ((), (), s32[]{:S(2)}) async-start(), calls=%async_computation.29 | async-start | bytes 5308416
  572.6 59.2 %reduce-scatter.43.cloned.1.call-start = ((), (), s32[]{:S(2)}) async-start(), calls=%async_computation.25 | async-start | bytes 7077888 | tf_op jit(solution)/shard_map/reduce_scatter | solution.py:305
  581.2 55.3 %reduce-scatter.61.cloned.1.call-start = ((), (), s32[]{:S(2)}) async-start(), calls=%async_computation.34 | async-start | bytes 7077888
  594.9 75.4 %reduce-scatter.49.cloned.1.call-start = ((), (), s32[]{:S(2)}) async-start(), calls=%async_computation.28 | async-start | bytes 294912
  608.0 152.5 %reduce-scatter.41.cloned.1.call-start = ((), (), s32[]{:S(2)}) async-start(), calls=%async_computation.24 | async-start | bytes 1253376 | tf_op jit(solution)/shard_map/reduce_scatter | solution.py:328
  612.4 277.2 %reduce-scatter.37.cloned.1.call-start = ((), (), s32[]{:S(2)}) async-start(), calls=%async_computation.22 | async-start | bytes 1253376 | tf_op jit(solution)/shard_map/reduce_scatter | solution.py:326
  617.0 401.9 %reduce-scatter.35.cloned.1.call-start = ((), (), s32[]{:S(2)}) async-start(), calls=%async_computation.21 | async-start | bytes 1253376 | tf_op jit(solution)/shard_map/reduce_scatter | solution.py:325
  621.4 530.9 %reduce-scatter.57.cloned.1.call-start = ((), (), s32[]{:S(2)}) async-start(), calls=%async_computation.32 | async-start | bytes 2506752
  624.2 667.2 %reduce-scatter.33.cloned.1.call-start = ((), (), s32[]{:S(2)}) async-start(), calls=%async_computation.20 | async-start | bytes 3760128 | tf_op jit(solution)/shard_map/reduce_scatter | solution.py:324
  631.7 803.1 %reduce-scatter.45.cloned.1.call-start = ((), (), s32[]{:S(2)}) async-start(), calls=%async_computation.26 | async-start | bytes 5013504 | tf_op jit(solution)/shard_map/reduce_scatter | solution.py:329
  636.3 942.0 %reduce-scatter.47.cloned.1.call-start = ((), (), s32[]{:S(2)}) async-start(), calls=%async_computation.27 | async-start | bytes 5013504 | tf_op jit(solution)/shard_map/reduce_scatter | solution.py:330
  652.3 16.5 %copy-start.58 = (f32[512]{0:T(512)S(1)}, f32[512]{0:T(512)}, u32[]{:S(2)}) copy-start(f32[512]{0:T(512)} %get-tuple-element.125) | copy-start | bytes 6148
  652.3 16.5 %copy-start.3 = (bf16[8,64,768]{2,1,0:T(8,128)(2,1)S(1)}, bf16[8,64,768]{2,1,0:T(8,128)(2,1)}, u32[]{:S(2)}) copy-start(bf16[8,64,768]{2,1,0:T(8,128)(2,1)} %param.17) | copy-start | bytes 2359300
  652.3 16.5 %copy-start.5 = (f32[512,768]{1,0:T(8,128)S(1)}, f32[512,768]{1,0:T(8,128)}, u32[]{:S(2)}) copy-start(f32[512,768]{1,0:T(8,128)} %copy-done.4) | copy-start | bytes 4718596
  652.3 16.5 %copy-start.19 = (f32[512,768]{1,0:T(8,128)S(1)}, f32[512,768]{1,0:T(8,128)}, u32[]{:S(2)}) copy-start(f32[512,768]{1,0:T(8,128)} %copy-done.18) | copy-start | bytes 4718596
  (65 other events, 184.7 us)
Sparse Core Ops, SparseCore 0:
  56.8 11.2 all-gather.5
  250.9 18.2 all-gather.7
  342.7 13.7 all-gather.9
  391.2 10.2 reduce-scatter.30
  403.6 9.7 reduce-scatter.58
  436.2 9.8 reduce-scatter.54
  503.2 9.8 reduce-scatter.52
  520.1 11.4 reduce-scatter.38
  572.7 13.0 reduce-scatter.50
  588.5 13.6 reduce-scatter.42
  604.5 13.7 reduce-scatter.60
  620.4 8.7 reduce-scatter.48
  634.5 125.8 reduce-scatter.40
  765.6 123.9 reduce-scatter.36
  894.8 123.9 reduce-scatter.34
  1024.2 127.9 reduce-scatter.56
  1157.8 133.6 reduce-scatter.32
  1297.0 137.7 reduce-scatter.44
  1440.6 137.6 reduce-scatter.46
where the time goes:
time: 1600 us; the launch traced here: 1590 us
  waiting for transfers between devices  836 us (52%)
  local copies, waits for them, and re-layouts  363 us (23%)
  matrix products  226 us (14%)
  blocking collectives  79.6 us (5%)
  other arithmetic  63.5 us (4%)
    reduce_scatter x1, waiting for transfers between devices, body(): lax.psum_scatter(down_weight_gradient, 'dp', scatter_dimension=0, tiled=T...  143 us
    reduce_scatter x1, waiting for transfers between devices, body(): lax.psum_scatter(w_up_grad, 'dp', scatter_dimension=0, tiled=True)  143 us
    reduce_scatter x1, waiting for transfers between devices, body(): lax.psum_scatter(self_qkv_grad, 'dp', scatter_dimension=0, tiled=True)  139 us
    unnamed x26, waiting for transfers between devices  134 us
    reduce_scatter x1, waiting for transfers between devices, body(): lax.psum_scatter(self_out_grad, 'dp', scatter_dimension=0, tiled=True)  129 us
    reduce_scatter x1, waiting for transfers between devices, body(): lax.psum_scatter(cross_q_grad, 'dp', scatter_dimension=0, tiled=True)  129 us
    unnamed x173, local copies, waits for them, and re-layouts  111 us
    psum x1, blocking collectives, body(): gain_terms = lax.psum(gain_terms, 'dp')  71.8 us
  transfers between devices with their start and end apart: 19, of which 8 were waited for; matrix products, arithmetic and copies ran while one was open for 30% of the time, Pallas kernels for 0%

commit v1 on v0

v1 whole, which is shorter than its diff:
```python
import functools
import math

import jax
import jax.numpy as jnp
from jax import lax
from jax.experimental import pallas as pl
from jax.experimental.pallas import tpu as pltpu
from jax.sharding import PartitionSpec as P

HEADS = 12
HEAD_DIM = 64
SHORT = 196
LANES = 256
PACK = LANES // HEAD_DIM
GROUPS = HEADS // PACK
SCALE = HEAD_DIM ** (-0.5)
NEG = -1e30
F32 = jnp.float32
BF16 = jnp.bfloat16
VMEM_LIMIT = 60 * 1024 * 1024


def dot(a, b):
    return jnp.dot(a, b, preferred_element_type=F32)


def dot_nt(a, b):
    return lax.dot_general(a, b, (((1,), (1,)), ((), ())), preferred_element_type=F32)


def dot_tn(a, b):
    return lax.dot_general(a, b, (((0,), (0,)), ((), ())), preferred_element_type=F32)


def normalize(values):
    centered = values - jnp.mean(values, axis=-1, keepdims=True)
    inverse = lax.rsqrt(jnp.mean(centered * centered, axis=-1, keepdims=True) + 1e-05)
    return centered * inverse, inverse


def norm_back(grad, gain, unit, inverse):
    scaled = grad * gain
    mean_one = jnp.mean(scaled, axis=-1, keepdims=True)
    mean_two = jnp.mean(scaled * unit, axis=-1, keepdims=True)
    return (scaled - mean_one - unit * mean_two) * inverse


def iota(shape, dim):
    return lax.broadcasted_iota(jnp.int32, shape, dim)


def same_head():
    shape = (LANES, LANES)
    return (iota(shape, 0) // HEAD_DIM) == (iota(shape, 1) // HEAD_DIM)


def spread(rows, mask):
    stacked = jnp.concatenate([rows] * PACK, axis=0)
    return jnp.where(mask, stacked, jnp.zeros_like(stacked))


def gather_heads(full):
    count = full.shape[0] // PACK
    head = iota((count, LANES), 1) // HEAD_DIM
    out = full[:count]
    for index in range(1, PACK):
        out = jnp.where(head == index, full[index * count : (index + 1) * count], out)
    return out


def split_two(value):
    high = value.astype(BF16)
    return high, (value - high.astype(F32)).astype(BF16)


def lanes_to_rows(row, mask_low):
    shape = (HEAD_DIM, LANES)
    pick = iota(shape, 0) == (iota(shape, 1) % HEAD_DIM)
    high, low = split_two(jnp.where(pick, row, 0.0))
    return dot(high, mask_low) + dot(low, mask_low)


def rows_to_lanes(rows, mask_low):
    high, low = split_two(rows)
    summed = dot(high, mask_low) + dot(low, mask_low)
    shape = (HEAD_DIM, LANES)
    pick = iota(shape, 0) == (iota(shape, 1) % HEAD_DIM)
    return jnp.sum(jnp.where(pick, summed, 0.0), axis=0, keepdims=True)


def lane_slice(group):
    return slice(group * LANES, (group + 1) * LANES)


def causal_mask(length):
    shape = (length, LANES)
    return iota(shape, 0) <= (iota(shape, 1) % HEAD_DIM)


def token_start_body(
    tok_ref, gain_one, shift_one, qkv_mat, out_mat, gain_two, shift_two, query_mat,
    qkv_ref, att_ref, hidden_ref, query_ref, *, length
):
    x = tok_ref[...].astype(F32)
    unit, _ = normalize(x)
    normed = (unit * gain_one[...] + shift_one[...]).astype(BF16)
    width = x.shape[1]
    qkv_ref[...] = dot(normed, qkv_mat[...]).astype(BF16)
    mask = same_head()
    causal = causal_mask(length)
    for cap in range(x.shape[0] // length):
        rows = slice(cap * length, (cap + 1) * length)
        for group in range(GROUPS):
            lo = group * LANES
            query = qkv_ref[rows, lo : lo + LANES] * SCALE
            key = qkv_ref[rows, width + lo : width + lo + LANES]
            value = qkv_ref[rows, 2 * width + lo : 2 * width + lo + LANES]
            scores = jnp.where(causal, dot_nt(key, spread(query, mask)), NEG)
            exponent = jnp.exp(scores - jnp.max(scores, axis=0, keepdims=True))
            probs = exponent / jnp.sum(exponent, axis=0, keepdims=True)
            full = dot_tn(probs.astype(BF16), value)
            att_ref[rows, lo : lo + LANES] = gather_heads(full).astype(BF16)
    hidden = x + dot(att_ref[...], out_mat[...])
    hidden_ref[...] = hidden
    unit, _ = normalize(hidden)
    normed = (unit * gain_two[...] + shift_two[...]).astype(BF16)
    query_ref[...] = (dot(normed, query_mat[...]).astype(BF16).astype(F32) * SCALE).astype(BF16)


def whole(shape):
    zeros = (0,) * len(shape)
    return pl.BlockSpec(shape, lambda *_: zeros)


def token_start(tokens, gain_one, shift_one, qkv_mat, out_mat, gain_two, shift_two, query_mat, length):
    rows, width = tokens.shape
    tile = min(256, rows)
    row_block = lambda cols: pl.BlockSpec((tile, cols), lambda i: (i, 0))
    return pl.pallas_call(
        functools.partial(token_start_body, length=length),
        grid=(rows // tile,),
        in_specs=[
            row_block(width), whole((1, width)), whole((1, width)), whole(qkv_mat.shape),
            whole(out_mat.shape), whole((1, width)), whole((1, width)), whole(query_mat.shape),
        ],
        out_specs=[row_block(3 * width), row_block(width), row_block(width), row_block(width)],
        out_shape=[
            jax.ShapeDtypeStruct((rows, 3 * width), BF16),
            jax.ShapeDtypeStruct((rows, width), BF16),
            jax.ShapeDtypeStruct((rows, width), F32),
            jax.ShapeDtypeStruct((rows, width), BF16),
        ],
        compiler_params=pltpu.CompilerParams(vmem_limit_bytes=VMEM_LIMIT),
        name="token_start",
    )(tokens, gain_one, shift_one, qkv_mat, out_mat, gain_two, shift_two, query_mat)


def cross_start_body(valid_ref, img_ref, kv_mat, query_ref, kv_ref, att_ref, lse_ref, *, short):
    cap = pl.program_id(0)
    valid = valid_ref[cap]
    width = query_ref.shape[2]
    slots = img_ref.shape[1]

    def work(count):
        kv_ref[0, :count] = dot(img_ref[0, :count], kv_mat[...]).astype(BF16)
        mask = same_head()
        inside = iota((count, LANES), 0) < valid
        for group in range(GROUPS):
            lo = group * LANES
            key = kv_ref[0, :count, lo : lo + LANES]
            value = kv_ref[0, :count, width + lo : width + lo + LANES]
            scores = dot_nt(key, spread(query_ref[0, :, lo : lo + LANES], mask))
            scores = jnp.where(inside, scores, NEG)
            peak = jnp.max(scores, axis=0, keepdims=True)
            exponent = jnp.where(inside, jnp.exp(scores - peak), 0.0)
            total = jnp.sum(exponent, axis=0, keepdims=True)
            probs = (exponent * (1.0 / total)).astype(BF16)
            att_ref[0, :, lo : lo + LANES] = gather_heads(dot_tn(probs, value)).astype(BF16)
            lse_ref[0, group : group + 1] = peak + jnp.log(total)

    @pl.when(valid <= 0)
    def _():
        att_ref[...] = jnp.zeros_like(att_ref)
        lse_ref[...] = jnp.full_like(lse_ref, NEG)

    if short < slots:
        pl.when((valid > 0) & (valid <= short))(lambda: work(short))
        pl.when(valid > short)(lambda: work(slots))
    else:
        pl.when(valid > 0)(lambda: work(slots))


def cross_start(valid, images, kv_mat, queries, short):
    caps, slots, width = images.shape
    length = queries.shape[1]
    block = lambda *shape: pl.BlockSpec((1,) + shape, lambda i, *_: (i, 0, 0))
    return pl.pallas_call(
        functools.partial(cross_start_body, short=short),
        grid_spec=pltpu.PrefetchScalarGridSpec(
            num_scalar_prefetch=1,
            grid=(caps,),
            in_specs=[block(slots, width), whole(kv_mat.shape), block(length, width)],
            out_specs=[block(slots, 2 * width), block(length, width), block(GROUPS, LANES)],
        ),
        out_shape=[
            jax.ShapeDtypeStruct((caps, slots, 2 * width), BF16),
            jax.ShapeDtypeStruct((caps, length, width), BF16),
            jax.ShapeDtypeStruct((caps, GROUPS, LANES), F32),
        ],
        compiler_params=pltpu.CompilerParams(vmem_limit_bytes=VMEM_LIMIT),
        name="cross_start",
    )(valid, images, kv_mat, queries)


def feed_body(
    side_ref, att_one, lse_one, att_two, lse_two, hidden_ref, cot_ref, cross_mat, gain_ref,
    shift_ref, up_mat, down_mat,
    out_ref, grad_two_ref, grad_att_ref, lse_ref, delta_ref, up_mine, up_send, down_mine,
    down_send, cross_mine, cross_send, gain_grad, shift_grad,
    att_full, att_low, hidden_two, normed_ref, acc_out, acc_grad, *, length, tile
):
    step = pl.program_id(0)
    steps = pl.num_programs(0)
    side = side_ref[0]
    rows, width = hidden_ref.shape
    captions = rows // length
    tiles = rows // tile
    half = width // 2

    @pl.when(step == 0)
    def _():
        mask_low = same_head().astype(BF16)

        def one_caption(cap, carry):
            span = pl.ds(pl.multiple_of(cap * length, length), length)
            for group in range(GROUPS):
                lo = group * LANES
                first = lse_one[cap, group : group + 1]
                second = lse_two[cap, group : group + 1]
                peak = jnp.maximum(first, second)
                lse = peak + jnp.log(jnp.exp(first - peak) + jnp.exp(second - peak))
                lse_ref[cap, group : group + 1] = lse
                weight_one = lanes_to_rows(jnp.exp(first - lse), mask_low)
                weight_two = lanes_to_rows(jnp.exp(second - lse), mask_low)
                mixed = (
                    weight_one * att_one[span, lo : lo + LANES].astype(F32)
                    + weight_two * att_two[span, lo : lo + LANES].astype(F32)
                )
                att_full[span, lo : lo + LANES] = mixed
                att_low[span, lo : lo + LANES] = mixed.astype(BF16)
            return carry

        lax.fori_loop(0, captions, one_caption, 0)

        def one_tile(index, carry):
            span = pl.ds(pl.multiple_of(index * tile, tile), tile)
            two = hidden_ref[span, :] + dot(att_low[span, :], cross_mat[...])
            hidden_two[span, :] = two
            unit, _ = normalize(two)
            normed_ref[span, :] = (unit * gain_ref[...] + shift_ref[...]).astype(BF16)
            acc_out[span, :] = two
            acc_grad[span, :] = jnp.zeros_like(two)
            return carry

        lax.fori_loop(0, tiles, one_tile, 0)

    pre = dot(normed_ref[...], up_mat[...])
    cdf = 0.5 * (1.0 + lax.erf(pre * 0.7071067811865476))
    act = (pre * cdf).astype(BF16)
    acc_out[...] += dot(act, down_mat[...])
    cot = cot_ref[...]
    density = jnp.exp(-0.5 * pre * pre) * 0.3989422804014327
    grad_up = (dot_nt(cot, down_mat[...]) * (cdf + pre * density)).astype(BF16)
    acc_grad[...] += dot_nt(grad_up, up_mat[...])
    grad_down = dot_tn(act, cot).astype(BF16)
    grad_w = dot_tn(normed_ref[...], grad_up).astype(BF16)
    in_mine = (step >= steps // 2) == (side == 1)

    @pl.when(in_mine)
    def _():
        up_mine[...] = grad_w

    @pl.when(jnp.logical_not(in_mine))
    def _():
        up_send[...] = grad_w

    @pl.when(side == 0)
    def _():
        down_mine[...] = grad_down[:, :half]
        down_send[...] = grad_down[:, half:]

    @pl.when(side == 1)
    def _():
        down_mine[...] = grad_down[:, half:]
        down_send[...] = grad_down[:, :half]

    @pl.when(step == steps - 1)
    def _():
        mask_low = same_head().astype(BF16)
        gain_grad[...] = jnp.zeros_like(gain_grad)
        shift_grad[...] = jnp.zeros_like(shift_grad)

        def one_tile(index, carry):
            span = pl.ds(pl.multiple_of(index * tile, tile), tile)
            out_ref[span, :] = acc_out[span, :].astype(BF16)
            unit, inverse = normalize(hidden_two[span, :])
            grad = acc_grad[span, :]
            gain_grad[...] += jnp.sum(grad * unit, axis=0, keepdims=True)
            shift_grad[...] += jnp.sum(grad, axis=0, keepdims=True)
            two = cot_ref[span, :].astype(F32) + norm_back(grad, gain_ref[...], unit, inverse)
            grad_two_ref[span, :] = two
            low = two.astype(BF16)
            normed_ref[span, :] = low
            grad_att_ref[span, :] = dot_nt(low, cross_mat[...]).astype(BF16)
            return carry

        lax.fori_loop(0, tiles, one_tile, 0)
        grad_cross = dot_tn(att_low[...], normed_ref[...]).astype(BF16)

        @pl.when(side == 0)
        def _():
            cross_mine[...] = grad_cross[:, :half]
            cross_send[...] = grad_cross[:, half:]

        @pl.when(side == 1)
        def _():
            cross_mine[...] = grad_cross[:, half:]
            cross_send[...] = grad_cross[:, :half]

        def one_caption(cap, carry):
            span = pl.ds(pl.multiple_of(cap * length, length), length)
            for group in range(GROUPS):
                lo = group * LANES
                product = grad_att_ref[span, lo : lo + LANES].astype(F32) * att_full[span, lo : lo + LANES]
                delta_ref[cap, group : group + 1] = rows_to_lanes(product, mask_low)
            return carry

        lax.fori_loop(0, captions, one_caption, 0)


def feed(side, att_one, lse_one, att_two, lse_two, hidden, cot, cross_mat, gain, shift, up_mat, down_mat, length):
    rows, width = hidden.shape
    captions = rows // length
    units = up_mat.shape[1]
    chunk = 512
    steps = units // chunk
    middle = steps // 2
    tile = min(256, rows)
    half = width // 2
    stat = (captions, GROUPS, LANES)
    sds = jax.ShapeDtypeStruct
    clip = lambda v: jnp.minimum(jnp.maximum(v, 0), middle - 1)
    mine_map = lambda i, side: (0, clip(i - middle * side[0]))
    send_map = lambda i, side: (0, clip(i - middle * (1 - side[0])))
    return pl.pallas_call(
        functools.partial(feed_body, length=length, tile=tile),
        grid_spec=pltpu.PrefetchScalarGridSpec(
            num_scalar_prefetch=1,
            grid=(steps,),
            in_specs=[
                whole((rows, width)), whole(stat), whole((rows, width)), whole(stat),
                whole((rows, width)), whole((rows, width)), whole((width, width)),
                whole((1, width)), whole((1, width)),
                pl.BlockSpec((width, chunk), lambda i, *_: (0, i)),
                pl.BlockSpec((chunk, width), lambda i, *_: (i, 0)),
            ],
            out_specs=[
                whole((rows, width)), whole((rows, width)), whole((rows, width)), whole(stat),
                whole(stat),
                pl.BlockSpec((width, chunk), mine_map), pl.BlockSpec((width, chunk), send_map),
                pl.BlockSpec((chunk, half), lambda i, *_: (i, 0)),
                pl.BlockSpec((chunk, half), lambda i, *_: (i, 0)),
                whole((width, half)), whole((width, half)),
                whole((1, width)), whole((1, width)),
            ],
            scratch_shapes=[
                pltpu.VMEM((rows, width), F32), pltpu.VMEM((rows, width), BF16),
                pltpu.VMEM((rows, width), F32), pltpu.VMEM((rows, width), BF16),
                pltpu.VMEM((rows, width), F32), pltpu.VMEM((rows, width), F32),
            ],
        ),
        out_shape=[
            sds((rows, width), BF16), sds((rows, width), F32), sds((rows, width), BF16),
            sds(stat, F32), sds(stat, F32),
            sds((width, units // 2), BF16), sds((width, units // 2), BF16),
            sds((units, half), BF16), sds((units, half), BF16),
            sds((width, half), BF16), sds((width, half), BF16),
            sds((1, width), F32), sds((1, width), F32),
        ],
        compiler_params=pltpu.CompilerParams(vmem_limit_bytes=VMEM_LIMIT),
        name="feed",
    )(side, att_one, lse_one, att_two, lse_two, hidden, cot, cross_mat, gain, shift, up_mat, down_mat)


def cross_back_body(
    valid_ref, kv_ref, query_ref, grad_ref, lse_ref, delta_ref, kv_mat,
    grad_query_ref, grad_kv_ref, grad_img_ref, *, short
):
    cap = pl.program_id(0)
    valid = valid_ref[cap]
    width = query_ref.shape[2]
    slots = kv_ref.shape[1]

    def work(count):
        mask = same_head()
        inside = iota((count, LANES), 0) < valid
        for group in range(GROUPS):
            lo = group * LANES
            key = kv_ref[0, :count, lo : lo + LANES]
            value = kv_ref[0, :count, width + lo : width + lo + LANES]
            query = spread(query_ref[0, :, lo : lo + LANES], mask)
            grad = spread(grad_ref[0, :, lo : lo + LANES], mask)
            scores = dot_nt(key, query)
            probs = jnp.where(inside, jnp.exp(scores - lse_ref[0, group : group + 1]), 0.0)
            grad_probs = dot_nt(value, grad)
            grad_scores = (probs * (grad_probs - delta_ref[0, group : group + 1])).astype(BF16)
            back = gather_heads(dot_tn(grad_scores, key)) * SCALE
            grad_query_ref[0, :, lo : lo + LANES] = back.astype(BF16)
            grad_kv_ref[0, :count, lo : lo + LANES] = dot(grad_scores, query).astype(BF16)
            grad_kv_ref[0, :count, width + lo : width + lo + LANES] = dot(
                probs.astype(BF16), grad
            ).astype(BF16)
        grad_img_ref[0, :count] = dot_nt(grad_kv_ref[0, :count], kv_mat[...]).astype(BF16)
        if count < slots:
            grad_kv_ref[0, count:] = jnp.zeros((slots - count, 2 * width), BF16)
            grad_img_ref[0, count:] = jnp.zeros((slots - count, width), BF16)

    @pl.when(valid <= 0)
    def _():
        grad_query_ref[...] = jnp.zeros_like(grad_query_ref)
        grad_kv_ref[...] = jnp.zeros_like(grad_kv_ref)
        grad_img_ref[...] = jnp.zeros_like(grad_img_ref)

    if short < slots:
        pl.when((valid > 0) & (valid <= short))(lambda: work(short))
        pl.when(valid > short)(lambda: work(slots))
    else:
        pl.when(valid > 0)(lambda: work(slots))


def cross_back(valid, kv, queries, grads, lse, delta, kv_mat, short):
    caps, slots, double = kv.shape
    width = double // 2
    length = queries.shape[1]
    block = lambda *shape: pl.BlockSpec((1,) + shape, lambda i, *_: (i, 0, 0))
    sds = jax.ShapeDtypeStruct
    return pl.pallas_call(
        functools.partial(cross_back_body, short=short),
        grid_spec=pltpu.PrefetchScalarGridSpec(
            num_scalar_prefetch=1,
            grid=(caps,),
            in_specs=[
                block(slots, double), block(length, width), block(length, width),
                block(GROUPS, LANES), block(GROUPS, LANES), whole(kv_mat.shape),
            ],
            out_specs=[block(length, width), block(slots, double), block(slots, width)],
        ),
        out_shape=[
            sds((caps, length, width), BF16), sds((caps, slots, double), BF16),
            sds((caps, slots, width), BF16),
        ],
        compiler_params=pltpu.CompilerParams(vmem_limit_bytes=VMEM_LIMIT),
        name="cross_back",
    )(valid, kv, queries, grads, lse, delta, kv_mat)


def image_weight_body(side_ref, img_ref, grad_ref, mine_ref, send_ref, acc_ref):
    step = pl.program_id(0)

    @pl.when(step == 0)
    def _():
        acc_ref[...] = jnp.zeros_like(acc_ref)

    acc_ref[...] += dot_tn(img_ref[...], grad_ref[...])

    @pl.when(step == pl.num_programs(0) - 1)
    def _():
        half = acc_ref.shape[1] // 2
        side = side_ref[0]

        @pl.when(side == 0)
        def _():
            mine_ref[...] = acc_ref[:, :half].astype(BF16)
            send_ref[...] = acc_ref[:, half:].astype(BF16)

        @pl.when(side == 1)
        def _():
            mine_ref[...] = acc_ref[:, half:].astype(BF16)
            send_ref[...] = acc_ref[:, :half].astype(BF16)


def image_weight(side, images, grads):
    rows, width = images.shape
    double = grads.shape[1]
    tile = 512 if rows % 512 == 0 else rows // 4
    sds = jax.ShapeDtypeStruct
    return pl.pallas_call(
        image_weight_body,
        grid_spec=pltpu.PrefetchScalarGridSpec(
            num_scalar_prefetch=1,
            grid=(rows // tile,),
            in_specs=[
                pl.BlockSpec((tile, width), lambda i, *_: (i, 0)),
                pl.BlockSpec((tile, double), lambda i, *_: (i, 0)),
            ],
            out_specs=[whole((width, double // 2)), whole((width, double // 2))],
            scratch_shapes=[pltpu.VMEM((width, double), F32)],
        ),
        out_shape=[sds((width, double // 2), BF16)] * 2,
        compiler_params=pltpu.CompilerParams(vmem_limit_bytes=VMEM_LIMIT),
        name="image_weight",
    )(side, images, grads)


def token_end_body(
    side_ref, back_one, back_two, hidden_ref, grad_two_ref, att_ref, qkv_ref, tok_ref,
    gain_one, shift_one, qkv_mat, out_mat, gain_two, shift_two, query_mat,
    grad_tok_ref, qkv_mine, qkv_send, out_mine, out_send, query_mine, query_send, gains_ref,
    grad_qkv_ref, acc_qkv, acc_out, acc_query, *, length
):
    step = pl.program_id(0)

    @pl.when(step == 0)
    def _():
        acc_qkv[...] = jnp.zeros_like(acc_qkv)
        acc_out[...] = jnp.zeros_like(acc_out)
        acc_query[...] = jnp.zeros_like(acc_query)
        gains_ref[...] = jnp.zeros_like(gains_ref)

    back = (back_one[...].astype(F32) + back_two[...].astype(F32)).astype(BF16)
    unit, inverse = normalize(hidden_ref[...])
    normed = (unit * gain_two[...] + shift_two[...]).astype(BF16)
    acc_query[...] += dot_tn(normed, back)
    grad = dot_nt(back, query_mat[...])
    gains_ref[2:3] += jnp.sum(grad * unit, axis=0, keepdims=True)
    gains_ref[3:4] += jnp.sum(grad, axis=0, keepdims=True)
    grad_one = grad_two_ref[...] + norm_back(grad, gain_two[...], unit, inverse)
    low = grad_one.astype(BF16)
    acc_out[...] += dot_tn(att_ref[...], low)
    grad_att = dot_nt(low, out_mat[...]).astype(BF16)
    rows, width = grad_att.shape
    mask = same_head()
    causal = causal_mask(length)
    for cap in range(rows // length):
        span = slice(cap * length, (cap + 1) * length)
        for group in range(GROUPS):
            lo = group * LANES
            query = spread(qkv_ref[span, lo : lo + LANES] * SCALE, mask)
            key = qkv_ref[span, width + lo : width + lo + LANES]
            value = qkv_ref[span, 2 * width + lo : 2 * width + lo + LANES]
            cot = spread(grad_att[span, lo : lo + LANES], mask)
            scores = jnp.where(causal, dot_nt(key, query), NEG)
            exponent = jnp.exp(scores - jnp.max(scores, axis=0, keepdims=True))
            probs = exponent / jnp.sum(exponent, axis=0, keepdims=True)
            grad_probs = dot_nt(value, cot)
            mean = jnp.sum(probs * grad_probs, axis=0, keepdims=True)
            grad_scores = (probs * (grad_probs - mean)).astype(BF16)
            grad_q = gather_heads(dot_tn(grad_scores, key)) * SCALE
            grad_qkv_ref[span, lo : lo + LANES] = grad_q.astype(BF16)
            grad_qkv_ref[span, width + lo : width + lo + LANES] = dot(grad_scores, query).astype(BF16)
            grad_qkv_ref[span, 2 * width + lo : 2 * width + lo + LANES] = dot(
                probs.astype(BF16), cot
            ).astype(BF16)
    unit, inverse = normalize(tok_ref[...].astype(F32))
    normed = (unit * gain_one[...] + shift_one[...]).astype(BF16)
    acc_qkv[...] += dot_tn(normed, grad_qkv_ref[...])
    grad = dot_nt(grad_qkv_ref[...], qkv_mat[...])
    gains_ref[0:1] += jnp.sum(grad * unit, axis=0, keepdims=True)
    gains_ref[1:2] += jnp.sum(grad, axis=0, keepdims=True)
    grad_tok_ref[...] = (grad_one + norm_back(grad, gain_one[...], unit, inverse)).astype(BF16)

    @pl.when(step == pl.num_programs(0) - 1)
    def _():
        for acc, mine, send in (
            (acc_qkv, qkv_mine, qkv_send),
            (acc_out, out_mine, out_send),
            (acc_query, query_mine, query_send),
        ):
            half = acc.shape[1] // 2

            @pl.when(side_ref[0] == 0)
            def _():
                mine[...] = acc[:, :half].astype(BF16)
                send[...] = acc[:, half:].astype(BF16)

            @pl.when(side_ref[0] == 1)
            def _():
                mine[...] = acc[:, half:].astype(BF16)
                send[...] = acc[:, :half].astype(BF16)


def token_end(
    side, back_one, back_two, hidden, grad_two, att, qkv, tokens,
    gain_one, shift_one, qkv_mat, out_mat, gain_two, shift_two, query_mat, length
):
    rows, width = tokens.shape
    tile = min(256, rows)
    row_block = lambda cols: pl.BlockSpec((tile, cols), lambda i, *_: (i, 0))
    sds = jax.ShapeDtypeStruct
    halves = [(width, 3 * width // 2)] * 2 + [(width, width // 2)] * 4
    return pl.pallas_call(
        functools.partial(token_end_body, length=length),
        grid_spec=pltpu.PrefetchScalarGridSpec(
            num_scalar_prefetch=1,
            grid=(rows // tile,),
            in_specs=[
                row_block(width), row_block(width), row_block(width), row_block(width),
                row_block(width), row_block(3 * width), row_block(width),
                whole((1, width)), whole((1, width)), whole(qkv_mat.shape), whole(out_mat.shape),
                whole((1, width)), whole((1, width)), whole(query_mat.shape),
            ],
            out_specs=[row_block(width)] + [whole(s) for s in halves] + [whole((4, width))],
            scratch_shapes=[
                pltpu.VMEM((tile, 3 * width), BF16), pltpu.VMEM((width, 3 * width), F32),
                pltpu.VMEM((width, width), F32), pltpu.VMEM((width, width), F32),
            ],
        ),
        out_shape=[sds((rows, width), BF16)] + [sds(s, BF16) for s in halves] + [sds((4, width), F32)],
        compiler_params=pltpu.CompilerParams(vmem_limit_bytes=VMEM_LIMIT),
        name="token_end",
    )(
        side, back_one, back_two, hidden, grad_two, att, qkv, tokens,
        gain_one, shift_one, qkv_mat, out_mat, gain_two, shift_two, query_mat,
    )


def add_low(first, second):
    return (first.astype(F32) + second.astype(F32)).astype(BF16)


def exchange(value, axis, bit, size):
    return lax.ppermute(value, axis, [(i, i ^ bit) for i in range(size)])


def reduce_blocks(mine, send, order, me, size):
    total = add_low(mine, exchange(send, "kv", 1, 2))
    bits = size.bit_length() - 1
    rows = total.shape[0] // size
    total = total.reshape((2,) * bits + (rows, total.shape[1]))
    left = list(range(bits))[::-1]
    for bit in order:
        axis = left.index(bit)
        own = (me >> bit) & 1
        keep = lax.dynamic_index_in_dim(total, own, axis, False)
        away = lax.dynamic_index_in_dim(total, 1 - own, axis, False)
        total = add_low(keep, exchange(away, "dp", 1 << bit, size))
        left.remove(bit)
    return total.astype(F32)


def body(
    tokens, images, image_counts, cotangent, norm1_gain, norm1_shift, self_qkv, self_out,
    norm2_gain, norm2_shift, cross_q, cross_kv, cross_out, norm3_gain, norm3_shift, w_up, w_down,
):
    captions, length, width = tokens.shape
    caps, slots, _ = images.shape
    side = lax.axis_index("kv")
    me = lax.axis_index("dp")
    groups = lax.axis_size("dp")
    side_arr = side.reshape(1)
    row = lambda v: v.reshape(1, width)
    tok = tokens.reshape(captions * length, width)
    cot = cotangent.reshape(captions * length, width)
    short = -(-SHORT // 16) * 16
    valid = jnp.clip(image_counts - side * slots, 0, slots)
    swap = lambda v: exchange(v, "kv", 1, 2)

    qkv, att, hidden, query = token_start(
        tok, row(norm1_gain), row(norm1_shift), self_qkv, self_out, row(norm2_gain),
        row(norm2_shift), cross_q, length,
    )

    def both(own):
        other = swap(own)
        first = jnp.where(side == 0, own, other)
        second = jnp.where(side == 0, other, own)
        return jnp.concatenate([first, second], axis=0)

    def own_part(array):
        return lax.dynamic_slice_in_dim(array, side * captions, captions, 0)

    def other_part(array):
        return lax.dynamic_slice_in_dim(array, (1 - side) * captions, captions, 0)

    queries = both(query.reshape(captions, length, width))
    kv, part, lse_part = cross_start(valid, images, cross_kv, queries, short)
    flat = lambda v: v.reshape(captions * length, width)
    (
        layer_out, grad_two, grad_att, lse, delta, up_mine, up_send, down_mine, down_send,
        cross_mine, cross_send, gain3, shift3,
    ) = feed(
        side_arr, flat(own_part(part)), own_part(lse_part), flat(swap(other_part(part))),
        swap(other_part(lse_part)), hidden, cot, cross_out, row(norm3_gain), row(norm3_shift),
        w_up, w_down, length,
    )
    bits = groups.bit_length() - 1
    turn = lambda start: [(start + i) % bits for i in range(bits)]
    w_up_grad = reduce_blocks(up_mine, up_send, turn(0), me, groups)
    down_grad = reduce_blocks(down_mine, down_send, turn(bits // 2), me, groups)
    cross_out_grad = reduce_blocks(cross_mine, cross_send, turn(bits // 4), me, groups)

    grads = both(grad_att.reshape(captions, length, width))
    back, grad_kv, images_grad = cross_back(
        valid, kv, queries, grads, both(lse), both(delta), cross_kv, short
    )
    kv_mine, kv_send = image_weight(
        side_arr, images.reshape(caps * slots, width), grad_kv.reshape(caps * slots, 2 * width)
    )
    cross_kv_grad = reduce_blocks(kv_mine, kv_send, turn(0), me, groups)
    (
        tokens_grad, qkv_mine, qkv_send, out_mine, out_send, query_mine, query_send, gains,
    ) = token_end(
        side_arr, flat(own_part(back)), flat(swap(other_part(back))), hidden, grad_two, att, qkv,
        tok, row(norm1_gain), row(norm1_shift), self_qkv, self_out, row(norm2_gain),
        row(norm2_shift), cross_q, length,
    )
    self_qkv_grad = reduce_blocks(qkv_mine, qkv_send, turn(0), me, groups)
    self_out_grad = reduce_blocks(out_mine, out_send, turn(bits // 2), me, groups)
    cross_q_grad = reduce_blocks(query_mine, query_send, turn(bits // 4), me, groups)
    gains = jnp.concatenate([gains, gain3, shift3], axis=0)
    gains = gains + swap(gains)
    gains = lax.dynamic_slice_in_dim(gains, side * (width // 2), width // 2, 1)
    for bit in range(bits):
        gains = gains + exchange(gains, "dp", 1 << bit, groups)
    return (
        layer_out.reshape(captions, length, width),
        tokens_grad.reshape(captions, length, width),
        images_grad,
        gains[0], gains[1], self_qkv_grad, self_out_grad, gains[2], gains[3], cross_q_grad,
        cross_kv_grad, cross_out_grad, gains[4], gains[5], w_up_grad, down_grad,
    )


def solution(mesh):
    return jax.shard_map(
        body,
        mesh=mesh,
        in_specs=(
            P(("dp", "kv"), None, None), P("dp", "kv", None), P("dp"), P(("dp", "kv"), None, None),
        ) + (P(),) * 13,
        out_specs=(
            P(("dp", "kv"), None, None), P(("dp", "kv"), None, None), P("dp", "kv", None),
            P("kv"), P("kv"), P("dp", "kv"), P("dp", "kv"), P("kv"), P("kv"), P("dp", "kv"),
            P("dp", "kv"), P("dp", "kv"), P("kv"), P("kv"), P("dp", "kv"), P("dp", "kv"),
        ),
        check_vma=False,
    )
```

time: 1600 us -> 356 us (0.22)
  waiting for transfers between devices: 836 us -> 105 us
  local copies, waits for them, and re-layouts: 363 us -> 19.7 us
  matrix products: 226 us -> 0 us
  Pallas kernels: 0 us -> 161 us
  blocking collectives: 79.6 us -> 0 us
  other arithmetic: 63.5 us -> 22.4 us
  starting transfers between devices: 1.55 us -> 38.6 us
    reduce_scatter x9 -> x0, waiting for transfers between devices: 701 us -> none  [the longest x1 143 us: body(): lax.psum_scatter(down_weight_gradient, 'dp', scatter_dimension=0, tiled=T...]
    dot_general x33 -> x0, matrix products: 226 us -> none  [the longest x1 22.2 us: cross_partial(): jnp.einsum('cqhp,cphd->cqhd', weights, values.astype(jnp.float32), precis...]
    pallas_call x0 -> x6, Pallas kernels: none -> 161 us  [the longest x1 40.1 us: cross_back(): pl.pallas_call(functools.partial(cross_back_body, short=short), grid_spec...]
    unnamed x26 -> x0, waiting for transfers between devices: 134 us -> none
    unnamed x173 -> x36, local copies, waits for them, and re-layouts: 111 us -> 4.12 us
    ppermute x0 -> x47, waiting for transfers between devices: none -> 105 us  [exchange(): return lax.ppermute(value, axis, [(i, i ^ bit) for i in range(size)])]
    reshape x17 -> x6, local copies, waits for them, and re-layouts: 93.5 us -> 6.25 us  [body(): row = lambda v: v.reshape(1, width)]
    convert_element_type x9 -> x0, local copies, waits for them, and re-layouts: 78.7 us -> none  [the longest x2 44 us: body(): grad_ckv = jnp.stack([grad_keys, grad_values], axis=2).astype(jnp.bfloat16)]
  transfers between devices with their start and end apart: 19 -> 47, of which waited for: 8 -> 23; matrix products, arithmetic and copies ran while one was open for 30% -> 8% of each run, Pallas kernels for 0% -> 24%
where the time goes in v1:
time: 356 us; the launch traced here: 348 us
  Pallas kernels  161 us (45%)
  waiting for transfers between devices  105 us (29%)
  starting transfers between devices  38.6 us (11%)
  other arithmetic  22.4 us (6%)
  local copies, waits for them, and re-layouts  19.7 us (6%)
    ppermute x47, waiting for transfers between devices, exchange(): return lax.ppermute(value, axis, [(i, i ^ bit) for i in range(size)])  105 us
    pallas_call x1, Pallas kernels, cross_back(): pl.pallas_call(functools.partial(cross_back_body, short=short), grid_spec...  40.1 us
    ppermute x47, starting transfers between devices, exchange(): return lax.ppermute(value, axis, [(i, i ^ bit) for i in range(size)])  38.6 us
    pallas_call x1, Pallas kernels, feed(): pl.pallas_call(functools.partial(feed_body, length=length, tile=tile), gr...  34.2 us
    pallas_call x1, Pallas kernels, cross_start(): pl.pallas_call(functools.partial(cross_start_body, short=short), grid_spe...  30.5 us
    pallas_call x1, Pallas kernels, token_end(): pl.pallas_call(functools.partial(token_end_body, length=length), grid_spe...  26.2 us
    pallas_call x1, Pallas kernels, image_weight(): pl.pallas_call(image_weight_body, grid_spec=pltpu.PrefetchScalarGridSpec(...  17.6 us
    pallas_call x1, Pallas kernels, token_start(): pl.pallas_call(functools.partial(token_start_body, length=length), grid=(...  12.5 us
  transfers between devices with their start and end apart: 47, of which 23 were waited for; matrix products, arithmetic and copies ran while one was open for 8% of the time, Pallas kernels for 24%

profile of v1, /device:TPU:2, one launch (start us, length us, event | category | flops | bytes accessed | tf_op | source)
XLA Modules:
  0.0 348.5 jit_solution(8975540791160493645)
XLA Ops:
  5.7 12.5 %token_start.1 = (bf16[512,2304]{1,0:T(8,128)(2,1)}, bf16[512,768]{1,0:T(8,128)(2,1)}, f32[512,768]{1,0:T(8,128)}, bf16[512,768]{1,0:T(8,128)(2,1)}) custom-call(bf16[512,768]{1,0:T(8,128)(2,1)} %bitcast.188, f32[1,768]{1,0:T(1,128)} %reshape.172.gain_one, f32[1,768]{1,0:T(1,128)} %reshape.173.shift_one, bf16[768,2304]{1,0:T(8,128)(2,1)} %qkv_mat.3, ...), custom_call_target="tpu_custom_call" | custom-call | tf_op jit(solution)/shard_map/token_start/pallas_call | solution.py:140
  18.8 2.0 collective-permute-done
  23.3 30.5 %cross_start.1 = (bf16[16,288,1536]{2,1,0:T(8,128)(2,1)}, bf16[16,64,768]{2,1,0:T(8,128)(2,1)}, f32[16,3,256]{2,1,0:T(4,128)}) custom-call(s32[16]{0:T(128)} %subtract_clamp_fusion.valid_ref, bf16[16,288,768]{2,1,0:T(8,128)(2,1)} %img_ref.1, bf16[768,1536]{1,0:T(8,128)(2,1)} %kv_mat.3, bf16[16,64,768]{2,1,0:T(8,128)(2,1)} %pad_maximum_fusion.query_ref), custom_call_target="tpu_custom_call" | custom-call | tf_op jit(solution)/shard_map/cross_start/pallas_call | solution.py:198
  53.9 2.4 constant_dynamic-slice_fusion.19
  59.5 34.2 %feed.1 = (bf16[512,768]{1,0:T(8,128)(2,1)}, f32[512,768]{1,0:T(8,128)}, bf16[512,768]{1,0:T(8,128)(2,1)}, f32[8,3,256]{2,1,0:T(4,128)}, f32[8,3,256]{2,1,0:T(4,...) custom-call(s32[1]{0:T(128)} %bitcast.side_ref, ...), custom_call_target="tpu_custom_call" | custom-call | tf_op jit(solution)/shard_map/feed/pallas_call | solution.py:356
  101.7 40.1 %cross_back.1 = (bf16[16,64,768]{2,1,0:T(8,128)(2,1)}, bf16[16,288,1536]{2,1,0:T(8,128)(2,1)}, bf16[16,288,768]{2,1,0:T(8,128)(2,1)}) custom-call(s32[16]{0:T(128)} %subtract_clamp_fusion.valid_ref, bf16[16,288,1536]{2,1,0:T(8,128)(2,1)} %get-tuple-element.54.kv_ref, bf16[16,64,768]{2,1,0:T(8,128)(2,1)} %pad_maximum_fusion.query_ref, ...), custom_call_target="tpu_custom_call" | custom-call | tf_op jit(solution)/shard_map/cross_back/pallas_call | solution.py:448
  142.5 1.7 collective-permute-start.34
  144.2 2.6 constant_dynamic-slice_fusion.16
  147.4 17.6 %image_weight.1 = (bf16[768,768]{1,0:T(8,128)(2,1)}, bf16[768,768]{1,0:T(8,128)(2,1)}) custom-call(s32[1]{0:T(128)} %bitcast.side_ref, bf16[4608,768]{1,0:T(8,128)(2,1)} %bitcast.181, bf16[4608,1536]{1,0:T(8,128)(2,1)} %bitcast.182), custom_call_target="tpu_custom_call" | custom-call | tf_op jit(solution)/shard_map/image_weight/pallas_call | solution.py:498
  166.7 2.4 collective-permute-start.35
  169.0 4.9 %collective-permute-done.35 = bf16[2,48,384]{2,1,0:T(8,128)(2,1)S(1)} collective-permute-done((bf16[2,48,384]{2,1,0:T(8,128)(2,1)S(1)}, bf16[2,48,384]{2,1,0:T(8,128)(2,1)S(1)}, u32[]{:S(2)}, u32[]{:S(2)}) %collective-permute-start.35) | collective-permute-done | bytes 73760 | tf_op jit(solution)/shard_map/ppermute | solution.py:633
  175.7 26.2 %token_end.1 = (bf16[512,768]{1,0:T(8,128)(2,1)}, bf16[768,1152]{1,0:T(8,128)(2,1)}, bf16[768,1152]{1,0:T(8,128)(2,1)}, bf16[768,384]{1,0:T(8,128)(2,1)}, bf16[7...) custom-call(s32[1]{0:T(128)} %bitcast.side_ref, ...), custom_call_target="tpu_custom_call" | custom-call | tf_op jit(solution)/shard_map/token_end/pallas_call | solution.py:602
  205.4 2.3 collective-permute-done.8
  208.9 2.6 collective-permute-done.9
  211.8 3.4 collective-permute-done.10
  216.0 1.7 collective-permute-start.11
  231.5 2.4 collective-permute-done.23
  237.2 2.5 collective-permute-done.28
  239.7 1.7 collective-permute-start.19
  241.6 25.1 %collective-permute-done.24 = bf16[2,2,48,384]{3,2,1,0:T(8,128)(2,1)S(1)} collective-permute-done((bf16[2,2,48,384]{3,2,1,0:T(8,128)(2,1)S(1)}, bf16[2,2,48,384]{3,2,1,0:T(8,128)(2,1)S(1)}, u32[]{:S(2)}, u32[]{:S(2)}) %collective-permute-start.24) | collective-permute-done | bytes 147488 | tf_op jit(solution)/shard_map/ppermute | solution.py:633
  269.1 4.8 %collective-permute-done.25 = bf16[2,48,384]{2,1,0:T(8,128)(2,1)S(1)} collective-permute-done((bf16[2,48,384]{2,1,0:T(8,128)(2,1)S(1)}, bf16[2,48,384]{2,1,0:T(8,128)(2,1)S(1)}, u32[]{:S(2)}, u32[]{:S(2)}) %collective-permute-start.25) | collective-permute-done | bytes 73760 | tf_op jit(solution)/shard_map/ppermute | solution.py:633
  275.0 3.2 collective-permute-done.20
  283.3 4.0 %collective-permute-done.30 = bf16[2,48,768]{2,1,0:T(8,128)(2,1)S(1)} collective-permute-done((bf16[2,48,768]{2,1,0:T(8,128)(2,1)S(1)}, bf16[2,48,768]{2,1,0:T(8,128)(2,1)S(1)}, u32[]{:S(2)}, u32[]{:S(2)}) %collective-permute-start.30) | collective-permute-done | bytes 147488 | tf_op jit(solution)/shard_map/ppermute | solution.py:633
  289.5 11.1 %collective-permute-done.31 = bf16[48,768]{1,0:T(8,128)(2,1)S(1)} collective-permute-done((bf16[48,768]{1,0:T(8,128)(2,1)S(1)}, bf16[48,768]{1,0:T(8,128)(2,1)S(1)}, u32[]{:S(2)}, u32[]{:S(2)}) %collective-permute-start.31) | collective-permute-done | bytes 73760 | tf_op jit(solution)/shard_map/ppermute | solution.py:633
  305.1 12.7 %collective-permute-done.44 = bf16[2,2,192,384]{3,2,0,1:T(8,128)(2,1)S(1)} collective-permute-done((bf16[2,2,192,384]{3,2,0,1:T(8,128)(2,1)S(1)}, bf16[2,2,192,384]{3,2,0,1:T(8,128)(2,1)S(1)}, u32[]{:S(2)}, u32[]{:S(2)}) %collective-permute-start.44) | collective-permute-done | bytes 589856 | tf_op jit(solution)/shard_map/ppermute | solution.py:633
  318.1 2.3 collective-permute-start.45
  322.0 3.0 collective-permute-done.45
  325.2 2.0 collective-permute-start.46
  327.2 4.1 %collective-permute-done.40 = bf16[2,48,1536]{2,1,0:T(8,128)(2,1)S(1)} collective-permute-done((bf16[2,48,1536]{2,1,0:T(8,128)(2,1)S(1)}, bf16[2,48,1536]{2,1,0:T(8,128)(2,1)S(1)}, u32[]{:S(2)}, u32[]{:S(2)}) %collective-permute-start.40) | collective-permute-done | bytes 294944 | tf_op jit(solution)/shard_map/ppermute | solution.py:633
  331.8 2.5 collective-permute-start.15
  334.3 5.8 %collective-permute-done.41 = bf16[48,1536]{1,0:T(8,128)(2,1)S(1)} collective-permute-done((bf16[48,1536]{1,0:T(8,128)(2,1)S(1)}, bf16[48,1536]{1,0:T(8,128)(2,1)S(1)}, u32[]{:S(2)}, u32[]{:S(2)}) %collective-permute-start.41) | collective-permute-done | bytes 147488 | tf_op jit(solution)/shard_map/ppermute | solution.py:633
  341.9 5.5 %collective-permute-done.16 = bf16[48,1152]{1,0:T(8,128)(2,1)S(1)} collective-permute-done((bf16[48,1152]{1,0:T(8,128)(2,1)S(1)}, bf16[48,1152]{1,0:T(8,128)(2,1)S(1)}, u32[]{:S(2)}, u32[]{:S(2)}) %collective-permute-start.16) | collective-permute-done | bytes 110624 | tf_op jit(solution)/shard_map/ppermute | solution.py:633
  (198 shorter events, 66.7 us)
Async XLA Ops:
  94.4 5.9 %collective-permute-start.3 = (bf16[8,64,768]{2,1,0:T(8,128)(2,1)}, bf16[8,64,768]{2,1,0:T(8,128)(2,1)S(1)}, u32[]{:S(2)}, u32[]{:S(2)}) collective-permute-start(bf16[8,64,768]{2,1,0:T(8,128)(2,1)} %bitcast.198), channel_id=1, source_target_pairs={{0,1},{1,0},{2,3},{3,2},{4,5},{5,4},{6,7},{7,6},{8,9},{9,8},{10,11... | collective-permute-start | bytes 2359304 | tf_op jit(solution)/shard_map/ppermute | solution.py:633
  99.0 42.8 %collective-permute-start.33 = (bf16[2,2,2,48,384]{4,3,2,0,1:T(8,128)(2,1)S(1)}, bf16[2,2,2,48,384]{4,3,2,0,1:T(8,128)(2,1)S(1)}, u32[]{:S(2)}, u32[]{:S(2)}) collective-permute-start(bf16[2,2,2,48,384]{4,3,2,0,1:T(8,128)(2,1)S(1)} %bitcast.207), channel_id=1, source_target_pairs={{0,4},{2,6},{4,0},{6,2},{8,12},{10,14},{12,8},{14,10},{16,20},{18,... | collective-permute-start | bytes 884744 | tf_op jit(solution)/shard_map/ppermute | solution.py:633
  142.5 22.5 %collective-permute-start.34 = (bf16[2,2,48,384]{3,2,1,0:T(8,128)(2,1)}, bf16[2,2,48,384]{3,2,1,0:T(8,128)(2,1)}, u32[]{:S(2)}, u32[]{:S(2)}) collective-permute-start(bf16[2,2,48,384]{3,2,1,0:T(8,128)(2,1)} %dynamic-slice_bitcast_fusion.9), channel_id=1, source_target_pairs={{0,8},{2,10},{4,12},{6,14},{8,0},{10,2},{12,4},{14,6},{16,24},{18,... | collective-permute-start | bytes 442376 | tf_op jit(solution)/shard_map/ppermute | solution.py:633
  146.9 27.9 %collective-permute-start.6 = (bf16[8,64,768]{2,1,0:T(8,128)(2,1)}, bf16[8,64,768]{2,1,0:T(8,128)(2,1)S(1)}, u32[]{:S(2)}, u32[]{:S(2)}) collective-permute-start(bf16[8,64,768]{2,1,0:T(8,128)(2,1)} %get-tuple-element.94), channel_id=1, source_target_pairs={{0,1},{1,0},{2,3},{3,2},{4,5},{5,4},{6,7},{7,6},{8,9},{9,8},{10,11... | collective-permute-start | bytes 2359304 | tf_op jit(solution)/shard_map/ppermute | solution.py:633
  146.9 79.8 %collective-permute-start.42 = (bf16[3072,384]{1,0:T(8,128)(2,1)}, bf16[3072,384]{1,0:T(8,128)(2,1)S(1)}, u32[]{:S(2)}, u32[]{:S(2)}) collective-permute-start(bf16[3072,384]{1,0:T(8,128)(2,1)} %get-tuple-element.81), channel_id=1, source_target_pairs={{0,1},{1,0},{2,3},{3,2},{4,5},{5,4},{6,7},{7,6},{8,9},{9,8},{10,11... | collective-permute-start | bytes 7077896 | tf_op jit(solution)/shard_map/ppermute | solution.py:633
  165.0 56.2 %collective-permute-start.27 = (bf16[768,768]{1,0:T(8,128)(2,1)}, bf16[768,768]{1,0:T(8,128)(2,1)}, u32[]{:S(2)}, u32[]{:S(2)}) collective-permute-start(bf16[768,768]{1,0:T(8,128)(2,1)} %get-tuple-element.75), channel_id=1, source_target_pairs={{0,1},{1,0},{2,3},{3,2},{4,5},{5,4},{6,7},{7,6},{8,9},{9,8},{10,11... | collective-permute-start | bytes 3538952 | tf_op jit(solution)/shard_map/ppermute | solution.py:633
  166.7 7.2 %collective-permute-start.35 = (bf16[2,48,384]{2,1,0:T(8,128)(2,1)S(1)}, bf16[2,48,384]{2,1,0:T(8,128)(2,1)S(1)}, u32[]{:S(2)}, u32[]{:S(2)}) collective-permute-start(bf16[2,48,384]{2,1,0:T(8,128)(2,1)S(1)} %dynamic-slice_bitcast_fusion.14), channel_id=1, source_target_pairs={{0,16},{2,18},{4,20},{6,22},{8,24},{10,26},{12,28},{14,30},{16,0},... | collective-permute-start | bytes 221192 | tf_op jit(solution)/shard_map/ppermute | solution.py:633
  203.4 12.6 %collective-permute-start.36 = (bf16[48,384]{1,0:T(8,128)(2,1)}, bf16[48,384]{1,0:T(8,128)(2,1)}, u32[]{:S(2)}, u32[]{:S(2)}) collective-permute-start(bf16[48,384]{1,0:T(8,128)(2,1)} %dynamic-slice_bitcast_fusion.18), channel_id=1, source_target_pairs={{0,2},{2,0},{4,6},{6,4},{8,10},{10,8},{12,14},{14,12},{16,18},{18,... | collective-permute-start | bytes 110600 | tf_op jit(solution)/shard_map/ppermute | solution.py:633
  211.8 17.2 %collective-permute-start.37 = (bf16[768,1536]{1,0:T(8,128)(2,1)}, bf16[768,1536]{1,0:T(8,128)(2,1)S(1)}, u32[]{:S(2)}, u32[]{:S(2)}) collective-permute-start(bf16[768,1536]{1,0:T(8,128)(2,1)} %get-tuple-element.79), channel_id=1, source_target_pairs={{0,1},{1,0},{2,3},{3,2},{4,5},{5,4},{6,7},{7,6},{8,9},{9,8},{10,11... | collective-permute-start | bytes 7077896 | tf_op jit(solution)/shard_map/ppermute | solution.py:633
  215.3 8.2 %collective-permute-start.22 = (bf16[768,384]{1,0:T(8,128)(2,1)}, bf16[768,384]{1,0:T(8,128)(2,1)S(1)}, u32[]{:S(2)}, u32[]{:S(2)}) collective-permute-start(bf16[768,384]{1,0:T(8,128)(2,1)} %get-tuple-element.72), channel_id=1, source_target_pairs={{0,1},{1,0},{2,3},{3,2},{4,5},{5,4},{6,7},{7,6},{8,9},{9,8},{10,11... | collective-permute-start | bytes 1769480 | tf_op jit(solution)/shard_map/ppermute | solution.py:633
  221.2 80.1 %collective-permute-start.12 = (bf16[768,1152]{1,0:T(8,128)(2,1)}, bf16[768,1152]{1,0:T(8,128)(2,1)S(1)}, u32[]{:S(2)}, u32[]{:S(2)}) collective-permute-start(bf16[768,1152]{1,0:T(8,128)(2,1)} %get-tuple-element.68), channel_id=1, source_target_pairs={{0,1},{1,0},{2,3},{3,2},{4,5},{5,4},{6,7},{7,6},{8,9},{9,8},{10,11... | collective-permute-start | bytes 5308424 | tf_op jit(solution)/shard_map/ppermute | solution.py:633
  223.4 16.3 %collective-permute-start.28 = (bf16[2,2,2,48,768]{4,3,0,1,2:T(8,128)(2,1)S(1)}, bf16[2,2,2,48,768]{4,3,0,1,2:T(8,128)(2,1)S(1)}, u32[]{:S(2)}, u32[]{:S(2)}) collective-permute-start(bf16[2,2,2,48,768]{4,3,0,1,2:T(8,128)(2,1)S(1)} %bitcast.204), channel_id=1, source_target_pairs={{0,2},{2,0},{4,6},{6,4},{8,10},{10,8},{12,14},{14,12},{16,18},{18,... | collective-permute-start | bytes 1769480 | tf_op jit(solution)/shard_map/ppermute | solution.py:633
  225.2 8.7 %collective-permute-start.23 = (bf16[2,2,2,48,384]{4,3,2,0,1:T(8,128)(2,1)S(1)}, bf16[2,2,2,48,384]{4,3,2,0,1:T(8,128)(2,1)S(1)}, u32[]{:S(2)}, u32[]{:S(2)}) collective-permute-start(bf16[2,2,2,48,384]{4,3,2,0,1:T(8,128)(2,1)S(1)} %bitcast.205), channel_id=1, source_target_pairs={{0,4},{2,6},{4,0},{6,2},{8,12},{10,14},{12,8},{14,10},{16,20},{18,... | collective-permute-start | bytes 884744 | tf_op jit(solution)/shard_map/ppermute | solution.py:633
  226.7 9.9 %collective-permute-start.18 = (bf16[2,2,2,48,384]{4,3,1,2,0:T(8,128)(2,1)S(1)}, bf16[2,2,2,48,384]{4,3,1,2,0:T(8,128)(2,1)S(1)}, u32[]{:S(2)}, u32[]{:S(2)}) collective-permute-start(bf16[2,2,2,48,384]{4,3,1,2,0:T(8,128)(2,1)S(1)} %bitcast.206), channel_id=1, source_target_pairs={{0,8},{2,10},{4,12},{6,14},{8,0},{10,2},{12,4},{14,6},{16,24},{18,... | collective-permute-start | bytes 884744 | tf_op jit(solution)/shard_map/ppermute | solution.py:633
  229.1 72.6 %collective-permute-start.43 = (bf16[2,2,2,192,384]{4,3,1,2,0:T(8,128)(2,1)S(1)}, bf16[2,2,2,192,384]{4,3,1,2,0:T(8,128)(2,1)S(1)}, u32[]{:S(2)}, u32[]{:S(2)}) collective-permute-start(bf16[2,2,2,192,384]{4,3,1,2,0:T(8,128)(2,1)S(1)} %bitcast.194), channel_id=1, source_target_pairs={{0,8},{2,10},{4,12},{6,14},{8,0},{10,2},{12,4},{14,6},{16,24},{18,... | collective-permute-start | bytes 3538952 | tf_op jit(solution)/shard_map/ppermute | solution.py:633
  233.9 68.3 %collective-permute-start.38 = (bf16[2,2,2,48,1536]{4,3,0,1,2:T(8,128)(2,1)S(1)}, bf16[2,2,2,48,1536]{4,3,0,1,2:T(8,128)(2,1)S(1)}, u32[]{:S(2)}, u32[]{:S(2)}) collective-permute-start(bf16[2,2,2,48,1536]{4,3,0,1,2:T(8,128)(2,1)S(1)} %bitcast.195), channel_id=1, source_target_pairs={{0,2},{2,0},{4,6},{6,4},{8,10},{10,8},{12,14},{14,12},{16,18},{18,... | collective-permute-start | bytes 3538952 | tf_op jit(solution)/shard_map/ppermute | solution.py:633
  236.6 30.1 %collective-permute-start.24 = (bf16[2,2,48,384]{3,2,1,0:T(8,128)(2,1)S(1)}, bf16[2,2,48,384]{3,2,1,0:T(8,128)(2,1)S(1)}, u32[]{:S(2)}, u32[]{:S(2)}) collective-permute-start(bf16[2,2,48,384]{3,2,1,0:T(8,128)(2,1)S(1)} %dynamic-slice_bitcast_fusion.11), channel_id=1, source_target_pairs={{0,8},{2,10},{4,12},{6,14},{8,0},{10,2},{12,4},{14,6},{16,24},{18,... | collective-permute-start | bytes 442376 | tf_op jit(solution)/shard_map/ppermute | solution.py:633
  239.7 28.1 %collective-permute-start.19 = (bf16[2,2,48,384]{3,2,0,1:T(8,128)(2,1)S(1)}, bf16[2,2,48,384]{3,2,0,1:T(8,128)(2,1)S(1)}, u32[]{:S(2)}, u32[]{:S(2)}) collective-permute-start(bf16[2,2,48,384]{3,2,0,1:T(8,128)(2,1)S(1)} %dynamic-slice_bitcast_fusion.12), channel_id=1, source_target_pairs={{0,16},{2,18},{4,20},{6,22},{8,24},{10,26},{12,28},{14,30},{16,0},... | collective-permute-start | bytes 442376 | tf_op jit(solution)/shard_map/ppermute | solution.py:633
  266.7 12.7 %collective-permute-start.29 = (bf16[2,2,48,768]{3,2,0,1:T(8,128)(2,1)S(1)}, bf16[2,2,48,768]{3,2,0,1:T(8,128)(2,1)S(1)}, u32[]{:S(2)}, u32[]{:S(2)}) collective-permute-start(bf16[2,2,48,768]{3,2,0,1:T(8,128)(2,1)S(1)} %dynamic-slice_bitcast_fusion.5), channel_id=1, source_target_pairs={{0,4},{2,6},{4,0},{6,2},{8,12},{10,14},{12,8},{14,10},{16,20},{18,... | collective-permute-start | bytes 884744 | tf_op jit(solution)/shard_map/ppermute | solution.py:633
  267.8 6.1 %collective-permute-start.25 = (bf16[2,48,384]{2,1,0:T(8,128)(2,1)S(1)}, bf16[2,48,384]{2,1,0:T(8,128)(2,1)S(1)}, u32[]{:S(2)}, u32[]{:S(2)}) collective-permute-start(bf16[2,48,384]{2,1,0:T(8,128)(2,1)S(1)} %dynamic-slice_bitcast_fusion.16), channel_id=1, source_target_pairs={{0,16},{2,18},{4,20},{6,22},{8,24},{10,26},{12,28},{14,30},{16,0},... | collective-permute-start | bytes 221192 | tf_op jit(solution)/shard_map/ppermute | solution.py:633
  279.4 9.4 %collective-permute-start.21 = (bf16[48,384]{1,0:T(8,128)(2,1)S(1)}, bf16[48,384]{1,0:T(8,128)(2,1)S(1)}, u32[]{:S(2)}, u32[]{:S(2)}) collective-permute-start(bf16[48,384]{1,0:T(8,128)(2,1)S(1)} %dynamic-slice_bitcast_fusion.20), channel_id=1, source_target_pairs={{0,4},{2,6},{4,0},{6,2},{8,12},{10,14},{12,8},{14,10},{16,20},{18,... | collective-permute-start | bytes 110600 | tf_op jit(solution)/shard_map/ppermute | solution.py:633
  287.4 13.2 %collective-permute-start.31 = (bf16[48,768]{1,0:T(8,128)(2,1)S(1)}, bf16[48,768]{1,0:T(8,128)(2,1)S(1)}, u32[]{:S(2)}, u32[]{:S(2)}) collective-permute-start(bf16[48,768]{1,0:T(8,128)(2,1)S(1)} %dynamic-slice_bitcast_fusion.15), channel_id=1, source_target_pairs={{0,16},{2,18},{4,20},{6,22},{8,24},{10,26},{12,28},{14,30},{16,0},... | collective-permute-start | bytes 221192 | tf_op jit(solution)/shard_map/ppermute | solution.py:633
  302.1 15.7 %collective-permute-start.44 = (bf16[2,2,192,384]{3,2,0,1:T(8,128)(2,1)S(1)}, bf16[2,2,192,384]{3,2,0,1:T(8,128)(2,1)S(1)}, u32[]{:S(2)}, u32[]{:S(2)}) collective-permute-start(bf16[2,2,192,384]{3,2,0,1:T(8,128)(2,1)S(1)} %dynamic-slice_bitcast_fusion), channel_id=1, source_target_pairs={{0,16},{2,18},{4,20},{6,22},{8,24},{10,26},{12,28},{14,30},{16,0},... | collective-permute-start | bytes 1769480 | tf_op jit(solution)/shard_map/ppermute | solution.py:633
  302.6 17.8 %collective-permute-start.39 = (bf16[2,2,48,1536]{3,2,0,1:T(8,128)(2,1)S(1)}, bf16[2,2,48,1536]{3,2,0,1:T(8,128)(2,1)S(1)}, u32[]{:S(2)}, u32[]{:S(2)}) collective-permute-start(bf16[2,2,48,1536]{3,2,0,1:T(8,128)(2,1)S(1)} %dynamic-slice_bitcast_fusion.1), channel_id=1, source_target_pairs={{0,4},{2,6},{4,0},{6,2},{8,12},{10,14},{12,8},{14,10},{16,20},{18,... | collective-permute-start | bytes 1769480 | tf_op jit(solution)/shard_map/ppermute | solution.py:633
  303.9 16.7 %collective-permute-start.13 = (bf16[2,2,2,48,1152]{4,3,0,1,2:T(8,128)(2,1)S(1)}, bf16[2,2,2,48,1152]{4,3,0,1,2:T(8,128)(2,1)S(1)}, u32[]{:S(2)}, u32[]{:S(2)}) collective-permute-start(bf16[2,2,2,48,1152]{4,3,0,1,2:T(8,128)(2,1)S(1)} %bitcast.196), channel_id=1, source_target_pairs={{0,2},{2,0},{4,6},{6,4},{8,10},{10,8},{12,14},{14,12},{16,18},{18,... | collective-permute-start | bytes 2654216 | tf_op jit(solution)/shard_map/ppermute | solution.py:633
  318.1 7.0 %collective-permute-start.45 = (bf16[2,192,384]{2,1,0:T(8,128)(2,1)S(1)}, bf16[2,192,384]{2,1,0:T(8,128)(2,1)S(1)}, u32[]{:S(2)}, u32[]{:S(2)}) collective-permute-start(bf16[2,192,384]{2,1,0:T(8,128)(2,1)S(1)} %dynamic-slice_bitcast_fusion.3), channel_id=1, source_target_pairs={{0,2},{2,0},{4,6},{6,4},{8,10},{10,8},{12,14},{14,12},{16,18},{18,... | collective-permute-start | bytes 884744 | tf_op jit(solution)/shard_map/ppermute | solution.py:633
  320.5 10.7 %collective-permute-start.40 = (bf16[2,48,1536]{2,1,0:T(8,128)(2,1)S(1)}, bf16[2,48,1536]{2,1,0:T(8,128)(2,1)S(1)}, u32[]{:S(2)}, u32[]{:S(2)}) collective-permute-start(bf16[2,48,1536]{2,1,0:T(8,128)(2,1)S(1)} %dynamic-slice_bitcast_fusion.4), channel_id=1, source_target_pairs={{0,8},{2,10},{4,12},{6,14},{8,0},{10,2},{12,4},{14,6},{16,24},{18,... | collective-permute-start | bytes 884744 | tf_op jit(solution)/shard_map/ppermute | solution.py:633
  320.9 10.7 %collective-permute-start.14 = (bf16[2,2,48,1152]{3,2,0,1:T(8,128)(2,1)S(1)}, bf16[2,2,48,1152]{3,2,0,1:T(8,128)(2,1)S(1)}, u32[]{:S(2)}, u32[]{:S(2)}) collective-permute-start(bf16[2,2,48,1152]{3,2,0,1:T(8,128)(2,1)S(1)} %dynamic-slice_bitcast_fusion.2), channel_id=1, source_target_pairs={{0,4},{2,6},{4,0},{6,2},{8,12},{10,14},{12,8},{14,10},{16,20},{18,... | collective-permute-start | bytes 1327112 | tf_op jit(solution)/shard_map/ppermute | solution.py:633
  325.2 15.9 %collective-permute-start.46 = (bf16[192,384]{1,0:T(8,128)(2,1)S(1)}, bf16[192,384]{1,0:T(8,128)(2,1)S(1)}, u32[]{:S(2)}, u32[]{:S(2)}) collective-permute-start(bf16[192,384]{1,0:T(8,128)(2,1)S(1)} %dynamic-slice_bitcast_fusion.7), channel_id=1, source_target_pairs={{0,4},{2,6},{4,0},{6,2},{8,12},{10,14},{12,8},{14,10},{16,20},{18,... | collective-permute-start | bytes 442376 | tf_op jit(solution)/shard_map/ppermute | solution.py:633
  331.4 8.8 %collective-permute-start.41 = (bf16[48,1536]{1,0:T(8,128)(2,1)S(1)}, bf16[48,1536]{1,0:T(8,128)(2,1)S(1)}, u32[]{:S(2)}, u32[]{:S(2)}) collective-permute-start(bf16[48,1536]{1,0:T(8,128)(2,1)S(1)} %dynamic-slice_bitcast_fusion.8), channel_id=1, source_target_pairs={{0,16},{2,18},{4,20},{6,22},{8,24},{10,26},{12,28},{14,30},{16,0},... | collective-permute-start | bytes 442376 | tf_op jit(solution)/shard_map/ppermute | solution.py:633
  331.8 9.1 %collective-permute-start.15 = (bf16[2,48,1152]{2,1,0:T(8,128)(2,1)S(1)}, bf16[2,48,1152]{2,1,0:T(8,128)(2,1)S(1)}, u32[]{:S(2)}, u32[]{:S(2)}) collective-permute-start(bf16[2,48,1152]{2,1,0:T(8,128)(2,1)S(1)} %dynamic-slice_bitcast_fusion.6), channel_id=1, source_target_pairs={{0,8},{2,10},{4,12},{6,14},{8,0},{10,2},{12,4},{14,6},{16,24},{18,... | collective-permute-start | bytes 663560 | tf_op jit(solution)/shard_map/ppermute | solution.py:633
  341.0 6.3 %collective-permute-start.16 = (bf16[48,1152]{1,0:T(8,128)(2,1)S(1)}, bf16[48,1152]{1,0:T(8,128)(2,1)S(1)}, u32[]{:S(2)}, u32[]{:S(2)}) collective-permute-start(bf16[48,1152]{1,0:T(8,128)(2,1)S(1)} %dynamic-slice_bitcast_fusion.13), channel_id=1, source_target_pairs={{0,16},{2,18},{4,20},{6,22},{8,24},{10,26},{12,28},{14,30},{16,0},... | collective-permute-start | bytes 331784 | tf_op jit(solution)/shard_map/ppermute | solution.py:633
  (33 other events, 242.4 us)

commit v2 on v1

--- a/solution.py
+++ b/solution.py
@@ -1,5 +1,4 @@
 import functools
-import math
 
 import jax
 import jax.numpy as jnp
@@ -46,6 +45,10 @@
     return (scaled - mean_one - unit * mean_two) * inverse
 
 
+def as_row(ref):
+    return ref[...].reshape(1, ref.shape[0])
+
+
 def iota(shape, dim):
     return lax.broadcasted_iota(jnp.int32, shape, dim)
 
@@ -104,7 +107,7 @@
 ):
     x = tok_ref[...].astype(F32)
     unit, _ = normalize(x)
-    normed = (unit * gain_one[...] + shift_one[...]).astype(BF16)
+    normed = (unit * as_row(gain_one) + as_row(shift_one)).astype(BF16)
     width = x.shape[1]
     qkv_ref[...] = dot(normed, qkv_mat[...]).astype(BF16)
     mask = same_head()
@@ -124,7 +127,7 @@
     hidden = x + dot(att_ref[...], out_mat[...])
     hidden_ref[...] = hidden
     unit, _ = normalize(hidden)
-    normed = (unit * gain_two[...] + shift_two[...]).astype(BF16)
+    normed = (unit * as_row(gain_two) + as_row(shift_two)).astype(BF16)
     query_ref[...] = (dot(normed, query_mat[...]).astype(BF16).astype(F32) * SCALE).astype(BF16)
 
 
@@ -141,8 +144,8 @@
         functools.partial(token_start_body, length=length),
         grid=(rows // tile,),
         in_specs=[
-            row_block(width), whole((1, width)), whole((1, width)), whole(qkv_mat.shape),
-            whole(out_mat.shape), whole((1, width)), whole((1, width)), whole(query_mat.shape),
+            row_block(width), whole((width,)), whole((width,)), whole(qkv_mat.shape),
+            whole(out_mat.shape), whole((width,)), whole((width,)), whole(query_mat.shape),
         ],
         out_specs=[row_block(3 * width), row_block(width), row_block(width), row_block(width)],
         out_shape=[
@@ -258,7 +261,7 @@
             two = hidden_ref[span, :] + dot(att_low[span, :], cross_mat[...])
             hidden_two[span, :] = two
             unit, _ = normalize(two)
-            normed_ref[span, :] = (unit * gain_ref[...] + shift_ref[...]).astype(BF16)
+            normed_ref[span, :] = (unit * as_row(gain_ref) + as_row(shift_ref)).astype(BF16)
             acc_out[span, :] = two
             acc_grad[span, :] = jnp.zeros_like(two)
             return carry
@@ -308,7 +311,7 @@
             grad = acc_grad[span, :]
             gain_grad[...] += jnp.sum(grad * unit, axis=0, keepdims=True)
             shift_grad[...] += jnp.sum(grad, axis=0, keepdims=True)
-            two = cot_ref[span, :].astype(F32) + norm_back(grad, gain_ref[...], unit, inverse)
+            two = cot_ref[span, :].astype(F32) + norm_back(grad, as_row(gain_ref), unit, inverse)
             grad_two_ref[span, :] = two
             low = two.astype(BF16)
             normed_ref[span, :] = low
@@ -361,7 +364,7 @@
             in_specs=[
                 whole((rows, width)), whole(stat), whole((rows, width)), whole(stat),
                 whole((rows, width)), whole((rows, width)), whole((width, width)),
-                whole((1, width)), whole((1, width)),
+                whole((width,)), whole((width,)),
                 pl.BlockSpec((width, chunk), lambda i, *_: (0, i)),
                 pl.BlockSpec((chunk, width), lambda i, *_: (i, 0)),
             ],
@@ -465,54 +468,6 @@
     )(valid, kv, queries, grads, lse, delta, kv_mat)
 
 
-def image_weight_body(side_ref, img_ref, grad_ref, mine_ref, send_ref, acc_ref):
-    step = pl.program_id(0)
-
-    @pl.when(step == 0)
-    def _():
-        acc_ref[...] = jnp.zeros_like(acc_ref)
-
-    acc_ref[...] += dot_tn(img_ref[...], grad_ref[...])
-
-    @pl.when(step == pl.num_programs(0) - 1)
-    def _():
-        half = acc_ref.shape[1] // 2
-        side = side_ref[0]
-
-        @pl.when(side == 0)
-        def _():
-            mine_ref[...] = acc_ref[:, :half].astype(BF16)
-            send_ref[...] = acc_ref[:, half:].astype(BF16)
-
-        @pl.when(side == 1)
-        def _():
-            mine_ref[...] = acc_ref[:, half:].astype(BF16)
-            send_ref[...] = acc_ref[:, :half].astype(BF16)
-
-
-def image_weight(side, images, grads):
-    rows, width = images.shape
-    double = grads.shape[1]
-    tile = 512 if rows % 512 == 0 else rows // 4
-    sds = jax.ShapeDtypeStruct
-    return pl.pallas_call(
-        image_weight_body,
-        grid_spec=pltpu.PrefetchScalarGridSpec(
-            num_scalar_prefetch=1,
-            grid=(rows // tile,),
-            in_specs=[
-                pl.BlockSpec((tile, width), lambda i, *_: (i, 0)),
-                pl.BlockSpec((tile, double), lambda i, *_: (i, 0)),
-            ],
-            out_specs=[whole((width, double // 2)), whole((width, double // 2))],
-            scratch_shapes=[pltpu.VMEM((width, double), F32)],
-        ),
-        out_shape=[sds((width, double // 2), BF16)] * 2,
-        compiler_params=pltpu.CompilerParams(vmem_limit_bytes=VMEM_LIMIT),
-        name="image_weight",
-    )(side, images, grads)
-
-
 def token_end_body(
     side_ref, back_one, back_two, hidden_ref, grad_two_ref, att_ref, qkv_ref, tok_ref,
     gain_one, shift_one, qkv_mat, out_mat, gain_two, shift_two, query_mat,
@@ -530,12 +485,12 @@
 
     back = (back_one[...].astype(F32) + back_two[...].astype(F32)).astype(BF16)
     unit, inverse = normalize(hidden_ref[...])
-    normed = (unit * gain_two[...] + shift_two[...]).astype(BF16)
+    normed = (unit * as_row(gain_two) + as_row(shift_two)).astype(BF16)
     acc_query[...] += dot_tn(normed, back)
     grad = dot_nt(back, query_mat[...])
     gains_ref[2:3] += jnp.sum(grad * unit, axis=0, keepdims=True)
     gains_ref[3:4] += jnp.sum(grad, axis=0, keepdims=True)
-    grad_one = grad_two_ref[...] + norm_back(grad, gain_two[...], unit, inverse)
+    grad_one = grad_two_ref[...] + norm_back(grad, as_row(gain_two), unit, inverse)
     low = grad_one.astype(BF16)
     acc_out[...] += dot_tn(att_ref[...], low)
     grad_att = dot_nt(low, out_mat[...]).astype(BF16)
@@ -563,12 +518,12 @@
                 probs.astype(BF16), cot
             ).astype(BF16)
     unit, inverse = normalize(tok_ref[...].astype(F32))
-    normed = (unit * gain_one[...] + shift_one[...]).astype(BF16)
+    normed = (unit * as_row(gain_one) + as_row(shift_one)).astype(BF16)
     acc_qkv[...] += dot_tn(normed, grad_qkv_ref[...])
     grad = dot_nt(grad_qkv_ref[...], qkv_mat[...])
     gains_ref[0:1] += jnp.sum(grad * unit, axis=0, keepdims=True)
     gains_ref[1:2] += jnp.sum(grad, axis=0, keepdims=True)
-    grad_tok_ref[...] = (grad_one + norm_back(grad, gain_one[...], unit, inverse)).astype(BF16)
+    grad_tok_ref[...] = (grad_one + norm_back(grad, as_row(gain_one), unit, inverse)).astype(BF16)
 
     @pl.when(step == pl.num_programs(0) - 1)
     def _():
@@ -607,8 +562,8 @@
             in_specs=[
                 row_block(width), row_block(width), row_block(width), row_block(width),
                 row_block(width), row_block(3 * width), row_block(width),
-                whole((1, width)), whole((1, width)), whole(qkv_mat.shape), whole(out_mat.shape),
-                whole((1, width)), whole((1, width)), whole(query_mat.shape),
+                whole((width,)), whole((width,)), whole(qkv_mat.shape), whole(out_mat.shape),
+                whole((width,)), whole((width,)), whole(query_mat.shape),
             ],
             out_specs=[row_block(width)] + [whole(s) for s in halves] + [whole((4, width))],
             scratch_shapes=[
@@ -629,16 +584,345 @@
     return (first.astype(F32) + second.astype(F32)).astype(BF16)
 
 
+class Piece:
+    def __init__(self, acc, recvs, out, col, bits, order, source=None, mine=None, send=None, kv_recv=None):
+        self.acc, self.recvs, self.out, self.col = acc, recvs, out, col
+        self.bits, self.order, self.source = bits, order, source
+        self.mine, self.send, self.kv_recv = mine, send, kv_recv
+        self.copies = 1 + len(order)
+        self.done = []
+
+    def columns(self, ref):
+        width = self.acc.shape[-1]
+        return (slice(None), pl.ds(self.col, width)) if ref.shape[-1] != width else (slice(None), slice(None))
+
+
+class Sums:
+    def __init__(self, send_sem, recv_sem, size):
+        self.send_sem, self.recv_sem, self.count, self.size = send_sem, recv_sem, 0, size
+        self.me, self.side = lax.axis_index("dp"), lax.axis_index("kv")
+
+    def own(self, bit):
+        return (self.me // (1 << bit)) % 2
+
+    def partner(self, bit):
+        return {"dp": self.me + (1 - 2 * self.own(bit)) * (1 << bit)}
+
+    def copy(self, src, dst, device):
+        index = self.count
+        self.count += 1
+        return pltpu.make_async_remote_copy(
+            src_ref=src, dst_ref=dst, send_sem=self.send_sem.at[index], recv_sem=self.recv_sem.at[index],
+            device_id=device, device_id_type=pl.DeviceIdType.MESH,
+        )
+
+    def greet(self, bits):
+        barrier = pltpu.get_barrier_semaphore()
+        for device in [{"kv": 1 - self.side}] + [self.partner(bit) for bit in bits]:
+            pl.semaphore_signal(barrier, inc=1, device_id=device, device_id_type=pl.DeviceIdType.MESH)
+        pl.semaphore_wait(barrier, 1 + len(bits))
+
+    def place(self, piece, now, value):
+        index = []
+        for bit in piece.bits:
+            if bit in piece.order[:now]:
+                index.append(self.own(bit))
+            elif bit == piece.order[now]:
+                index.append(value)
+            else:
+                index.append(slice(None))
+        return tuple(index)
+
+    def start_kv(self, piece):
+        piece.pending = self.copy(
+            piece.send.at[(slice(None),) * len(piece.bits) + piece.columns(piece.send)],
+            piece.kv_recv, {"kv": 1 - self.side},
+        )
+        piece.pending.start()
+
+    def end_kv(self, piece):
+        piece.pending.wait()
+        count = len(piece.bits)
+        cols = piece.columns(piece.mine)
+
+        def one(i, carry):
+            lead = tuple((i // (1 << (count - 1 - d))) % 2 for d in range(count))
+            piece.acc[lead] = add_low(piece.mine[lead + cols], piece.kv_recv[lead])
+            return carry
+
+        lax.fori_loop(0, 1 << count, one, 0)
+        piece.source = None
+
+    def start(self, piece, now):
+        bit = piece.order[now]
+        ref = piece.acc if piece.source is None else piece.source
+        lead = self.place(piece, now, 1 - self.own(bit))
+        piece.pending = self.copy(ref.at[lead + piece.columns(ref)], piece.recvs[now], self.partner(bit))
+        piece.pending.start()
+
+    def end(self, piece, now):
+        piece.pending.wait()
+        ref = piece.acc if piece.source is None else piece.source
+        cols = piece.columns(ref)
+        bit = piece.order[now]
+        left = [b for b in piece.bits if b not in piece.order[: now + 1]]
+        recv = piece.recvs[now]
+        if not left:
+            lead = self.place(piece, now, self.own(bit))
+            width = piece.acc.shape[-1]
+            piece.out[:, piece.col : piece.col + width] = ref[lead + cols].astype(F32) + recv[...].astype(F32)
+            return
+
+        def one(i, carry):
+            inner = {b: (i // (1 << (len(left) - 1 - d))) % 2 for d, b in enumerate(left)}
+            lead = tuple(inner[b] if b in inner else self.own(b) for b in piece.bits)
+            piece.acc[lead] = add_low(ref[lead + cols], recv[tuple(inner[b] for b in left)])
+            return carry
+
+        lax.fori_loop(0, 1 << len(left), one, 0)
+        piece.source = None
+
+
+def finish_body(
+    img_hbm, grad_hbm, up_ref, down_ref, cross_ref, qkv_mine, out_mine, query_mine,
+    qkv_send, out_send, query_send, gains_ref,
+    up_out, down_out, cross_out, qkv_out, out_out, query_out, kv_out, gains_out,
+    *scratch, plan, tile, size
+):
+    scratch = list(scratch)
+    send_sem, recv_sem, load_sem, img_buf, grad_buf, acc_kv, kv_mine, kv_send = scratch[:8]
+    gain_buf, gain_recv = scratch[8:10]
+    rest = scratch[10:]
+    sums = Sums(send_sem, recv_sem, size)
+    bits = list(range(size.bit_length() - 1))
+    named = dict(
+        up=(up_ref, None, None, up_out), down=(down_ref, None, None, down_out),
+        cross=(cross_ref, None, None, cross_out), qkv=(None, qkv_mine, qkv_send, qkv_out),
+        out=(None, out_mine, out_send, out_out), query=(None, query_mine, query_send, query_out),
+        kv=(None, kv_mine, kv_send, kv_out),
+    )
+    pieces = []
+    for name, col, width, piece_bits, order, kv in plan:
+        source, mine, send, out = named[name]
+        acc = rest.pop(0)
+        kv_recv = rest.pop(0) if kv else None
+        recvs = [rest.pop(0) for _ in order]
+        pieces.append((name, Piece(acc, recvs, out, col, piece_bits, order, source, mine, send, kv_recv)))
+    early = [p for n, p in pieces if n in ("up", "down", "cross")]
+    late = [p for n, p in pieces if n in ("qkv", "out", "query")]
+    image = [p for n, p in pieces if n == "kv"]
+
+    steps = img_hbm.shape[0] // tile
+
+    def load(step, slot):
+        rows = pl.ds(pl.multiple_of(step * tile, tile), tile)
+        return (
+            pltpu.make_async_copy(img_hbm.at[rows], img_buf.at[slot], load_sem.at[0, slot]),
+            pltpu.make_async_copy(grad_hbm.at[rows], grad_buf.at[slot], load_sem.at[1, slot]),
+        )
+
+    for copy in load(0, 0):
+        copy.start()
+    sums.greet(bits)
+    for piece in late:
+        sums.start_kv(piece)
+    for piece in early:
+        sums.start(piece, 0)
+    half = gains_ref.shape[1] // 2
+    gains_kv = sums.copy(gains_ref, gain_recv.at[0], {"kv": 1 - sums.side})
+    gains_kv.start()
+    acc_kv[...] = jnp.zeros_like(acc_kv)
+
+    def multiply(first, last):
+        def one(step, carry):
+            slot = step % 2
+
+            @pl.when(step + 1 < steps)
+            def _():
+                for copy in load(step + 1, 1 - slot):
+                    copy.start()
+
+            for copy in load(step, slot):
+                copy.wait()
+            acc_kv[...] += dot_tn(img_buf[slot], grad_buf[slot])
+            return carry
+
+        lax.fori_loop(first, last, one, 0)
+
+    multiply(0, min(3, steps))
+    for piece in late:
+        sums.end_kv(piece)
+        sums.start(piece, 0)
+    multiply(min(3, steps), steps)
+    gains_kv.wait()
+    total = gains_ref[...] + gain_recv[0]
+
+    @pl.when(sums.side == 0)
+    def _():
+        gain_buf[0] = total[:, :half]
+
+    @pl.when(sums.side == 1)
+    def _():
+        gain_buf[0] = total[:, half:]
+
+    def gain_start(now):
+        copy = sums.copy(gain_buf.at[now], gain_recv.at[now + 1, :, pl.ds(0, half)], sums.partner(bits[now]))
+        copy.start()
+        return copy
+
+    def gain_end(now, copy):
+        copy.wait()
+        gain_buf[now + 1] = gain_buf[now] + gain_recv[now + 1, :, :half]
+
+    gain_copy = gain_start(0)
+
+    def store_kv(ref, second):
+        count = len(bits)
+        rows = ref.shape[-2]
+        width = ref.shape[-1]
+
+        def one(i, carry):
+            lead = tuple((i // (1 << (count - 1 - d))) % 2 for d in range(count))
+            span = pl.ds(i * rows, rows)
+            ref[lead] = acc_kv[span, second * width : (second + 1) * width].astype(BF16)
+            return carry
+
+        if rows % 8 == 0:
+            lax.fori_loop(0, 1 << count, one, 0)
+        else:
+            for i in range(1 << count):
+                one(i, 0)
+
+    @pl.when(sums.side == 0)
+    def _():
+        store_kv(kv_mine, 0)
+        store_kv(kv_send, 1)
+
+    @pl.when(sums.side == 1)
+    def _():
+        store_kv(kv_mine, 1)
+        store_kv(kv_send, 0)
+
+    for piece in image:
+        sums.start_kv(piece)
+    for now in range(len(bits)):
+        for piece in early:
+            if now < len(piece.order):
+                sums.end(piece, now)
+                if now + 1 < len(piece.order):
+                    sums.start(piece, now + 1)
+        for piece in image:
+            if now == 0:
+                sums.end_kv(piece)
+            else:
+                sums.end(piece, now - 1)
+            sums.start(piece, now)
+        gain_end(now, gain_copy)
+        if now + 1 < len(bits):
+            gain_copy = gain_start(now + 1)
+        for piece in late:
+            sums.end(piece, now)
+            if now + 1 < len(bits):
+                sums.start(piece, now + 1)
+    for piece in image:
+        sums.end(piece, len(bits) - 1)
+    gains_out[...] = gain_buf[len(bits)]
+
+
+def hand_over_body(*refs):
+    count = len(refs) // 2
+    for source, target in zip(refs[:count], refs[count:]):
+        target[...] = source[...]
+
+
+def hand_over(*arrays):
+    vmem = pl.BlockSpec(memory_space=pltpu.VMEM)
+    return pl.pallas_call(
+        hand_over_body,
+        in_specs=[vmem] * len(arrays),
+        out_specs=[vmem] * len(arrays),
+        out_shape=[jax.ShapeDtypeStruct(v.shape, v.dtype) for v in arrays],
+        name="hand_over",
+    )(*arrays)
+
+
+def finish(images, grads, early, mines, sends, gains, size):
+    bits = list(range(size.bit_length() - 1))
+    down_bits = bits[::-1]
+    left = bits[-2:]
+    left_down = left[::-1]
+    forward = bits
+    turned = bits[1:2] + bits[0:1] + bits[2:]
+    rows, width = images.shape
+    double = grads.shape[1]
+    tile = 512 if rows % 512 == 0 else rows // 4
+    up, down, cross = early
+    qkv, out, query = mines
+    split = (qkv.shape[-1] // 256 + 1) * 128
+    plan = [
+        ("up", 0, up.shape[-1], left_down, left, False),
+        ("down", 0, down.shape[-1], left_down, left, False),
+        ("cross", 0, cross.shape[-1], left_down, left, False),
+        ("qkv", 0, split, down_bits, forward, True),
+        ("qkv", split, qkv.shape[-1] - split, down_bits, turned, True),
+        ("out", 0, out.shape[-1], down_bits, forward, True),
+        ("query", 0, query.shape[-1], down_bits, turned, True),
+        ("kv", 0, double // 4, down_bits, forward, True),
+        ("kv", double // 4, double // 4, down_bits, turned, True),
+    ]
+    shapes = dict(up=up, down=down, cross=cross, qkv=qkv, out=out, query=query)
+    lead = (2,) * len(bits)
+    kv_shape = lead + (width // size, double // 2)
+    buffers = []
+    copies = 1 + len(bits)
+    for name, col, cols, piece_bits, order, kv in plan:
+        block = (kv_shape if name == "kv" else shapes[name].shape)[-2]
+        full = (2,) * len(piece_bits) + (block, cols)
+        buffers.append(pltpu.VMEM(full, BF16))
+        if kv:
+            buffers.append(pltpu.VMEM(full, BF16))
+            copies += 1
+        for now in range(len(order)):
+            buffers.append(pltpu.VMEM((2,) * (len(piece_bits) - now - 1) + (block, cols), BF16))
+            copies += 1
+    vmem = pl.BlockSpec(memory_space=pltpu.VMEM)
+    hbm = pl.BlockSpec(memory_space=pl.ANY)
+    sds = jax.ShapeDtypeStruct
+    outs = [sds(v.shape[-2:], F32) for v in (up, down, cross, qkv, out, query)]
+    outs += [sds(kv_shape[-2:], F32), sds((gains.shape[0], width // 2), F32)]
+    return pl.pallas_call(
+        functools.partial(finish_body, plan=plan, tile=tile, size=size),
+        in_specs=[hbm, hbm] + [vmem] * 6 + [hbm] * 3 + [vmem],
+        out_specs=[vmem] * len(outs),
+        out_shape=outs,
+        scratch_shapes=[
+            pltpu.SemaphoreType.DMA((copies,)), pltpu.SemaphoreType.DMA((copies,)),
+            pltpu.SemaphoreType.DMA((2, 2)),
+            pltpu.VMEM((2, tile, width), BF16), pltpu.VMEM((2, tile, double), BF16),
+            pltpu.VMEM((width, double), F32), pltpu.VMEM(kv_shape, BF16), pltpu.VMEM(kv_shape, BF16),
+            pltpu.VMEM((len(bits) + 1, gains.shape[0], width // 2), F32),
+            pltpu.VMEM((len(bits) + 1, gains.shape[0], width), F32),
+        ] + buffers,
+        compiler_params=pltpu.CompilerParams(
+            vmem_limit_bytes=VMEM_LIMIT, collective_id=0, has_side_effects=True
+        ),
+        name="finish",
+    )(images, grads, up, down, cross, qkv, out, query, *sends, gains)
+
+
 def exchange(value, axis, bit, size):
     return lax.ppermute(value, axis, [(i, i ^ bit) for i in range(size)])
 
 
-def reduce_blocks(mine, send, order, me, size):
+def split_rows(array, size):
+    bits = size.bit_length() - 1
+    return array.reshape((2,) * bits + (array.shape[0] // size, array.shape[1]))
+
+
+def reduce_some(mine, send, order, me, size):
     total = add_low(mine, exchange(send, "kv", 1, 2))
-    bits = size.bit_length() - 1
-    rows = total.shape[0] // size
-    total = total.reshape((2,) * bits + (rows, total.shape[1]))
-    left = list(range(bits))[::-1]
+    left = list(range(size.bit_length() - 1))[::-1]
+    total = split_rows(total, size)
     for bit in order:
         axis = left.index(bit)
         own = (me >> bit) & 1
@@ -646,7 +930,7 @@
         away = lax.dynamic_index_in_dim(total, 1 - own, axis, False)
         total = add_low(keep, exchange(away, "dp", 1 << bit, size))
         left.remove(bit)
-    return total.astype(F32)
+    return total
 
 
 def body(
@@ -659,7 +943,7 @@
     me = lax.axis_index("dp")
     groups = lax.axis_size("dp")
     side_arr = side.reshape(1)
-    row = lambda v: v.reshape(1, width)
+    row = lambda v: v
     tok = tokens.reshape(captions * length, width)
     cot = cotangent.reshape(captions * length, width)
     short = -(-SHORT // 16) * 16
@@ -694,20 +978,18 @@
         swap(other_part(lse_part)), hidden, cot, cross_out, row(norm3_gain), row(norm3_shift),
         w_up, w_down, length,
     )
-    bits = groups.bit_length() - 1
-    turn = lambda start: [(start + i) % bits for i in range(bits)]
-    w_up_grad = reduce_blocks(up_mine, up_send, turn(0), me, groups)
-    down_grad = reduce_blocks(down_mine, down_send, turn(bits // 2), me, groups)
-    cross_out_grad = reduce_blocks(cross_mine, cross_send, turn(bits // 4), me, groups)
+    first_bits = list(range(groups.bit_length() - 1))[:-2]
+    turned = first_bits[1:] + first_bits[:1]
+    early = [
+        reduce_some(up_mine, up_send, first_bits, me, groups),
+        reduce_some(down_mine, down_send, turned, me, groups),
+        reduce_some(cross_mine, cross_send, turned, me, groups),
+    ]
 
     grads = both(grad_att.reshape(captions, length, width))
     back, grad_kv, images_grad = cross_back(
         valid, kv, queries, grads, both(lse), both(delta), cross_kv, short
     )
-    kv_mine, kv_send = image_weight(
-        side_arr, images.reshape(caps * slots, width), grad_kv.reshape(caps * slots, 2 * width)
-    )
-    cross_kv_grad = reduce_blocks(kv_mine, kv_send, turn(0), me, groups)
     (
         tokens_grad, qkv_mine, qkv_send, out_mine, out_send, query_mine, query_send, gains,
     ) = token_end(
@@ -715,14 +997,16 @@
         tok, row(norm1_gain), row(norm1_shift), self_qkv, self_out, row(norm2_gain),
         row(norm2_shift), cross_q, length,
     )
-    self_qkv_grad = reduce_blocks(qkv_mine, qkv_send, turn(0), me, groups)
-    self_out_grad = reduce_blocks(out_mine, out_send, turn(bits // 2), me, groups)
-    cross_q_grad = reduce_blocks(query_mine, query_send, turn(bits // 4), me, groups)
-    gains = jnp.concatenate([gains, gain3, shift3], axis=0)
-    gains = gains + swap(gains)
-    gains = lax.dynamic_slice_in_dim(gains, side * (width // 2), width // 2, 1)
-    for bit in range(bits):
-        gains = gains + exchange(gains, "dp", 1 << bit, groups)
+    gains = jnp.concatenate([gains, gain3, shift3, jnp.zeros((2, width), F32)], axis=0)
+    cut = lambda v: split_rows(v, groups)
+    (
+        w_up_grad, down_grad, cross_out_grad, self_qkv_grad, self_out_grad, cross_q_grad,
+        cross_kv_grad, gains,
+    ) = hand_over(*finish(
+        images.reshape(caps * slots, width), grad_kv.reshape(caps * slots, 2 * width), early,
+        [cut(qkv_mine), cut(out_mine), cut(query_mine)],
+        [cut(qkv_send), cut(out_send), cut(query_send)], gains, groups,
+    ))
     return (
         layer_out.reshape(captions, length, width),
         tokens_grad.reshape(captions, length, width),

time: 356 us -> 267 us (0.75); the launches traced: 348 us -> 264 us
  waiting for transfers between devices: 105 us -> 19 us
  Pallas kernels: 161 us -> 207 us
  starting transfers between devices: 38.6 us -> 8.81 us
  local copies, waits for them, and re-layouts: 19.7 us -> 11.9 us
  other arithmetic: 22.4 us -> 16.2 us
    ppermute x47 -> x16, waiting for transfers between devices: 105 us -> 19 us  [exchange(): return lax.ppermute(value, axis, [(i, i ^ bit) for i in range(size)])]
    pallas_call x1 -> x2, Pallas kernels: 17.6 us -> 64.4 us  [the longest x1 62 us: finish(): pl.pallas_call(functools.partial(finish_body, plan=plan, tile=tile, size=...]
    ppermute x47 -> x16, starting transfers between devices: 38.6 us -> 8.81 us  [exchange(): return lax.ppermute(value, axis, [(i, i ^ bit) for i in range(size)])]
    reshape x6 -> x0, local copies, waits for them, and re-layouts: 6.25 us -> none  [body(): row = lambda v: v.reshape(1, width)]
    convert_element_type x7 -> x0, other arithmetic: 5.59 us -> none  [reduce_blocks(): return total.astype(F32)]
    convert_element_type x28 -> x9, other arithmetic: 8.73 us -> 8.76 us  [add_low(): return (first.astype(F32) + second.astype(F32)).astype(BF16)]
  transfers between devices with their start and end apart: 47 -> 16, of which waited for: 23 -> 5; matrix products, arithmetic and copies ran while one was open for 8% -> 7% of each run, Pallas kernels for 24% -> 25%
where the time goes in v2:
time: 267 us; the launch traced here: 264 us
  Pallas kernels  207 us (78%)
  waiting for transfers between devices  19 us (7%)
  other arithmetic  16.2 us (6%)
  local copies, waits for them, and re-layouts  11.9 us (4%)
  starting transfers between devices  8.81 us (3%)
    pallas_call x1, Pallas kernels, finish(): pl.pallas_call(functools.partial(finish_body, plan=plan, tile=tile, size=...  62 us
    pallas_call x1, Pallas kernels, cross_back(): pl.pallas_call(functools.partial(cross_back_body, short=short), grid_spec...  39.5 us
    pallas_call x1, Pallas kernels, feed(): pl.pallas_call(functools.partial(feed_body, length=length, tile=tile), gr...  34.2 us
    pallas_call x1, Pallas kernels, cross_start(): pl.pallas_call(functools.partial(cross_start_body, short=short), grid_spe...  30.8 us
    pallas_call x1, Pallas kernels, token_end(): pl.pallas_call(functools.partial(token_end_body, length=length), grid_spe...  25.9 us
    ppermute x16, waiting for transfers between devices, exchange(): return lax.ppermute(value, axis, [(i, i ^ bit) for i in range(size)])  19 us
    pallas_call x1, Pallas kernels, token_start(): pl.pallas_call(functools.partial(token_start_body, length=length), grid=(...  12.5 us
    ppermute x16, starting transfers between devices, exchange(): return lax.ppermute(value, axis, [(i, i ^ bit) for i in range(size)])  8.81 us
  transfers between devices with their start and end apart: 16, of which 5 were waited for; matrix products, arithmetic and copies ran while one was open for 7% of the time, Pallas kernels for 25%

profile of v2, /device:TPU:2, one launch (start us, length us, event | category | flops | bytes accessed | tf_op | source)
XLA Modules:
  0.0 264.0 jit_solution(9648655134140952360)
XLA Ops:
  0.7 12.5 %token_start.1 = (bf16[512,2304]{1,0:T(8,128)(2,1)}, bf16[512,768]{1,0:T(8,128)(2,1)}, f32[512,768]{1,0:T(8,128)}, bf16[512,768]{1,0:T(8,128)(2,1)}) custom-call(bf16[512,768]{1,0:T(8,128)(2,1)} %bitcast.65, f32[768]{0:T(1024)} %gain_one.3, f32[768]{0:T(1024)} %shift_one.3, bf16[768,2304]{1,0:T(8,128)(2,1)} %qkv_mat.3, bf16[768,768]{1,0:T(8,128)(2,1)} %out_mat.3, ...), custom_call_target="tpu_custom_call" | custom-call | tf_op jit(solution)/shard_map/token_start/pallas_call | solution.py:143
  13.7 2.0 collective-permute-done
  15.7 1.2 broadcast_select_fusion.3
  16.9 1.3 pad_maximum_fusion.query_ref
  18.2 30.8 %cross_start.1 = (bf16[16,288,1536]{2,1,0:T(8,128)(2,1)}, bf16[16,64,768]{2,1,0:T(8,128)(2,1)}, f32[16,3,256]{2,1,0:T(4,128)}) custom-call(s32[16]{0:T(128)} %subtract_clamp_fusion.valid_ref, bf16[16,288,768]{2,1,0:T(8,128)(2,1)} %img_ref.1, bf16[768,1536]{1,0:T(8,128)(2,1)} %kv_mat.3, bf16[16,64,768]{2,1,0:T(8,128)(2,1)} %pad_maximum_fusion.query_ref), custom_call_target="tpu_custom_call" | custom-call | tf_op jit(solution)/shard_map/cross_start/pallas_call | solution.py:201
  49.1 2.4 constant_dynamic-slice_fusion.9
  52.6 1.2 collective-permute-done.2.lse_two
  54.7 34.2 %feed.1 = (bf16[512,768]{1,0:T(8,128)(2,1)}, f32[512,768]{1,0:T(8,128)}, bf16[512,768]{1,0:T(8,128)(2,1)}, f32[8,3,256]{2,1,0:T(4,128)}, f32[8,3,256]{2,1,0:T(4,...) custom-call(s32[1]{0:T(128)} %bitcast.side_ref, ...), custom_call_target="tpu_custom_call" | custom-call | tf_op jit(solution)/shard_map/feed/pallas_call | solution.py:359
  90.1 3.6 %collective-permute-done.4 = f32[8,3,256]{2,1,0:T(4,128)S(1)} collective-permute-done((f32[8,3,256]{2,1,0:T(4,128)}, f32[8,3,256]{2,1,0:T(4,128)S(1)}, u32[]{:S(2)}, u32[]{:S(2)}) %collective-permute-start.4) | collective-permute-done | bytes 24608 | tf_op jit(solution)/shard_map/ppermute | solution.py:914
  93.9 0.8 broadcast_select_fusion.7
  94.6 0.8 broadcast_select_fusion.5
  96.1 1.3 add_convert_fusion.2
  97.5 1.6 collective-permute-start.14
  99.2 1.3 pad_maximum_fusion.1.grad_ref
  100.5 39.5 %cross_back.1 = (bf16[16,64,768]{2,1,0:T(8,128)(2,1)}, bf16[16,288,1536]{2,1,0:T(8,128)(2,1)}, bf16[16,288,768]{2,1,0:T(8,128)(2,1)}) custom-call(s32[16]{0:T(128)} %subtract_clamp_fusion.valid_ref, bf16[16,288,1536]{2,1,0:T(8,128)(2,1)} %get-tuple-element.68.kv_ref, bf16[16,64,768]{2,1,0:T(8,128)(2,1)} %pad_maximum_fusion.query_ref, ...), custom_call_target="tpu_custom_call" | custom-call | tf_op jit(solution)/shard_map/cross_back/pallas_call | solution.py:451
  140.1 2.6 constant_dynamic-slice_fusion.6
  142.7 1.9 collective-permute-start.15
  145.5 1.1 copy.55
  146.8 0.8 copy-done
  147.6 2.3 add_convert_fusion
  150.1 1.1 copy.54
  152.0 25.9 %token_end.1 = (bf16[512,768]{1,0:T(8,128)(2,1)}, bf16[768,1152]{1,0:T(8,128)(2,1)}, bf16[768,1152]{1,0:T(8,128)(2,1)}, bf16[768,384]{1,0:T(8,128)(2,1)}, bf16[7...) custom-call(s32[1]{0:T(128)} %bitcast.side_ref, ...), custom_call_target="tpu_custom_call" | custom-call | tf_op jit(solution)/shard_map/token_end/pallas_call | solution.py:557
  178.3 2.1 collective-permute-start.9
  180.4 1.6 fusion
  182.1 1.1 collective-permute-start.12
  183.9 9.9 %collective-permute-done.9 = bf16[2,2,48,1536]{3,2,1,0:T(8,128)(2,1)S(1)} collective-permute-done((bf16[2,2,48,1536]{3,2,1,0:T(8,128)(2,1)S(1)}, bf16[2,2,48,1536]{3,2,1,0:T(8,128)(2,1)S(1)}, u32[]{:S(2)}, u32[]{:S(2)}) %collective-permute-start.9) | collective-permute-done | bytes 589856 | tf_op jit(solution)/shard_map/ppermute | solution.py:914
  193.9 1.0 fusion.3.up_ref
  194.8 2.2 collective-permute-done.12
  197.1 1.0 fusion.2.down_ref
  198.0 62.0 %finish.1 = (f32[48,1536]{1,0:T(8,128)}, f32[192,384]{1,0:T(8,128)}, f32[48,384]{1,0:T(8,128)}, f32[48,1152]{1,0:T(8,128)}, f32[48,384]{1,0:T(8,128)}, /*index=5...) custom-call(bf16[4608,768]{1,0:T(8,128)(2,1)} %bitcast.61, bf16[4608,1536]{1,0:T(8,128)(2,1)} %bitcast.62, ...), custom_call_target="tpu_custom_call" | custom-call | tf_op jit(solution)/shard_map/finish/pallas_call | solution.py:893
  260.1 2.3 hand_over.1
  262.4 1.6 slice_reduce_fusion
  (60 shorter events, 8.1 us)
Async XLA Ops:
  0.6 12.6 %copy-start.9 = (s32[16]{0:T(128)S(1)}, s32[16]{0:T(128)}, u32[]{:S(2)}) copy-start(s32[16]{0:T(128)} %param.19) | copy-start | bytes 196
  13.2 2.5 collective-permute-start
  49.0 2.4 copy-start.4
  51.5 2.3 collective-permute-start.1
  52.1 1.7 collective-permute-start.2
  53.8 0.6 copy-start.5
  53.8 0.9 copy-start.3
  88.9 55.8 %collective-permute-start.7 = (bf16[768,1536]{1,0:T(8,128)(2,1)}, bf16[768,1536]{1,0:T(8,128)(2,1)S(1)}, u32[]{:S(2)}, u32[]{:S(2)}) collective-permute-start(bf16[768,1536]{1,0:T(8,128)(2,1)} %get-tuple-element.80), channel_id=1, source_target_pairs={{0,1},{1,0},{2,3},{3,2},{4,5},{5,4},{6,7},{7,6},{8,9},{9,8},{10,11... | collective-permute-start | bytes 7077896 | tf_op jit(solution)/shard_map/ppermute | solution.py:914
  89.1 4.6 %collective-permute-start.4 = (f32[8,3,256]{2,1,0:T(4,128)}, f32[8,3,256]{2,1,0:T(4,128)S(1)}, u32[]{:S(2)}, u32[]{:S(2)}) collective-permute-start(f32[8,3,256]{2,1,0:T(4,128)} %get-tuple-element.70), channel_id=1, source_target_pairs={{0,1},{1,0},{2,3},{3,2},{4,5},{5,4},{6,7},{7,6},{8,9},{9,8},{10,11... | collective-permute-start | bytes 73736 | tf_op jit(solution)/shard_map/ppermute | solution.py:914
  89.4 6.7 %collective-permute-start.13 = (bf16[768,384]{1,0:T(8,128)(2,1)}, bf16[768,384]{1,0:T(8,128)(2,1)S(1)}, u32[]{:S(2)}, u32[]{:S(2)}) collective-permute-start(bf16[768,384]{1,0:T(8,128)(2,1)} %get-tuple-element.84), channel_id=1, source_target_pairs={{0,1},{1,0},{2,3},{3,2},{4,5},{5,4},{6,7},{7,6},{8,9},{9,8},{10,11... | collective-permute-start | bytes 1769480 | tf_op jit(solution)/shard_map/ppermute | solution.py:914
  89.6 5.1 %collective-permute-start.5 = (f32[8,3,256]{2,1,0:T(4,128)}, f32[8,3,256]{2,1,0:T(4,128)S(1)}, u32[]{:S(2)}, u32[]{:S(2)}) collective-permute-start(f32[8,3,256]{2,1,0:T(4,128)} %get-tuple-element.71), channel_id=1, source_target_pairs={{0,1},{1,0},{2,3},{3,2},{4,5},{5,4},{6,7},{7,6},{8,9},{9,8},{10,11... | collective-permute-start | bytes 73736 | tf_op jit(solution)/shard_map/ppermute | solution.py:914
  89.9 9.2 %collective-permute-start.3 = (bf16[8,64,768]{2,1,0:T(8,128)(2,1)}, bf16[8,64,768]{2,1,0:T(8,128)(2,1)S(1)}, u32[]{:S(2)}, u32[]{:S(2)}) collective-permute-start(bf16[8,64,768]{2,1,0:T(8,128)(2,1)} %bitcast.72), channel_id=1, source_target_pairs={{0,1},{1,0},{2,3},{3,2},{4,5},{5,4},{6,7},{7,6},{8,9},{9,8},{10,11... | collective-permute-start | bytes 2359304 | tf_op jit(solution)/shard_map/ppermute | solution.py:914
  93.7 53.1 %collective-permute-start.10 = (bf16[3072,384]{1,0:T(8,128)(2,1)}, bf16[3072,384]{1,0:T(8,128)(2,1)}, u32[]{:S(2)}, u32[]{:S(2)}) collective-permute-start(bf16[3072,384]{1,0:T(8,128)(2,1)} %get-tuple-element.82), channel_id=1, source_target_pairs={{0,1},{1,0},{2,3},{3,2},{4,5},{5,4},{6,7},{7,6},{8,9},{9,8},{10,11... | collective-permute-start | bytes 7077896 | tf_op jit(solution)/shard_map/ppermute | solution.py:914
  96.1 3.0 %copy-start.2 = (bf16[512,768]{1,0:T(8,128)(2,1)S(1)}, bf16[512,768]{1,0:T(8,128)(2,1)}, u32[]{:S(2)}) copy-start(bf16[512,768]{1,0:T(8,128)(2,1)} %get-tuple-element.69) | copy-start | bytes 2359300
  97.5 45.1 %collective-permute-start.14 = (bf16[2,2,2,48,384]{4,3,1,0,2:T(8,128)(2,1)S(1)}, bf16[2,2,2,48,384]{4,3,1,0,2:T(8,128)(2,1)S(1)}, u32[]{:S(2)}, u32[]{:S(2)}) collective-permute-start(bf16[2,2,2,48,384]{4,3,1,0,2:T(8,128)(2,1)S(1)} %bitcast.82), channel_id=1, source_target_pairs={{0,4},{2,6},{4,0},{6,2},{8,12},{10,14},{12,8},{14,10},{16,20},{18,... | collective-permute-start | bytes 884744 | tf_op jit(solution)/shard_map/ppermute | solution.py:914
  140.1 4.6 %copy-start.1 = (bf16[768,1536]{1,0:T(8,128)(2,1)S(1)}, bf16[768,1536]{1,0:T(8,128)(2,1)}, u32[]{:S(2)}) copy-start(bf16[768,1536]{1,0:T(8,128)(2,1)} %get-tuple-element.79) | copy-start | bytes 7077892
  142.6 9.4 %collective-permute-start.6 = (bf16[8,64,768]{2,1,0:T(8,128)(2,1)S(1)}, bf16[8,64,768]{2,1,0:T(8,128)(2,1)}, u32[]{:S(2)}, u32[]{:S(2)}) collective-permute-start(bf16[8,64,768]{2,1,0:T(8,128)(2,1)S(1)} %get-tuple-element.120), channel_id=1, source_target_pairs={{0,1},{1,0},{2,3},{3,2},{4,5},{5,4},{6,7},{7,6},{8,9},{9,8},{10,11... | collective-permute-start | bytes 2359304 | tf_op jit(solution)/shard_map/ppermute | solution.py:914
  142.7 8.6 %collective-permute-start.15 = (bf16[2,2,48,384]{3,2,1,0:T(8,128)(2,1)S(1)}, bf16[2,2,48,384]{3,2,1,0:T(8,128)(2,1)S(1)}, u32[]{:S(2)}, u32[]{:S(2)}) collective-permute-start(bf16[2,2,48,384]{3,2,1,0:T(8,128)(2,1)S(1)} %dynamic-slice_bitcast_fusion.2), channel_id=1, source_target_pairs={{0,2},{2,0},{4,6},{6,4},{8,10},{10,8},{12,14},{14,12},{16,18},{18,... | collective-permute-start | bytes 442376 | tf_op jit(solution)/shard_map/ppermute | solution.py:914
  145.5 2.1 copy-start
  146.6 31.4 %collective-permute-start.8 = (bf16[2,2,2,48,1536]{4,3,1,0,2:T(8,128)(2,1)}, bf16[2,2,2,48,1536]{4,3,1,0,2:T(8,128)(2,1)S(1)}, u32[]{:S(2)}, u32[]{:S(2)}) collective-permute-start(bf16[2,2,2,48,1536]{4,3,1,0,2:T(8,128)(2,1)} %bitcast.59), channel_id=1, source_target_pairs={{0,2},{2,0},{4,6},{6,4},{8,10},{10,8},{12,14},{14,12},{16,18},{18,... | collective-permute-start | bytes 3538952 | tf_op jit(solution)/shard_map/ppermute | solution.py:914
  151.2 29.2 %collective-permute-start.11 = (bf16[2,2,2,192,384]{4,3,1,0,2:T(8,128)(2,1)}, bf16[2,2,2,192,384]{4,3,1,0,2:T(8,128)(2,1)}, u32[]{:S(2)}, u32[]{:S(2)}) collective-permute-start(bf16[2,2,2,192,384]{4,3,1,0,2:T(8,128)(2,1)} %bitcast.58), channel_id=1, source_target_pairs={{0,4},{2,6},{4,0},{6,2},{8,12},{10,14},{12,8},{14,10},{16,20},{18,... | collective-permute-start | bytes 3538952 | tf_op jit(solution)/shard_map/ppermute | solution.py:914
  178.3 15.5 %collective-permute-start.9 = (bf16[2,2,48,1536]{3,2,1,0:T(8,128)(2,1)S(1)}, bf16[2,2,48,1536]{3,2,1,0:T(8,128)(2,1)S(1)}, u32[]{:S(2)}, u32[]{:S(2)}) collective-permute-start(bf16[2,2,48,1536]{3,2,1,0:T(8,128)(2,1)S(1)} %dynamic-slice_bitcast_fusion.1), channel_id=1, source_target_pairs={{0,4},{2,6},{4,0},{6,2},{8,12},{10,14},{12,8},{14,10},{16,20},{18,... | collective-permute-start | bytes 1769480 | tf_op jit(solution)/shard_map/ppermute | solution.py:914
  180.4 2.8 %copy-start.6 = (f32[4,768]{1,0:T(4,128)S(1)}, f32[4,768]{1,0:T(4,128)}, u32[]{:S(2)}) copy-start(f32[4,768]{1,0:T(4,128)} %get-tuple-element.91) | copy-start | bytes 36868
  180.4 2.8 %copy-start.7 = (f32[1,768]{1,0:T(1,128)S(1)}, f32[1,768]{1,0:T(1,128)}, u32[]{:S(2)}) copy-start(f32[1,768]{1,0:T(1,128)} %get-tuple-element.92) | copy-start | bytes 9220
  180.4 2.8 %copy-start.8 = (f32[1,768]{1,0:T(1,128)S(1)}, f32[1,768]{1,0:T(1,128)}, u32[]{:S(2)}) copy-start(f32[1,768]{1,0:T(1,128)} %get-tuple-element.93) | copy-start | bytes 9220
  182.1 15.0 %collective-permute-start.12 = (bf16[2,2,192,384]{3,2,1,0:T(8,128)(2,1)S(1)}, bf16[2,2,192,384]{3,2,1,0:T(8,128)(2,1)S(1)}, u32[]{:S(2)}, u32[]{:S(2)}) collective-permute-start(bf16[2,2,192,384]{3,2,1,0:T(8,128)(2,1)S(1)} %dynamic-slice_bitcast_fusion), channel_id=1, source_target_pairs={{0,2},{2,0},{4,6},{6,4},{8,10},{10,8},{12,14},{14,12},{16,18},{18,... | collective-permute-start | bytes 1769480 | tf_op jit(solution)/shard_map/ppermute | solution.py:914

commit v3 on v1

--- a/solution.py
+++ b/solution.py
@@ -1,5 +1,4 @@
 import functools
-import math
 
 import jax
 import jax.numpy as jnp
@@ -19,6 +18,7 @@
 F32 = jnp.float32
 BF16 = jnp.bfloat16
 VMEM_LIMIT = 60 * 1024 * 1024
+VMEM_MOST = 67043328
 
 
 def dot(a, b):
@@ -44,6 +44,10 @@
     mean_one = jnp.mean(scaled, axis=-1, keepdims=True)
     mean_two = jnp.mean(scaled * unit, axis=-1, keepdims=True)
     return (scaled - mean_one - unit * mean_two) * inverse
+
+
+def as_row(ref):
+    return ref[...].reshape(1, ref.shape[0])
 
 
 def iota(shape, dim):
@@ -104,7 +108,7 @@
 ):
     x = tok_ref[...].astype(F32)
     unit, _ = normalize(x)
-    normed = (unit * gain_one[...] + shift_one[...]).astype(BF16)
+    normed = (unit * as_row(gain_one) + as_row(shift_one)).astype(BF16)
     width = x.shape[1]
     qkv_ref[...] = dot(normed, qkv_mat[...]).astype(BF16)
     mask = same_head()
@@ -124,7 +128,7 @@
     hidden = x + dot(att_ref[...], out_mat[...])
     hidden_ref[...] = hidden
     unit, _ = normalize(hidden)
-    normed = (unit * gain_two[...] + shift_two[...]).astype(BF16)
+    normed = (unit * as_row(gain_two) + as_row(shift_two)).astype(BF16)
     query_ref[...] = (dot(normed, query_mat[...]).astype(BF16).astype(F32) * SCALE).astype(BF16)
 
 
@@ -141,8 +145,8 @@
         functools.partial(token_start_body, length=length),
         grid=(rows // tile,),
         in_specs=[
-            row_block(width), whole((1, width)), whole((1, width)), whole(qkv_mat.shape),
-            whole(out_mat.shape), whole((1, width)), whole((1, width)), whole(query_mat.shape),
+            row_block(width), whole((width,)), whole((width,)), whole(qkv_mat.shape),
+            whole(out_mat.shape), whole((width,)), whole((width,)), whole(query_mat.shape),
         ],
         out_specs=[row_block(3 * width), row_block(width), row_block(width), row_block(width)],
         out_shape=[
@@ -258,7 +262,7 @@
             two = hidden_ref[span, :] + dot(att_low[span, :], cross_mat[...])
             hidden_two[span, :] = two
             unit, _ = normalize(two)
-            normed_ref[span, :] = (unit * gain_ref[...] + shift_ref[...]).astype(BF16)
+            normed_ref[span, :] = (unit * as_row(gain_ref) + as_row(shift_ref)).astype(BF16)
             acc_out[span, :] = two
             acc_grad[span, :] = jnp.zeros_like(two)
             return carry
@@ -308,7 +312,7 @@
             grad = acc_grad[span, :]
             gain_grad[...] += jnp.sum(grad * unit, axis=0, keepdims=True)
             shift_grad[...] += jnp.sum(grad, axis=0, keepdims=True)
-            two = cot_ref[span, :].astype(F32) + norm_back(grad, gain_ref[...], unit, inverse)
+            two = cot_ref[span, :].astype(F32) + norm_back(grad, as_row(gain_ref), unit, inverse)
             grad_two_ref[span, :] = two
             low = two.astype(BF16)
             normed_ref[span, :] = low
@@ -361,7 +365,7 @@
             in_specs=[
                 whole((rows, width)), whole(stat), whole((rows, width)), whole(stat),
                 whole((rows, width)), whole((rows, width)), whole((width, width)),
-                whole((1, width)), whole((1, width)),
+                whole((width,)), whole((width,)),
                 pl.BlockSpec((width, chunk), lambda i, *_: (0, i)),
                 pl.BlockSpec((chunk, width), lambda i, *_: (i, 0)),
             ],
@@ -394,13 +398,19 @@
 
 
 def cross_back_body(
-    valid_ref, kv_ref, query_ref, grad_ref, lse_ref, delta_ref, kv_mat,
-    grad_query_ref, grad_kv_ref, grad_img_ref, *, short
+    valid_ref, side_ref, kv_ref, query_ref, grad_ref, lse_ref, delta_ref, kv_mat, img_ref,
+    grad_query_ref, grad_img_ref, mine_ref, send_ref, grad_kv_ref, acc_ref, *, short
 ):
     cap = pl.program_id(0)
     valid = valid_ref[cap]
     width = query_ref.shape[2]
     slots = kv_ref.shape[1]
+    batch = img_ref.shape[0]
+    place = cap % batch
+
+    @pl.when(cap == 0)
+    def _():
+        acc_ref[...] = jnp.zeros_like(acc_ref)
 
     def work(count):
         mask = same_head()
@@ -417,19 +427,19 @@
             grad_scores = (probs * (grad_probs - delta_ref[0, group : group + 1])).astype(BF16)
             back = gather_heads(dot_tn(grad_scores, key)) * SCALE
             grad_query_ref[0, :, lo : lo + LANES] = back.astype(BF16)
-            grad_kv_ref[0, :count, lo : lo + LANES] = dot(grad_scores, query).astype(BF16)
-            grad_kv_ref[0, :count, width + lo : width + lo + LANES] = dot(
+            grad_kv_ref[place, :count, lo : lo + LANES] = dot(grad_scores, query).astype(BF16)
+            grad_kv_ref[place, :count, width + lo : width + lo + LANES] = dot(
                 probs.astype(BF16), grad
             ).astype(BF16)
-        grad_img_ref[0, :count] = dot_nt(grad_kv_ref[0, :count], kv_mat[...]).astype(BF16)
+        grad_img_ref[0, :count] = dot_nt(grad_kv_ref[place, :count], kv_mat[...]).astype(BF16)
         if count < slots:
-            grad_kv_ref[0, count:] = jnp.zeros((slots - count, 2 * width), BF16)
+            grad_kv_ref[place, count:] = jnp.zeros((slots - count, 2 * width), BF16)
             grad_img_ref[0, count:] = jnp.zeros((slots - count, width), BF16)
 
     @pl.when(valid <= 0)
     def _():
         grad_query_ref[...] = jnp.zeros_like(grad_query_ref)
-        grad_kv_ref[...] = jnp.zeros_like(grad_kv_ref)
+        grad_kv_ref[place] = jnp.zeros((slots, 2 * width), BF16)
         grad_img_ref[...] = jnp.zeros_like(grad_img_ref)
 
     if short < slots:
@@ -438,117 +448,274 @@
     else:
         pl.when(valid > 0)(lambda: work(slots))
 
-
-def cross_back(valid, kv, queries, grads, lse, delta, kv_mat, short):
+    @pl.when(place == batch - 1)
+    def _():
+        left = img_ref[...].reshape(batch * slots, width)
+        right = grad_kv_ref[...].reshape(batch * slots, 2 * width)
+        acc_ref[...] += dot_tn(left, right)
+
+    @pl.when(cap == pl.num_programs(0) - 1)
+    def _():
+        side = side_ref[0]
+        own = pl.ds(pl.multiple_of(side * width, width), width)
+        other = pl.ds(pl.multiple_of((1 - side) * width, width), width)
+        mine_ref[...] = acc_ref[:, own].astype(BF16)
+        send_ref[...] = acc_ref[:, other].astype(BF16)
+
+
+def cross_back(valid, side, kv, queries, grads, lse, delta, kv_mat, images, short):
     caps, slots, double = kv.shape
     width = double // 2
     length = queries.shape[1]
+    batch = 4 if caps % 4 == 0 else 1
     block = lambda *shape: pl.BlockSpec((1,) + shape, lambda i, *_: (i, 0, 0))
     sds = jax.ShapeDtypeStruct
     return pl.pallas_call(
         functools.partial(cross_back_body, short=short),
         grid_spec=pltpu.PrefetchScalarGridSpec(
-            num_scalar_prefetch=1,
+            num_scalar_prefetch=2,
             grid=(caps,),
             in_specs=[
                 block(slots, double), block(length, width), block(length, width),
                 block(GROUPS, LANES), block(GROUPS, LANES), whole(kv_mat.shape),
+                pl.BlockSpec((batch, slots, width), lambda i, *_: (i // batch, 0, 0)),
             ],
-            out_specs=[block(length, width), block(slots, double), block(slots, width)],
+            out_specs=[
+                block(length, width), block(slots, width), whole((width, width)), whole((width, width)),
+            ],
+            scratch_shapes=[
+                pltpu.VMEM((batch, slots, double), BF16), pltpu.VMEM((width, double), F32),
+            ],
         ),
         out_shape=[
-            sds((caps, length, width), BF16), sds((caps, slots, double), BF16),
-            sds((caps, slots, width), BF16),
+            sds((caps, length, width), BF16), sds((caps, slots, width), BF16),
+            sds((width, width), BF16), sds((width, width), BF16),
         ],
         compiler_params=pltpu.CompilerParams(vmem_limit_bytes=VMEM_LIMIT),
         name="cross_back",
-    )(valid, kv, queries, grads, lse, delta, kv_mat)
-
-
-def image_weight_body(side_ref, img_ref, grad_ref, mine_ref, send_ref, acc_ref):
-    step = pl.program_id(0)
-
-    @pl.when(step == 0)
-    def _():
-        acc_ref[...] = jnp.zeros_like(acc_ref)
-
-    acc_ref[...] += dot_tn(img_ref[...], grad_ref[...])
-
-    @pl.when(step == pl.num_programs(0) - 1)
-    def _():
-        half = acc_ref.shape[1] // 2
-        side = side_ref[0]
-
-        @pl.when(side == 0)
-        def _():
-            mine_ref[...] = acc_ref[:, :half].astype(BF16)
-            send_ref[...] = acc_ref[:, half:].astype(BF16)
-
-        @pl.when(side == 1)
-        def _():
-            mine_ref[...] = acc_ref[:, half:].astype(BF16)
-            send_ref[...] = acc_ref[:, :half].astype(BF16)
-
-
-def image_weight(side, images, grads):
-    rows, width = images.shape
-    double = grads.shape[1]
-    tile = 512 if rows % 512 == 0 else rows // 4
-    sds = jax.ShapeDtypeStruct
-    return pl.pallas_call(
-        image_weight_body,
-        grid_spec=pltpu.PrefetchScalarGridSpec(
-            num_scalar_prefetch=1,
-            grid=(rows // tile,),
-            in_specs=[
-                pl.BlockSpec((tile, width), lambda i, *_: (i, 0)),
-                pl.BlockSpec((tile, double), lambda i, *_: (i, 0)),
-            ],
-            out_specs=[whole((width, double // 2)), whole((width, double // 2))],
-            scratch_shapes=[pltpu.VMEM((width, double), F32)],
-        ),
-        out_shape=[sds((width, double // 2), BF16)] * 2,
-        compiler_params=pltpu.CompilerParams(vmem_limit_bytes=VMEM_LIMIT),
-        name="image_weight",
-    )(side, images, grads)
-
-
-def token_end_body(
-    side_ref, back_one, back_two, hidden_ref, grad_two_ref, att_ref, qkv_ref, tok_ref,
-    gain_one, shift_one, qkv_mat, out_mat, gain_two, shift_two, query_mat,
-    grad_tok_ref, qkv_mine, qkv_send, out_mine, out_send, query_mine, query_send, gains_ref,
-    grad_qkv_ref, acc_qkv, acc_out, acc_query, *, length
+    )(valid, side, kv, queries, grads, lse, delta, kv_mat, images)
+
+
+def add_low(first, second):
+    return (first.astype(F32) + second.astype(F32)).astype(BF16)
+
+
+class Piece:
+    def __init__(self, sums, source, out, col, width, bits, order, recvs, mine=None, send=None, kv_recv=None):
+        self.sums, self.out, self.col, self.width = sums, out, col, width
+        self.bits, self.order, self.recvs = list(bits), list(order), recvs
+        self.mine, self.send, self.kv_recv = mine, send, kv_recv
+        self.now, self.holds, self.pending = 0, source, None
+
+    def columns(self, ref):
+        return (slice(None), pl.ds(self.col, self.width) if ref.shape[-1] != self.width else slice(None))
+
+    def start_kv(self):
+        whole_lead = (slice(None),) * len(self.bits)
+        self.pending = self.sums.copy(
+            self.send.at[whole_lead + self.columns(self.send)], self.kv_recv, {"kv": 1 - self.sums.side}
+        )
+        self.pending.start()
+
+    def start(self):
+        bit = self.order[self.now]
+        lead = tuple(1 - self.sums.own(bit) if b == bit else slice(None) for b in self.bits)
+        self.pending = self.sums.copy(
+            self.holds.at[lead + self.columns(self.holds)], self.recvs[self.now], self.sums.partner(bit)
+        )
+        self.pending.start()
+
+    def add(self, kept, arrived, cols, left, fixed):
+        def one(i, carry):
+            inner = {b: (i // (1 << (len(left) - 1 - d))) % 2 for d, b in enumerate(left)}
+            lead = tuple(inner[b] if b in inner else fixed[b] for b in self.bits)
+            into = tuple(inner[b] for b in left)
+            arrived[into] = add_low(kept[lead + cols], arrived[into])
+            return carry
+
+        lax.fori_loop(0, 1 << len(left), one, 0)
+
+    def advance(self):
+        if self.pending is None:
+            return True
+        self.pending.wait()
+        self.pending = None
+        if self.holds is None:
+            self.add(self.mine, self.kv_recv, self.columns(self.mine), self.bits, {})
+            self.holds = self.kv_recv
+            self.start()
+            return False
+        bit = self.order[self.now]
+        arrived, cols = self.recvs[self.now], self.columns(self.holds)
+        left = [b for b in self.bits if b != bit]
+        if not left:
+            total = self.holds[(self.sums.own(bit),) + cols].astype(F32) + arrived[...].astype(F32)
+            self.out[:, self.col : self.col + self.width] = total
+            return True
+        self.add(self.holds, arrived, cols, left, {bit: self.sums.own(bit)})
+        self.bits, self.holds, self.now = left, arrived, self.now + 1
+        self.start()
+        return False
+
+
+class Sums:
+    def __init__(self, send_sem, recv_sem):
+        self.send_sem, self.recv_sem, self.count = send_sem, recv_sem, 0
+        self.me, self.side = lax.axis_index("dp"), lax.axis_index("kv")
+
+    def own(self, bit):
+        return (self.me // (1 << bit)) % 2
+
+    def partner(self, bit):
+        return {"dp": self.me + (1 - 2 * self.own(bit)) * (1 << bit)}
+
+    def copy(self, src, dst, device):
+        index = self.count
+        self.count += 1
+        return pltpu.make_async_remote_copy(
+            src_ref=src, dst_ref=dst, send_sem=self.send_sem.at[index], recv_sem=self.recv_sem.at[index],
+            device_id=device, device_id_type=pl.DeviceIdType.MESH,
+        )
+
+    def greet(self, bits):
+        barrier = pltpu.get_barrier_semaphore()
+        for device in [{"kv": 1 - self.side}] + [self.partner(bit) for bit in bits]:
+            pl.semaphore_signal(barrier, inc=1, device_id=device, device_id_type=pl.DeviceIdType.MESH)
+        pl.semaphore_wait(barrier, 1 + len(bits))
+
+
+def turned(bits, by):
+    first = bits[:-1]
+    by %= len(first)
+    return first[by:] + first[:by] + bits[-1:]
+
+
+def end_body(
+    back_hbm, hidden_hbm, grad_two_hbm, att_hbm, qkv_hbm, tok_hbm, qkv_mat_hbm, out_mat_hbm, query_mat_hbm,
+    gain_one, shift_one, gain_two, shift_two, gain_three, shift_three,
+    up_ref, down_ref, cross_ref, kv_mine, kv_send,
+    grad_tok, up_out, down_out, cross_out, qkv_out, out_out, query_out, kv_out, gains_out,
+    *scratch, plan, bits, length, tile
 ):
-    step = pl.program_id(0)
-
-    @pl.when(step == 0)
-    def _():
-        acc_qkv[...] = jnp.zeros_like(acc_qkv)
-        acc_out[...] = jnp.zeros_like(acc_out)
-        acc_query[...] = jnp.zeros_like(acc_query)
-        gains_ref[...] = jnp.zeros_like(gains_ref)
-
-    back = (back_one[...].astype(F32) + back_two[...].astype(F32)).astype(BF16)
-    unit, inverse = normalize(hidden_ref[...])
-    normed = (unit * gain_two[...] + shift_two[...]).astype(BF16)
-    acc_query[...] += dot_tn(normed, back)
-    grad = dot_nt(back, query_mat[...])
-    gains_ref[2:3] += jnp.sum(grad * unit, axis=0, keepdims=True)
-    gains_ref[3:4] += jnp.sum(grad, axis=0, keepdims=True)
-    grad_one = grad_two_ref[...] + norm_back(grad, gain_two[...], unit, inverse)
-    low = grad_one.astype(BF16)
-    acc_out[...] += dot_tn(att_ref[...], low)
-    grad_att = dot_nt(low, out_mat[...]).astype(BF16)
-    rows, width = grad_att.shape
+    scratch = list(scratch)
+    (
+        send_sem, recv_sem, load_sem, back_one, back_two, hidden, grad_two, att, qkv, tok, qkv_mat,
+        out_mat, query_mat, back_sum, normed, low, grad_att, grad_qkv, acc, gains_all, gain_kv,
+        gain_buf, gain_recv, qkv_mine, qkv_send, out_mine, out_send, query_mine, query_send,
+    ) = scratch[:29]
+    rest = scratch[29:]
+    sums = Sums(send_sem, recv_sem)
+    side = sums.side
+    captions = back_one.shape[0]
+    rows, width = hidden.shape
+    half = width // 2
+    named = dict(
+        up=(up_ref, None, None, up_out), down=(down_ref, None, None, down_out),
+        cross=(cross_ref, None, None, cross_out), qkv=(None, qkv_mine, qkv_send, qkv_out),
+        out=(None, out_mine, out_send, out_out), query=(None, query_mine, query_send, query_out),
+        kv=(None, kv_mine, kv_send, kv_out),
+    )
+    pieces = {}
+    for name, col, cols, axes, order, kv in plan:
+        source, mine, send, out = named[name]
+        kv_recv = rest.pop(0) if kv else None
+        recvs = [rest.pop(0) for _ in order]
+        pieces.setdefault(name, []).append(
+            Piece(sums, source, out, col, cols, axes, order, recvs, mine, send, kv_recv)
+        )
+    early = pieces["up"] + pieces["down"] + pieces["cross"]
+    image = pieces["kv"]
+    middle = pieces["query"] + pieces["out"]
+    late = pieces["qkv"]
+
+    own_caps = pl.ds(pl.multiple_of(side * captions, captions), captions)
+    other_caps = pl.ds(pl.multiple_of((1 - side) * captions, captions), captions)
+    pairs = [
+        (back_hbm.at[own_caps], back_one), (hidden_hbm, hidden), (query_mat_hbm, query_mat),
+        (grad_two_hbm, grad_two), (out_mat_hbm, out_mat), (att_hbm, att), (qkv_hbm, qkv),
+        (tok_hbm, tok), (qkv_mat_hbm, qkv_mat),
+    ]
+    loads = [pltpu.make_async_copy(src, dst, load_sem.at[i]) for i, (src, dst) in enumerate(pairs)]
+    for load in loads:
+        load.start()
+    sums.greet(bits)
+    swap = sums.copy(back_hbm.at[other_caps], back_two, {"kv": 1 - side})
+    swap.start()
+    for piece in image:
+        piece.start_kv()
+    for piece in early:
+        piece.start()
+    gains_all[...] = jnp.zeros_like(gains_all)
+    gains_all[4:5] = gain_three[...]
+    gains_all[5:6] = shift_three[...]
+    for load in loads[:5]:
+        load.wait()
+    swap.wait()
+
+    def rows_at(index):
+        return pl.ds(pl.multiple_of(index * tile, tile), tile)
+
+    def query_back(index, carry):
+        span = rows_at(index)
+        caps = pl.ds(index * (tile // length), tile // length)
+        back = add_low(back_one[caps], back_two[caps]).reshape(tile, width)
+        back_sum[span, :] = back
+        unit, inverse = normalize(hidden[span, :])
+        normed[span, :] = (unit * as_row(gain_two) + as_row(shift_two)).astype(BF16)
+        grad = dot_nt(back, query_mat[...])
+        gains_all[2:3] += jnp.sum(grad * unit, axis=0, keepdims=True)
+        gains_all[3:4] += jnp.sum(grad, axis=0, keepdims=True)
+        grad_one = grad_two[span, :] + norm_back(grad, as_row(gain_two), unit, inverse)
+        grad_two[span, :] = grad_one
+        low[span, :] = grad_one.astype(BF16)
+        grad_att[span, :] = dot_nt(grad_one.astype(BF16), out_mat[...]).astype(BF16)
+        return carry
+
+    lax.fori_loop(0, rows // tile, query_back, 0)
+    for piece in image:
+        piece.advance()
+
+    def weight(left, right, target, which):
+        cols = target.shape[-1]
+        block = target.shape[-2]
+        start = pl.multiple_of(which * cols, 128)
+        acc[:, :cols] = dot_tn(left[...], right[:, pl.ds(start, cols)])
+
+        def one(i, carry):
+            lead = tuple((i // (1 << (len(bits) - 1 - d))) % 2 for d in range(len(bits)))
+            span = pl.ds(i * block, block) if isinstance(i, int) else pl.ds(pl.multiple_of(i * block, 8), block)
+            target[lead] = acc[span, :cols].astype(BF16)
+            return carry
+
+        if block % 8 == 0:
+            lax.fori_loop(0, 1 << len(bits), one, 0)
+        else:
+            for i in range(1 << len(bits)):
+                one(i, 0)
+
+    def weights(left, right, mine, send, group):
+        weight(left, right, send, 1 - side)
+        for piece in group:
+            piece.start_kv()
+        weight(left, right, mine, side)
+
+    weights(normed, back_sum, query_mine, query_send, pieces["query"])
+    loads[5].wait()
+    loads[6].wait()
+    weights(att, low, out_mine, out_send, pieces["out"])
+    for piece in middle:
+        piece.advance()
+
     mask = same_head()
     causal = causal_mask(length)
-    for cap in range(rows // length):
-        span = slice(cap * length, (cap + 1) * length)
+
+    def attend(cap, carry):
+        span = pl.ds(pl.multiple_of(cap * length, length), length)
         for group in range(GROUPS):
             lo = group * LANES
-            query = spread(qkv_ref[span, lo : lo + LANES] * SCALE, mask)
-            key = qkv_ref[span, width + lo : width + lo + LANES]
-            value = qkv_ref[span, 2 * width + lo : 2 * width + lo + LANES]
+            query = spread(qkv[span, lo : lo + LANES] * SCALE, mask)
+            key = qkv[span, width + lo : width + lo + LANES]
+            value = qkv[span, 2 * width + lo : 2 * width + lo + LANES]
             cot = spread(grad_att[span, lo : lo + LANES], mask)
             scores = jnp.where(causal, dot_nt(key, query), NEG)
             exponent = jnp.exp(scores - jnp.max(scores, axis=0, keepdims=True))
@@ -557,96 +724,165 @@
             mean = jnp.sum(probs * grad_probs, axis=0, keepdims=True)
             grad_scores = (probs * (grad_probs - mean)).astype(BF16)
             grad_q = gather_heads(dot_tn(grad_scores, key)) * SCALE
-            grad_qkv_ref[span, lo : lo + LANES] = grad_q.astype(BF16)
-            grad_qkv_ref[span, width + lo : width + lo + LANES] = dot(grad_scores, query).astype(BF16)
-            grad_qkv_ref[span, 2 * width + lo : 2 * width + lo + LANES] = dot(
+            grad_qkv[span, lo : lo + LANES] = grad_q.astype(BF16)
+            grad_qkv[span, width + lo : width + lo + LANES] = dot(grad_scores, query).astype(BF16)
+            grad_qkv[span, 2 * width + lo : 2 * width + lo + LANES] = dot(
                 probs.astype(BF16), cot
             ).astype(BF16)
-    unit, inverse = normalize(tok_ref[...].astype(F32))
-    normed = (unit * gain_one[...] + shift_one[...]).astype(BF16)
-    acc_qkv[...] += dot_tn(normed, grad_qkv_ref[...])
-    grad = dot_nt(grad_qkv_ref[...], qkv_mat[...])
-    gains_ref[0:1] += jnp.sum(grad * unit, axis=0, keepdims=True)
-    gains_ref[1:2] += jnp.sum(grad, axis=0, keepdims=True)
-    grad_tok_ref[...] = (grad_one + norm_back(grad, gain_one[...], unit, inverse)).astype(BF16)
-
-    @pl.when(step == pl.num_programs(0) - 1)
-    def _():
-        for acc, mine, send in (
-            (acc_qkv, qkv_mine, qkv_send),
-            (acc_out, out_mine, out_send),
-            (acc_query, query_mine, query_send),
-        ):
-            half = acc.shape[1] // 2
-
-            @pl.when(side_ref[0] == 0)
-            def _():
-                mine[...] = acc[:, :half].astype(BF16)
-                send[...] = acc[:, half:].astype(BF16)
-
-            @pl.when(side_ref[0] == 1)
-            def _():
-                mine[...] = acc[:, half:].astype(BF16)
-                send[...] = acc[:, :half].astype(BF16)
-
-
-def token_end(
-    side, back_one, back_two, hidden, grad_two, att, qkv, tokens,
-    gain_one, shift_one, qkv_mat, out_mat, gain_two, shift_two, query_mat, length
+        return carry
+
+    lax.fori_loop(0, captions // 2, attend, 0)
+    lax.fori_loop(captions // 2, captions, attend, 0)
+    for piece in early:
+        piece.advance()
+    loads[7].wait()
+    loads[8].wait()
+
+    def token_norm(index, carry):
+        span = rows_at(index)
+        unit, _ = normalize(tok[span, :].astype(F32))
+        normed[span, :] = (unit * as_row(gain_one) + as_row(shift_one)).astype(BF16)
+        return carry
+
+    lax.fori_loop(0, rows // tile, token_norm, 0)
+    weights(normed, grad_qkv, qkv_mine, qkv_send, late)
+    for piece in late + image:
+        piece.advance()
+
+    def token_back(index, carry):
+        span = rows_at(index)
+        unit, inverse = normalize(tok[span, :].astype(F32))
+        grad = dot_nt(grad_qkv[span, :], qkv_mat[...])
+        gains_all[0:1] += jnp.sum(grad * unit, axis=0, keepdims=True)
+        gains_all[1:2] += jnp.sum(grad, axis=0, keepdims=True)
+        back = grad_two[span, :] + norm_back(grad, as_row(gain_one), unit, inverse)
+        grad_tok[span, :] = back.astype(BF16)
+        return carry
+
+    lax.fori_loop(0, rows // tile, token_back, 0)
+    own_cols = pl.ds(pl.multiple_of(side * half, 128), half)
+    other_cols = pl.ds(pl.multiple_of((1 - side) * half, 128), half)
+    gain_copy = sums.copy(gains_all.at[:, other_cols], gain_kv, {"kv": 1 - side})
+    gain_copy.start()
+    stage = -1
+    everything = early + image + middle + late
+    while stage < len(bits) or not all(piece.pending is None for piece in everything):
+        if stage < len(bits):
+            gain_copy.wait()
+            if stage < 0:
+                gain_buf[0] = gains_all[:, own_cols] + gain_kv[...]
+            else:
+                gain_buf[stage + 1] = gain_buf[stage] + gain_recv[stage]
+            stage += 1
+            if stage < len(bits):
+                gain_copy = sums.copy(gain_buf.at[stage], gain_recv.at[stage], sums.partner(bits[stage]))
+                gain_copy.start()
+            else:
+                gains_out[...] = gain_buf[stage]
+        for piece in everything:
+            piece.advance()
+
+
+def end(
+    back, hidden, grad_two, att, qkv, tokens, qkv_mat, out_mat, query_mat, gain_one, shift_one,
+    gain_two, shift_two, gain_three, shift_three, early, kv_mine, kv_send, length, size
 ):
-    rows, width = tokens.shape
+    bits = list(range(size.bit_length() - 1))
+    axes = bits[::-1]
+    rows, width = hidden.shape
+    captions = rows // length
     tile = min(256, rows)
-    row_block = lambda cols: pl.BlockSpec((tile, cols), lambda i, *_: (i, 0))
+    block = width // size
+    lead = (2,) * len(bits)
+    up, down, cross = early
+    cut_up = up.shape[-1] // 384 * 256
+    cut_down = down.shape[-1] // 384 * 256
+    third = width // 3
+    early_order = lambda by, array: [b for b in turned(bits, by) if b in bits[len(bits) + 2 - array.ndim :]]
+    early_axes = lambda array: axes[: array.ndim - 2]
+    plan = []
+    for name, array, cuts in (
+        ("up", up, ((0, cut_up, 0), (cut_up, up.shape[-1] - cut_up, 2))),
+        ("down", down, ((0, cut_down, 1), (cut_down, down.shape[-1] - cut_down, 2))),
+        ("cross", cross, ((0, cross.shape[-1], 1),)),
+    ):
+        for col, cols, by in cuts:
+            plan.append((name, col, cols, early_axes(array), early_order(by, array), False))
+    plan.append(("query", 0, width // 2, axes, turned(bits, 0), True))
+    plan.append(("out", 0, width // 2, axes, turned(bits, 1), True))
+    for by in range(3):
+        plan.append(("kv", by * third, third, axes, turned(bits, by), True))
+        plan.append(("qkv", by * (width // 2), width // 2, axes, turned(bits, by), True))
+    heights = dict(up=up.shape[-2], down=down.shape[-2], cross=cross.shape[-2])
+    buffers = []
+    copies = 2 + len(bits)
+    for name, col, cols, piece_axes, order, kv in plan:
+        shape = (heights.get(name, block), cols)
+        for count in range(len(order) if kv else len(order) - 1, -1, -1):
+            buffers.append(pltpu.VMEM((2,) * count + shape, BF16))
+            copies += 1
+    vmem = pl.BlockSpec(memory_space=pltpu.VMEM)
+    hbm = pl.BlockSpec(memory_space=pl.ANY)
     sds = jax.ShapeDtypeStruct
-    halves = [(width, 3 * width // 2)] * 2 + [(width, width // 2)] * 4
+    cut = lambda cols: pltpu.VMEM(lead + (block, cols), BF16)
+    outs = [sds((rows, width), BF16)]
+    outs += [sds(v.shape[-2:], F32) for v in (up, down, cross)]
+    outs += [sds((block, cols), F32) for cols in (3 * width // 2, width // 2, width // 2, width)]
+    outs += [sds((8, width // 2), F32)]
+    low_rows = lambda cols: pltpu.VMEM((rows, cols), BF16)
     return pl.pallas_call(
-        functools.partial(token_end_body, length=length),
-        grid_spec=pltpu.PrefetchScalarGridSpec(
-            num_scalar_prefetch=1,
-            grid=(rows // tile,),
-            in_specs=[
-                row_block(width), row_block(width), row_block(width), row_block(width),
-                row_block(width), row_block(3 * width), row_block(width),
-                whole((1, width)), whole((1, width)), whole(qkv_mat.shape), whole(out_mat.shape),
-                whole((1, width)), whole((1, width)), whole(query_mat.shape),
-            ],
-            out_specs=[row_block(width)] + [whole(s) for s in halves] + [whole((4, width))],
-            scratch_shapes=[
-                pltpu.VMEM((tile, 3 * width), BF16), pltpu.VMEM((width, 3 * width), F32),
-                pltpu.VMEM((width, width), F32), pltpu.VMEM((width, width), F32),
-            ],
+        functools.partial(end_body, plan=plan, bits=bits, length=length, tile=tile),
+        in_specs=[hbm] * 9 + [vmem] * 6 + [vmem] * 4 + [hbm],
+        out_specs=[vmem] * len(outs),
+        out_shape=outs,
+        scratch_shapes=[
+            pltpu.SemaphoreType.DMA((copies,)), pltpu.SemaphoreType.DMA((copies,)),
+            pltpu.SemaphoreType.DMA((9,)),
+            pltpu.VMEM((captions, length, width), BF16), pltpu.VMEM((captions, length, width), BF16),
+            pltpu.VMEM((rows, width), F32), pltpu.VMEM((rows, width), F32), low_rows(width),
+            low_rows(3 * width), low_rows(width), pltpu.VMEM(qkv_mat.shape, BF16),
+            pltpu.VMEM(out_mat.shape, BF16), pltpu.VMEM(query_mat.shape, BF16),
+            low_rows(width), low_rows(width), low_rows(width), low_rows(width), low_rows(3 * width),
+            pltpu.VMEM((width, 3 * width // 2), F32), pltpu.VMEM((8, width), F32),
+            pltpu.VMEM((8, width // 2), F32), pltpu.VMEM((len(bits) + 1, 8, width // 2), F32),
+            pltpu.VMEM((len(bits), 8, width // 2), F32),
+            cut(3 * width // 2), cut(3 * width // 2), cut(width // 2), cut(width // 2),
+            cut(width // 2), cut(width // 2),
+        ] + buffers,
+        compiler_params=pltpu.CompilerParams(
+            vmem_limit_bytes=VMEM_MOST, collective_id=0, has_side_effects=True
         ),
-        out_shape=[sds((rows, width), BF16)] + [sds(s, BF16) for s in halves] + [sds((4, width), F32)],
-        compiler_params=pltpu.CompilerParams(vmem_limit_bytes=VMEM_LIMIT),
-        name="token_end",
+        name="end",
     )(
-        side, back_one, back_two, hidden, grad_two, att, qkv, tokens,
-        gain_one, shift_one, qkv_mat, out_mat, gain_two, shift_two, query_mat,
+        back, hidden, grad_two, att, qkv, tokens, qkv_mat, out_mat, query_mat, gain_one, shift_one,
+        gain_two, shift_two, gain_three, shift_three, up, down, cross, kv_mine, kv_send,
     )
 
 
-def add_low(first, second):
-    return (first.astype(F32) + second.astype(F32)).astype(BF16)
+def hand_over_body(*refs):
+    count = len(refs) // 2
+    for source, target in zip(refs[:count], refs[count:]):
+        target[...] = source[...]
+
+
+def hand_over(*arrays):
+    vmem = pl.BlockSpec(memory_space=pltpu.VMEM)
+    return pl.pallas_call(
+        hand_over_body,
+        in_specs=[vmem] * len(arrays),
+        out_specs=[vmem] * len(arrays),
+        out_shape=[jax.ShapeDtypeStruct(v.shape, v.dtype) for v in arrays],
+        name="hand_over",
+    )(*arrays)
 
 
 def exchange(value, axis, bit, size):
     return lax.ppermute(value, axis, [(i, i ^ bit) for i in range(size)])
 
 
-def reduce_blocks(mine, send, order, me, size):
-    total = add_low(mine, exchange(send, "kv", 1, 2))
+def split_rows(array, size):
     bits = size.bit_length() - 1
-    rows = total.shape[0] // size
-    total = total.reshape((2,) * bits + (rows, total.shape[1]))
-    left = list(range(bits))[::-1]
-    for bit in order:
-        axis = left.index(bit)
-        own = (me >> bit) & 1
-        keep = lax.dynamic_index_in_dim(total, own, axis, False)
-        away = lax.dynamic_index_in_dim(total, 1 - own, axis, False)
-        total = add_low(keep, exchange(away, "dp", 1 << bit, size))
-        left.remove(bit)
-    return total.astype(F32)
+    return array.reshape((2,) * bits + (array.shape[0] // size, array.shape[1]))
 
 
 def body(
@@ -659,7 +895,7 @@
     me = lax.axis_index("dp")
     groups = lax.axis_size("dp")
     side_arr = side.reshape(1)
-    row = lambda v: v.reshape(1, width)
+    row = lambda v: v
     tok = tokens.reshape(captions * length, width)
     cot = cotangent.reshape(captions * length, width)
     short = -(-SHORT // 16) * 16
@@ -694,35 +930,23 @@
         swap(other_part(lse_part)), hidden, cot, cross_out, row(norm3_gain), row(norm3_shift),
         w_up, w_down, length,
     )
-    bits = groups.bit_length() - 1
-    turn = lambda start: [(start + i) % bits for i in range(bits)]
-    w_up_grad = reduce_blocks(up_mine, up_send, turn(0), me, groups)
-    down_grad = reduce_blocks(down_mine, down_send, turn(bits // 2), me, groups)
-    cross_out_grad = reduce_blocks(cross_mine, cross_send, turn(bits // 4), me, groups)
+    early = [
+        split_rows(add_low(mine, exchange(send, "kv", 1, 2)), groups)
+        for mine, send in ((up_mine, up_send), (down_mine, down_send), (cross_mine, cross_send))
+    ]
 
     grads = both(grad_att.reshape(captions, length, width))
-    back, grad_kv, images_grad = cross_back(
-        valid, kv, queries, grads, both(lse), both(delta), cross_kv, short
+    back, images_grad, kv_mine, kv_send = cross_back(
+        valid, side_arr, kv, queries, grads, both(lse), both(delta), cross_kv, images, short
     )
-    kv_mine, kv_send = image_weight(
-        side_arr, images.reshape(caps * slots, width), grad_kv.reshape(caps * slots, 2 * width)
-    )
-    cross_kv_grad = reduce_blocks(kv_mine, kv_send, turn(0), me, groups)
+    cut = lambda v: split_rows(v, groups)
     (
-        tokens_grad, qkv_mine, qkv_send, out_mine, out_send, query_mine, query_send, gains,
-    ) = token_end(
-        side_arr, flat(own_part(back)), flat(swap(other_part(back))), hidden, grad_two, att, qkv,
-        tok, row(norm1_gain), row(norm1_shift), self_qkv, self_out, row(norm2_gain),
-        row(norm2_shift), cross_q, length,
-    )
-    self_qkv_grad = reduce_blocks(qkv_mine, qkv_send, turn(0), me, groups)
-    self_out_grad = reduce_blocks(out_mine, out_send, turn(bits // 2), me, groups)
-    cross_q_grad = reduce_blocks(query_mine, query_send, turn(bits // 4), me, groups)
-    gains = jnp.concatenate([gains, gain3, shift3], axis=0)
-    gains = gains + swap(gains)
-    gains = lax.dynamic_slice_in_dim(gains, side * (width // 2), width // 2, 1)
-    for bit in range(bits):
-        gains = gains + exchange(gains, "dp", 1 << bit, groups)
+        tokens_grad, w_up_grad, down_grad, cross_out_grad, self_qkv_grad, self_out_grad, cross_q_grad,
+        cross_kv_grad, gains,
+    ) = hand_over(*end(
+        back, hidden, grad_two, att, qkv, tok, self_qkv, self_out, cross_q, norm1_gain, norm1_shift,
+        norm2_gain, norm2_shift, gain3, shift3, early, cut(kv_mine), cut(kv_send), length, groups,
+    ))
     return (
         layer_out.reshape(captions, length, width),
         tokens_grad.reshape(captions, length, width),

time: 356 us -> 262 us (0.74); the launches traced: 348 us -> 260 us
  waiting for transfers between devices: 105 us -> 10.2 us
  Pallas kernels: 161 us -> 225 us
  starting transfers between devices: 38.6 us -> 1.89 us
  local copies, waits for them, and re-layouts: 19.7 us -> 5.54 us
  other arithmetic: 22.4 us -> 16.2 us
    ppermute x47 -> x9, waiting for transfers between devices: 105 us -> 10.2 us  [exchange(): return lax.ppermute(value, axis, [(i, i ^ bit) for i in range(size)])]
    pallas_call x2, Pallas kernels: 43.8 us -> 92.4 us  [the longest x1 89.6 us: end(): pl.pallas_call(functools.partial(end_body, plan=plan, bits=bits, length=l...]
    ppermute x47 -> x9, starting transfers between devices: 38.6 us -> 1.89 us  [exchange(): return lax.ppermute(value, axis, [(i, i ^ bit) for i in range(size)])]
    pallas_call x1, Pallas kernels: 40.1 us -> 56.1 us  [cross_back(): pl.pallas_call(functools.partial(cross_back_body, short=short), grid_spec...]
    reshape x6 -> x0, local copies, waits for them, and re-layouts: 6.25 us -> none  [body(): row = lambda v: v.reshape(1, width)]
    convert_element_type x7 -> x0, other arithmetic: 5.59 us -> none  [reduce_blocks(): return total.astype(F32)]
    convert_element_type x28 -> x3, other arithmetic: 8.73 us -> 9.57 us  [add_low(): return (first.astype(F32) + second.astype(F32)).astype(BF16)]
  transfers between devices with their start and end apart: 47 -> 9, of which waited for: 23 -> 3; matrix products, arithmetic and copies ran while one was open for 8% -> 4% of each run, Pallas kernels for 24% -> 22%
where the time goes in v3:
time: 262 us; the launch traced here: 260 us
  Pallas kernels  225 us (86%)
  other arithmetic  16.2 us (6%)
  waiting for transfers between devices  10.2 us (4%)
  local copies, waits for them, and re-layouts  5.54 us (2%)
    pallas_call x1, Pallas kernels, end(): pl.pallas_call(functools.partial(end_body, plan=plan, bits=bits, length=l...  89.6 us
    pallas_call x1, Pallas kernels, cross_back(): pl.pallas_call(functools.partial(cross_back_body, short=short), grid_spec...  56.1 us
    pallas_call x1, Pallas kernels, feed(): pl.pallas_call(functools.partial(feed_body, length=length, tile=tile), gr...  34.2 us
    pallas_call x1, Pallas kernels, cross_start(): pl.pallas_call(functools.partial(cross_start_body, short=short), grid_spe...  30.2 us
    pallas_call x1, Pallas kernels, token_start(): pl.pallas_call(functools.partial(token_start_body, length=length), grid=(...  12.5 us
    ppermute x9, waiting for transfers between devices, exchange(): return lax.ppermute(value, axis, [(i, i ^ bit) for i in range(size)])  10.2 us
    convert_element_type x3, other arithmetic, add_low(): return (first.astype(F32) + second.astype(F32)).astype(BF16)  9.57 us
  transfers between devices with their start and end apart: 9, of which 3 were waited for; matrix products, arithmetic and copies ran while one was open for 4% of the time, Pallas kernels for 22%

profile of v3, /device:TPU:2, one launch (start us, length us, event | category | flops | bytes accessed | tf_op | source)
XLA Modules:
  0.0 260.1 jit_solution(1678124320195457430)
XLA Ops:
  0.7 12.5 %token_start.1 = (bf16[512,2304]{1,0:T(8,128)(2,1)}, bf16[512,768]{1,0:T(8,128)(2,1)}, f32[512,768]{1,0:T(8,128)}, bf16[512,768]{1,0:T(8,128)(2,1)}) custom-call(bf16[512,768]{1,0:T(8,128)(2,1)} %bitcast.16, f32[768]{0:T(1024)} %gain_one.3, f32[768]{0:T(1024)} %shift_one.3, bf16[768,2304]{1,0:T(8,128)(2,1)} %qkv_mat_hbm.1, bf16[768,768]{1,0:T(8,128)(2,1)} %out_mat_hbm.1, ...), custom_call_target="tpu_custom_call" | custom-call | tf_op jit(solution)/shard_map/token_start/pallas_call | solution.py:144
  13.2 0.5 subtract_clamp_fusion.valid_ref
  13.7 2.0 collective-permute-done
  15.7 1.2 broadcast_select_fusion.3
  16.9 1.3 pad_maximum_fusion.query_ref
  18.2 30.2 %cross_start.1 = (bf16[16,288,1536]{2,1,0:T(8,128)(2,1)}, bf16[16,64,768]{2,1,0:T(8,128)(2,1)}, f32[16,3,256]{2,1,0:T(4,128)}) custom-call(s32[16]{0:T(128)} %subtract_clamp_fusion.valid_ref, bf16[16,288,768]{2,1,0:T(8,128)(2,1)} %img_ref.3, bf16[768,1536]{1,0:T(8,128)(2,1)} %kv_mat.3, bf16[16,64,768]{2,1,0:T(8,128)(2,1)} %pad_maximum_fusion.query_ref), custom_call_target="tpu_custom_call" | custom-call | tf_op jit(solution)/shard_map/cross_start/pallas_call | solution.py:202
  48.4 2.5 constant_dynamic-slice_fusion.1
  50.9 0.6 constant_dynamic-slice_fusion
  51.5 0.5 collective-permute-start.2
  52.0 1.2 collective-permute-done.2.lse_two
  53.2 0.6 copy-done.5
  53.8 0.3 copy-done.3
  54.1 34.2 %feed.1 = (bf16[512,768]{1,0:T(8,128)(2,1)}, f32[512,768]{1,0:T(8,128)}, bf16[512,768]{1,0:T(8,128)(2,1)}, f32[8,3,256]{2,1,0:T(4,128)}, f32[8,3,256]{2,1,0:T(4,...) custom-call(s32[1]{0:T(128)} %bitcast.side_ref, ...), custom_call_target="tpu_custom_call" | custom-call | tf_op jit(solution)/shard_map/feed/pallas_call | solution.py:360
  88.3 0.2 collective-permute-start.7
  88.5 0.4 collective-permute-start.6
  88.9 0.1 collective-permute-start.5
  89.0 0.4 collective-permute-start.8
  89.4 0.1 collective-permute-start.4
  89.5 7.1 %collective-permute-done.5 = f32[8,3,256]{2,1,0:T(4,128)S(1)} collective-permute-done((f32[8,3,256]{2,1,0:T(4,128)}, f32[8,3,256]{2,1,0:T(4,128)S(1)}, u32[]{:S(2)}, u32[]{:S(2)}) %collective-permute-start.5) | collective-permute-done | bytes 24608 | tf_op jit(solution)/shard_map/ppermute | solution.py:880
  96.6 0.1 collective-permute-start.3
  96.8 0.8 broadcast_select_fusion.5
  97.5 0.8 broadcast_select_fusion.7
  98.3 0.7 pad_maximum_fusion.2
  99.0 2.0 add_convert_fusion.2
  101.1 0.1 broadcast_select_fusion.1
  101.2 1.3 pad_maximum_fusion.1.grad_ref
  102.5 56.1 %cross_back.1 = (bf16[16,64,768]{2,1,0:T(8,128)(2,1)}, bf16[16,288,768]{2,1,0:T(8,128)(2,1)}, bf16[768,768]{1,0:T(8,128)(2,1)}, bf16[768,768]{1,0:T(8,128)(2,1)}) custom-call(s32[16]{0:T(128)} %subtract_clamp_fusion.valid_ref, s32[1]{0:T(128)} %bitcast.side_ref, bf16[16,288,1536]{2,1,0:T(8,128)(2,1)} %get-tuple-element.63.kv_ref, ...), custom_call_target="tpu_custom_call" | custom-call | tf_op jit(solution)/shard_map/cross_back/pallas_call | solution.py:473
  158.6 3.8 %add_convert_fusion = bf16[3072,384]{1,0:T(8,128)(2,1)} fusion(bf16[3072,384]{1,0:T(8,128)(2,1)} %collective-permute-done.7, bf16[3072,384]{1,0:T(8,128)(2,1)S(1)} %copy-done.1), kind=kLoop, calls=%fused_computation | loop fusion | flops 4718592 | bytes 7077888 | tf_op jit(solution)/shard_map/convert_element_type | solution.py:500
  162.5 3.7 %add_convert_fusion.1 = bf16[768,1536]{1,0:T(8,128)(2,1)} fusion(bf16[768,1536]{1,0:T(8,128)(2,1)} %collective-permute-done.6, bf16[768,1536]{1,0:T(8,128)(2,1)S(1)} %copy-done), kind=kLoop, calls=%fused_computation.1 | loop fusion | flops 4718592 | bytes 7077888 | tf_op jit(solution)/shard_map/convert_element_type | solution.py:500
  166.2 89.6 %end.1 = (bf16[512,768]{1,0:T(8,128)(2,1)}, f32[48,1536]{1,0:T(8,128)}, f32[192,384]{1,0:T(8,128)}, f32[48,384]{1,0:T(8,128)}, f32[48,1152]{1,0:T(8,128)}, /*ind...) custom-call(bf16[16,64,768]{2,1,0:T(8,128)(2,1)} %get-tuple-element.67.back_hbm, ...), custom_call_target="tpu_custom_call" | custom-call | tf_op jit(solution)/shard_map/end/pallas_call | solution.py:833
  255.7 2.8 %hand_over.1 = (bf16[512,768]{1,0:T(8,128)(2,1)}, f32[48,1536]{1,0:T(8,128)}, f32[192,384]{1,0:T(8,128)}, f32[48,384]{1,0:T(8,128)}, f32[48,1152]{1,0:T(8,128)},...) custom-call(bf16[512,768]{1,0:T(8,128)(2,1)} %get-tuple-element.81.refs_0_, ...), custom_call_target="tpu_custom_call" | custom-call | tf_op jit(solution)/shard_map/hand_over/pallas_call | solution.py:870
  258.6 1.6 slice_reduce_fusion
  (20 shorter events, 0.0 us)
Async XLA Ops:
  0.6 12.6 %copy-start.6 = (s32[16]{0:T(128)S(1)}, s32[16]{0:T(128)}, u32[]{:S(2)}) copy-start(s32[16]{0:T(128)} %param.19) | copy-start | bytes 196
  13.2 2.5 collective-permute-start
  48.4 2.5 copy-start.4
  50.9 2.3 collective-permute-start.1
  51.5 1.7 collective-permute-start.2
  53.2 0.6 copy-start.5
  53.2 0.9 copy-start.3
  88.3 12.8 %copy-start.2 = (bf16[512,768]{1,0:T(8,128)(2,1)S(1)}, bf16[512,768]{1,0:T(8,128)(2,1)}, u32[]{:S(2)}) copy-start(bf16[512,768]{1,0:T(8,128)(2,1)} %get-tuple-element.64) | copy-start | bytes 2359300
  88.3 70.3 %collective-permute-start.7 = (bf16[3072,384]{1,0:T(8,128)(2,1)}, bf16[3072,384]{1,0:T(8,128)(2,1)}, u32[]{:S(2)}, u32[]{:S(2)}) collective-permute-start(bf16[3072,384]{1,0:T(8,128)(2,1)} %get-tuple-element.76), channel_id=1, source_target_pairs={{0,1},{1,0},{2,3},{3,2},{4,5},{5,4},{6,7},{7,6},{8,9},{9,8},{10,11... | collective-permute-start | bytes 7077896 | tf_op jit(solution)/shard_map/ppermute | solution.py:880
  88.5 73.9 %collective-permute-start.6 = (bf16[768,1536]{1,0:T(8,128)(2,1)}, bf16[768,1536]{1,0:T(8,128)(2,1)}, u32[]{:S(2)}, u32[]{:S(2)}) collective-permute-start(bf16[768,1536]{1,0:T(8,128)(2,1)} %get-tuple-element.74), channel_id=1, source_target_pairs={{0,1},{1,0},{2,3},{3,2},{4,5},{5,4},{6,7},{7,6},{8,9},{9,8},{10,11... | collective-permute-start | bytes 7077896 | tf_op jit(solution)/shard_map/ppermute | solution.py:880
  88.9 7.7 %collective-permute-start.5 = (f32[8,3,256]{2,1,0:T(4,128)}, f32[8,3,256]{2,1,0:T(4,128)S(1)}, u32[]{:S(2)}, u32[]{:S(2)}) collective-permute-start(f32[8,3,256]{2,1,0:T(4,128)} %get-tuple-element.66), channel_id=1, source_target_pairs={{0,1},{1,0},{2,3},{3,2},{4,5},{5,4},{6,7},{7,6},{8,9},{9,8},{10,11... | collective-permute-start | bytes 73736 | tf_op jit(solution)/shard_map/ppermute | solution.py:880
  89.0 10.0 %collective-permute-start.8 = (bf16[768,384]{1,0:T(8,128)(2,1)}, bf16[768,384]{1,0:T(8,128)(2,1)S(1)}, u32[]{:S(2)}, u32[]{:S(2)}) collective-permute-start(bf16[768,384]{1,0:T(8,128)(2,1)} %get-tuple-element.78), channel_id=1, source_target_pairs={{0,1},{1,0},{2,3},{3,2},{4,5},{5,4},{6,7},{7,6},{8,9},{9,8},{10,11... | collective-permute-start | bytes 1769480 | tf_op jit(solution)/shard_map/ppermute | solution.py:880
  89.4 8.2 %collective-permute-start.4 = (f32[8,3,256]{2,1,0:T(4,128)}, f32[8,3,256]{2,1,0:T(4,128)S(1)}, u32[]{:S(2)}, u32[]{:S(2)}) collective-permute-start(f32[8,3,256]{2,1,0:T(4,128)} %get-tuple-element.65), channel_id=1, source_target_pairs={{0,1},{1,0},{2,3},{3,2},{4,5},{5,4},{6,7},{7,6},{8,9},{9,8},{10,11... | collective-permute-start | bytes 73736 | tf_op jit(solution)/shard_map/ppermute | solution.py:880
  96.6 4.4 %collective-permute-start.3 = (bf16[8,64,768]{2,1,0:T(8,128)(2,1)}, bf16[8,64,768]{2,1,0:T(8,128)(2,1)S(1)}, u32[]{:S(2)}, u32[]{:S(2)}) collective-permute-start(bf16[8,64,768]{2,1,0:T(8,128)(2,1)} %bitcast.22), channel_id=1, source_target_pairs={{0,1},{1,0},{2,3},{3,2},{4,5},{5,4},{6,7},{7,6},{8,9},{9,8},{10,11... | collective-permute-start | bytes 2359304 | tf_op jit(solution)/shard_map/ppermute | solution.py:880
  102.5 56.1 %copy-start.1 = (bf16[3072,384]{1,0:T(8,128)(2,1)S(1)}, bf16[3072,384]{1,0:T(8,128)(2,1)}, u32[]{:S(2)}) copy-start(bf16[3072,384]{1,0:T(8,128)(2,1)} %get-tuple-element.75) | copy-start | bytes 7077892
  158.6 3.9 %copy-start = (bf16[768,1536]{1,0:T(8,128)(2,1)S(1)}, bf16[768,1536]{1,0:T(8,128)(2,1)}, u32[]{:S(2)}) copy-start(bf16[768,1536]{1,0:T(8,128)(2,1)} %get-tuple-element.73) | copy-start | bytes 7077892

commit v4 on v3

--- a/solution.py
+++ b/solution.py
@@ -218,23 +218,72 @@
 
 
 def feed_body(
-    side_ref, att_one, lse_one, att_two, lse_two, hidden_ref, cot_ref, cross_mat, gain_ref,
-    shift_ref, up_mat, down_mat,
-    out_ref, grad_two_ref, grad_att_ref, lse_ref, delta_ref, up_mine, up_send, down_mine,
-    down_send, cross_mine, cross_send, gain_grad, shift_grad,
-    att_full, att_low, hidden_two, normed_ref, acc_out, acc_grad, *, length, tile
+    part_hbm, lse_hbm, hidden_ref, cot_ref, cross_mat, gain_ref, shift_ref, up_one, up_two, down_ref,
+    out_ref, grad_two_ref, grads_hbm, lse_out, delta_out, up_keep, up_first, up_second, up_both,
+    down_keep, down_away, cross_sum, gain_grad, shift_grad,
+    send_sem, recv_sem, load_sem, att_one, att_two, lse_one, lse_two, att_full, att_low, hidden_two,
+    normed_ref, acc_out, acc_grad, grad_att, lse_own, delta_own, up_pair, up_got, down_pair, down_got,
+    cross_pair, cross_got, *, length, tile, bits, steps
 ):
     step = pl.program_id(0)
-    steps = pl.num_programs(0)
-    side = side_ref[0]
+    me, side = lax.axis_index("dp"), lax.axis_index("kv")
     rows, width = hidden_ref.shape
     captions = rows // length
     tiles = rows // tile
     half = width // 2
+    sub = up_one.shape[1]
+    blocks = up_pair.shape[2]
+    own = lambda bit: (me // (1 << bit)) % 2
+
+    def remote(src, dst, index):
+        return pltpu.make_async_remote_copy(
+            src_ref=src, dst_ref=dst, send_sem=send_sem.at[index], recv_sem=recv_sem.at[index],
+            device_id={"kv": 1 - side}, device_id_type=pl.DeviceIdType.MESH,
+        )
+
+    def row_span(index):
+        return pl.ds(pl.multiple_of(index * tile, tile), tile)
+
+    def chunk_copies(slot):
+        return (
+            remote(up_pair.at[slot, 1 - side], up_got.at[slot], 2 + slot),
+            remote(down_pair.at[slot, 1 - side], down_got.at[slot], 4 + slot),
+        )
+
+    cross_copy = lambda: remote(cross_pair.at[1 - side], cross_got, 6)
+    lse_copy = lambda: remote(lse_own, lse_out.at[side], 7)
+    delta_copy = lambda: remote(delta_own, delta_out.at[side], 8)
+    grad_copy = lambda index: remote(
+        grad_att.at[pl.ds(index * tile, tile)], grads_hbm.at[side, pl.ds(index * tile, tile)], 9 + index
+    )
+    lse_store = lambda: pltpu.make_async_copy(lse_own, lse_out.at[side], load_sem.at[2])
+
+    def cut(target, value):
+        count, height, _ = target.shape
+        if height % 16 == 0:
+            target[...] = value.astype(BF16).reshape(target.shape)
+        else:
+            for index in range(count):
+                target[index] = value[index * height : (index + 1) * height].astype(BF16)
 
     @pl.when(step == 0)
     def _():
+        part_load = pltpu.make_async_copy(part_hbm.at[side], att_one, load_sem.at[0])
+        lse_load = pltpu.make_async_copy(lse_hbm.at[side], lse_one, load_sem.at[1])
+        part_load.start()
+        lse_load.start()
+        barrier = pltpu.get_barrier_semaphore()
+        pl.semaphore_signal(barrier, inc=1, device_id={"kv": 1 - side}, device_id_type=pl.DeviceIdType.MESH)
+        pl.semaphore_wait(barrier, 1)
+        part_swap = remote(part_hbm.at[1 - side], att_two, 0)
+        lse_swap = remote(lse_hbm.at[1 - side], lse_two, 1)
+        lse_swap.start()
+        part_swap.start()
         mask_low = same_head().astype(BF16)
+        lse_load.wait()
+        part_load.wait()
+        lse_swap.wait()
+        part_swap.wait()
 
         def one_caption(cap, carry):
             span = pl.ds(pl.multiple_of(cap * length, length), length)
@@ -244,7 +293,7 @@
                 second = lse_two[cap, group : group + 1]
                 peak = jnp.maximum(first, second)
                 lse = peak + jnp.log(jnp.exp(first - peak) + jnp.exp(second - peak))
-                lse_ref[cap, group : group + 1] = lse
+                lse_own[cap, group : group + 1] = lse
                 weight_one = lanes_to_rows(jnp.exp(first - lse), mask_low)
                 weight_two = lanes_to_rows(jnp.exp(second - lse), mask_low)
                 mixed = (
@@ -256,9 +305,11 @@
             return carry
 
         lax.fori_loop(0, captions, one_caption, 0)
+        lse_copy().start()
+        lse_store().start()
 
         def one_tile(index, carry):
-            span = pl.ds(pl.multiple_of(index * tile, tile), tile)
+            span = row_span(index)
             two = hidden_ref[span, :] + dot(att_low[span, :], cross_mat[...])
             hidden_two[span, :] = two
             unit, _ = normalize(two)
@@ -269,45 +320,64 @@
 
         lax.fori_loop(0, tiles, one_tile, 0)
 
-    pre = dot(normed_ref[...], up_mat[...])
+    slot = step % 2
+    up_mat = jnp.concatenate([up_one[...], up_two[...]], axis=1)
+    down_mat = down_ref[...].reshape(2 * sub, width)
+    pre = dot(normed_ref[...], up_mat)
     cdf = 0.5 * (1.0 + lax.erf(pre * 0.7071067811865476))
     act = (pre * cdf).astype(BF16)
-    acc_out[...] += dot(act, down_mat[...])
+    acc_out[...] += dot(act, down_mat)
     cot = cot_ref[...]
     density = jnp.exp(-0.5 * pre * pre) * 0.3989422804014327
-    grad_up = (dot_nt(cot, down_mat[...]) * (cdf + pre * density)).astype(BF16)
-    acc_grad[...] += dot_nt(grad_up, up_mat[...])
+    grad_up = (dot_nt(cot, down_mat) * (cdf + pre * density)).astype(BF16)
+    acc_grad[...] += dot_nt(grad_up, up_mat)
     grad_down = dot_tn(act, cot).astype(BF16)
-    grad_w = dot_tn(normed_ref[...], grad_up).astype(BF16)
-    in_mine = (step >= steps // 2) == (side == 1)
-
-    @pl.when(in_mine)
+    grad_w = dot_tn(normed_ref[...], grad_up)
+    for part in range(2):
+        cut(up_pair.at[slot, part], grad_w[:, part * sub : (part + 1) * sub])
+        down_pair[slot, part] = grad_down[:, part * half : (part + 1) * half].reshape(2, sub, half)
+
+    def take(chunk, place):
+        for copy in chunk_copies(place):
+            copy.wait()
+        cols = pl.ds(pl.multiple_of(chunk * sub, sub), sub)
+        for index, target in enumerate((up_keep, up_first, up_second, up_both)):
+            flip = (index % 2, index // 2)
+            low_bit, high_bit = (own(b) + f - 2 * own(b) * f for b, f in zip(bits[:2], flip))
+            near = high_bit * 2 + low_bit
+
+            def one(block, carry):
+                source = block * 4 + near
+                target[block, :, cols] = add_low(up_pair[place, side, source], up_got[place, source])
+                return carry
+
+            lax.fori_loop(0, blocks // 4, one, 0)
+        total = add_low(down_pair[place, side], down_got[place])
+        span = pl.ds(pl.multiple_of(chunk % (steps // 2) * sub, sub), sub)
+        stays = chunk // (steps // 2) == own(bits[-2])
+
+        @pl.when(stays)
+        def _():
+            down_keep[:, span, :] = total
+
+        @pl.when(jnp.logical_not(stays))
+        def _():
+            down_away[:, span, :] = total
+
+    @pl.when(step > 0)
     def _():
-        up_mine[...] = grad_w
-
-    @pl.when(jnp.logical_not(in_mine))
-    def _():
-        up_send[...] = grad_w
-
-    @pl.when(side == 0)
-    def _():
-        down_mine[...] = grad_down[:, :half]
-        down_send[...] = grad_down[:, half:]
-
-    @pl.when(side == 1)
-    def _():
-        down_mine[...] = grad_down[:, half:]
-        down_send[...] = grad_down[:, :half]
+        take(step - 1, (step + 1) % 2)
+
+    for copy in chunk_copies(slot):
+        copy.start()
 
     @pl.when(step == steps - 1)
     def _():
         mask_low = same_head().astype(BF16)
         gain_grad[...] = jnp.zeros_like(gain_grad)
         shift_grad[...] = jnp.zeros_like(shift_grad)
-
-        def one_tile(index, carry):
-            span = pl.ds(pl.multiple_of(index * tile, tile), tile)
-            out_ref[span, :] = acc_out[span, :].astype(BF16)
+        for index in range(tiles):
+            span = pl.ds(index * tile, tile)
             unit, inverse = normalize(hidden_two[span, :])
             grad = acc_grad[span, :]
             gain_grad[...] += jnp.sum(grad * unit, axis=0, keepdims=True)
@@ -316,85 +386,101 @@
             grad_two_ref[span, :] = two
             low = two.astype(BF16)
             normed_ref[span, :] = low
-            grad_att_ref[span, :] = dot_nt(low, cross_mat[...]).astype(BF16)
-            return carry
-
-        lax.fori_loop(0, tiles, one_tile, 0)
-        grad_cross = dot_tn(att_low[...], normed_ref[...]).astype(BF16)
-
-        @pl.when(side == 0)
-        def _():
-            cross_mine[...] = grad_cross[:, :half]
-            cross_send[...] = grad_cross[:, half:]
-
-        @pl.when(side == 1)
-        def _():
-            cross_mine[...] = grad_cross[:, half:]
-            cross_send[...] = grad_cross[:, :half]
+            grad_att[span, :] = dot_nt(low, cross_mat[...]).astype(BF16)
+            grad_copy(index).start()
+        grad_store = pltpu.make_async_copy(grad_att, grads_hbm.at[side], load_sem.at[0])
+        grad_store.start()
 
         def one_caption(cap, carry):
             span = pl.ds(pl.multiple_of(cap * length, length), length)
             for group in range(GROUPS):
                 lo = group * LANES
-                product = grad_att_ref[span, lo : lo + LANES].astype(F32) * att_full[span, lo : lo + LANES]
-                delta_ref[cap, group : group + 1] = rows_to_lanes(product, mask_low)
+                product = grad_att[span, lo : lo + LANES].astype(F32) * att_full[span, lo : lo + LANES]
+                delta_own[cap, group : group + 1] = rows_to_lanes(product, mask_low)
             return carry
 
         lax.fori_loop(0, captions, one_caption, 0)
-
-
-def feed(side, att_one, lse_one, att_two, lse_two, hidden, cot, cross_mat, gain, shift, up_mat, down_mat, length):
+        delta_copy().start()
+        delta_store = pltpu.make_async_copy(delta_own, delta_out.at[side], load_sem.at[1])
+        delta_store.start()
+        grad_cross = dot_tn(att_low[...], normed_ref[...])
+        for part in range(2):
+            cut(cross_pair.at[part], grad_cross[:, part * half : (part + 1) * half])
+        cross_copy().start()
+        out_ref[...] = acc_out[...].astype(BF16)
+        take(steps - 1, (steps - 1) % 2)
+        cross_copy().wait()
+
+        def one(block, carry):
+            cross_sum[block] = add_low(cross_pair[side, block], cross_got[block])
+            return carry
+
+        lax.fori_loop(0, blocks, one, 0)
+        for copy in [lse_copy(), lse_store(), delta_copy(), delta_store, grad_store]:
+            copy.wait()
+        for index in range(tiles):
+            grad_copy(index).wait()
+
+
+def feed(part, lse_part, hidden, cot, cross_mat, gain, shift, up_mat, down_mat, length, size):
     rows, width = hidden.shape
     captions = rows // length
     units = up_mat.shape[1]
-    chunk = 512
-    steps = units // chunk
-    middle = steps // 2
+    sub = 256
+    steps = units // 2 // sub
     tile = min(256, rows)
     half = width // 2
+    block = width // size
+    bits = list(range(size.bit_length() - 1))
     stat = (captions, GROUPS, LANES)
     sds = jax.ShapeDtypeStruct
-    clip = lambda v: jnp.minimum(jnp.maximum(v, 0), middle - 1)
-    mine_map = lambda i, side: (0, clip(i - middle * side[0]))
-    send_map = lambda i, side: (0, clip(i - middle * (1 - side[0])))
+    once = lambda shape: pl.BlockSpec(shape, lambda *_: (0,) * len(shape), pipeline_mode=pl.Buffered(1))
+    hbm = pl.BlockSpec(memory_space=pl.ANY)
+    copies = 9 + rows // tile
+    f32_rows = lambda: pltpu.VMEM((rows, width), F32)
+    low_rows = lambda: pltpu.VMEM((rows, width), BF16)
+    quarter = (size // 4, block, units // 2)
     return pl.pallas_call(
-        functools.partial(feed_body, length=length, tile=tile),
-        grid_spec=pltpu.PrefetchScalarGridSpec(
-            num_scalar_prefetch=1,
-            grid=(steps,),
-            in_specs=[
-                whole((rows, width)), whole(stat), whole((rows, width)), whole(stat),
-                whole((rows, width)), whole((rows, width)), whole((width, width)),
-                whole((width,)), whole((width,)),
-                pl.BlockSpec((width, chunk), lambda i, *_: (0, i)),
-                pl.BlockSpec((chunk, width), lambda i, *_: (i, 0)),
-            ],
-            out_specs=[
-                whole((rows, width)), whole((rows, width)), whole((rows, width)), whole(stat),
-                whole(stat),
-                pl.BlockSpec((width, chunk), mine_map), pl.BlockSpec((width, chunk), send_map),
-                pl.BlockSpec((chunk, half), lambda i, *_: (i, 0)),
-                pl.BlockSpec((chunk, half), lambda i, *_: (i, 0)),
-                whole((width, half)), whole((width, half)),
-                whole((1, width)), whole((1, width)),
-            ],
-            scratch_shapes=[
-                pltpu.VMEM((rows, width), F32), pltpu.VMEM((rows, width), BF16),
-                pltpu.VMEM((rows, width), F32), pltpu.VMEM((rows, width), BF16),
-                pltpu.VMEM((rows, width), F32), pltpu.VMEM((rows, width), F32),
-            ],
+        functools.partial(feed_body, length=length, tile=tile, bits=bits, steps=steps),
+        grid=(steps,),
+        in_specs=[
+            hbm, hbm, once((rows, width)), once((rows, width)), once((width, width)),
+            once((width,)), once((width,)),
+            pl.BlockSpec((width, sub), lambda i: (0, i)),
+            pl.BlockSpec((width, sub), lambda i: (0, i + steps)),
+            pl.BlockSpec((2, sub, width), lambda i: (0, i, 0)),
+        ],
+        out_specs=[
+            whole((rows, width)), whole((rows, width)), hbm, hbm, hbm,
+            whole(quarter), whole(quarter), whole(quarter), whole(quarter),
+            whole((2, units // 4, half)), whole((2, units // 4, half)),
+            whole((size, block, half)), whole((1, width)), whole((1, width)),
+        ],
+        out_shape=[
+            sds((rows, width), BF16), sds((rows, width), F32), sds((2, rows, width), BF16),
+            sds((2,) + stat, F32), sds((2,) + stat, F32),
+            sds(quarter, BF16), sds(quarter, BF16), sds(quarter, BF16), sds(quarter, BF16),
+            sds((2, units // 4, half), BF16), sds((2, units // 4, half), BF16),
+            sds((size, block, half), BF16), sds((1, width), F32), sds((1, width), F32),
+        ],
+        scratch_shapes=[
+            pltpu.SemaphoreType.DMA((copies,)), pltpu.SemaphoreType.DMA((copies,)),
+            pltpu.SemaphoreType.DMA((3,)),
+            low_rows(), low_rows(), pltpu.VMEM(stat, F32), pltpu.VMEM(stat, F32), f32_rows(), low_rows(),
+            f32_rows(), low_rows(), f32_rows(), f32_rows(), low_rows(),
+            pltpu.VMEM(stat, F32), pltpu.VMEM(stat, F32),
+            pltpu.VMEM((2, 2, size, block, sub), BF16), pltpu.VMEM((2, size, block, sub), BF16),
+            pltpu.VMEM((2, 2, 2, sub, half), BF16), pltpu.VMEM((2, 2, sub, half), BF16),
+            pltpu.VMEM((2, size, block, half), BF16), pltpu.VMEM((size, block, half), BF16),
+        ],
+        compiler_params=pltpu.CompilerParams(
+            vmem_limit_bytes=VMEM_MOST, collective_id=1, has_side_effects=True
         ),
-        out_shape=[
-            sds((rows, width), BF16), sds((rows, width), F32), sds((rows, width), BF16),
-            sds(stat, F32), sds(stat, F32),
-            sds((width, units // 2), BF16), sds((width, units // 2), BF16),
-            sds((units, half), BF16), sds((units, half), BF16),
-            sds((width, half), BF16), sds((width, half), BF16),
-            sds((1, width), F32), sds((1, width), F32),
-        ],
-        compiler_params=pltpu.CompilerParams(vmem_limit_bytes=VMEM_LIMIT),
         name="feed",
-    )(side, att_one, lse_one, att_two, lse_two, hidden, cot, cross_mat, gain, shift, up_mat, down_mat)
+    )(
+        part.reshape(2, rows, width), lse_part.reshape((2,) + stat), hidden, cot, cross_mat, gain, shift,
+        up_mat, up_mat, down_mat.reshape(2, units // 2, width),
+    )
 
 
 def cross_back_body(
@@ -593,7 +679,7 @@
 def end_body(
     back_hbm, hidden_hbm, grad_two_hbm, att_hbm, qkv_hbm, tok_hbm, qkv_mat_hbm, out_mat_hbm, query_mat_hbm,
     gain_one, shift_one, gain_two, shift_two, gain_three, shift_three,
-    up_ref, down_ref, cross_ref, kv_mine, kv_send,
+    up_keep, up_first, up_second, up_both, down_keep, down_away, cross_ref, kv_mine, kv_send,
     grad_tok, up_out, down_out, cross_out, qkv_out, out_out, query_out, kv_out, gains_out,
     *scratch, plan, bits, length, tile
 ):
@@ -602,8 +688,9 @@
         send_sem, recv_sem, load_sem, back_one, back_two, hidden, grad_two, att, qkv, tok, qkv_mat,
         out_mat, query_mat, back_sum, normed, low, grad_att, grad_qkv, acc, gains_all, gain_kv,
         gain_buf, gain_recv, qkv_mine, qkv_send, out_mine, out_send, query_mine, query_send,
-    ) = scratch[:29]
-    rest = scratch[29:]
+        up_ref, down_ref,
+    ) = scratch[:31]
+    rest = scratch[31:]
     sums = Sums(send_sem, recv_sem)
     side = sums.side
     captions = back_one.shape[0]
@@ -643,6 +730,22 @@
     swap.start()
     for piece in image:
         piece.start_kv()
+
+    def sum_terms(target, terms):
+        count = len(target.shape) - 2
+
+        def one(i, carry):
+            lead = tuple((i // (1 << (count - 1 - d))) % 2 for d in range(count))
+            total = terms[0][lead].astype(F32)
+            for term in terms[1:]:
+                total += term[lead].astype(F32)
+            target[lead] = total.astype(BF16)
+            return carry
+
+        lax.fori_loop(0, 1 << count, one, 0)
+
+    sum_terms(up_ref, (up_keep, up_first, up_second, up_both))
+    sum_terms(down_ref, (down_keep, down_away))
     for piece in early:
         piece.start()
     gains_all[...] = jnp.zeros_like(gains_all)
@@ -794,20 +897,16 @@
     tile = min(256, rows)
     block = width // size
     lead = (2,) * len(bits)
-    up, down, cross = early
-    cut_up = up.shape[-1] // 384 * 256
+    up_terms, down_terms, cross = early
+    up, down = up_terms[0], down_terms[0]
     cut_down = down.shape[-1] // 384 * 256
     third = width // 3
-    early_order = lambda by, array: [b for b in turned(bits, by) if b in bits[len(bits) + 2 - array.ndim :]]
-    early_axes = lambda array: axes[: array.ndim - 2]
-    plan = []
-    for name, array, cuts in (
-        ("up", up, ((0, cut_up, 0), (cut_up, up.shape[-1] - cut_up, 2))),
-        ("down", down, ((0, cut_down, 1), (cut_down, down.shape[-1] - cut_down, 2))),
-        ("cross", cross, ((0, cross.shape[-1], 1),)),
-    ):
-        for col, cols, by in cuts:
-            plan.append((name, col, cols, early_axes(array), early_order(by, array), False))
+    plan = [("up", 0, up.shape[-1], axes[:-2], bits[2:], False)]
+    down_axes = axes[:1] + axes[2:]
+    for col, cols, by in ((0, cut_down, 0), (cut_down, down.shape[-1] - cut_down, 1)):
+        order = [b for b in turned(bits, by) if b in down_axes]
+        plan.append(("down", col, cols, down_axes, order, False))
+    plan.append(("cross", 0, cross.shape[-1], axes, turned(bits, 2), False))
     plan.append(("query", 0, width // 2, axes, turned(bits, 0), True))
     plan.append(("out", 0, width // 2, axes, turned(bits, 1), True))
     for by in range(3):
@@ -832,7 +931,7 @@
     low_rows = lambda cols: pltpu.VMEM((rows, cols), BF16)
     return pl.pallas_call(
         functools.partial(end_body, plan=plan, bits=bits, length=length, tile=tile),
-        in_specs=[hbm] * 9 + [vmem] * 6 + [vmem] * 4 + [hbm],
+        in_specs=[hbm] * 9 + [vmem] * 6 + [vmem] * 8 + [hbm],
         out_specs=[vmem] * len(outs),
         out_shape=outs,
         scratch_shapes=[
@@ -847,7 +946,7 @@
             pltpu.VMEM((8, width // 2), F32), pltpu.VMEM((len(bits) + 1, 8, width // 2), F32),
             pltpu.VMEM((len(bits), 8, width // 2), F32),
             cut(3 * width // 2), cut(3 * width // 2), cut(width // 2), cut(width // 2),
-            cut(width // 2), cut(width // 2),
+            cut(width // 2), cut(width // 2), pltpu.VMEM(up.shape, BF16), pltpu.VMEM(down.shape, BF16),
         ] + buffers,
         compiler_params=pltpu.CompilerParams(
             vmem_limit_bytes=VMEM_MOST, collective_id=0, has_side_effects=True
@@ -855,7 +954,7 @@
         name="end",
     )(
         back, hidden, grad_two, att, qkv, tokens, qkv_mat, out_mat, query_mat, gain_one, shift_one,
-        gain_two, shift_two, gain_three, shift_three, up, down, cross, kv_mine, kv_send,
+        gain_two, shift_two, gain_three, shift_three, *up_terms, *down_terms, cross, kv_mine, kv_send,
     )
 
 
@@ -895,7 +994,6 @@
     me = lax.axis_index("dp")
     groups = lax.axis_size("dp")
     side_arr = side.reshape(1)
-    row = lambda v: v
     tok = tokens.reshape(captions * length, width)
     cot = cotangent.reshape(captions * length, width)
     short = -(-SHORT // 16) * 16
@@ -903,8 +1001,8 @@
     swap = lambda v: exchange(v, "kv", 1, 2)
 
     qkv, att, hidden, query = token_start(
-        tok, row(norm1_gain), row(norm1_shift), self_qkv, self_out, row(norm2_gain),
-        row(norm2_shift), cross_q, length,
+        tok, norm1_gain, norm1_shift, self_qkv, self_out, norm2_gain,
+        norm2_shift, cross_q, length,
     )
 
     def both(own):
@@ -913,40 +1011,38 @@
         second = jnp.where(side == 0, other, own)
         return jnp.concatenate([first, second], axis=0)
 
-    def own_part(array):
-        return lax.dynamic_slice_in_dim(array, side * captions, captions, 0)
-
-    def other_part(array):
-        return lax.dynamic_slice_in_dim(array, (1 - side) * captions, captions, 0)
-
     queries = both(query.reshape(captions, length, width))
     kv, part, lse_part = cross_start(valid, images, cross_kv, queries, short)
-    flat = lambda v: v.reshape(captions * length, width)
     (
-        layer_out, grad_two, grad_att, lse, delta, up_mine, up_send, down_mine, down_send,
-        cross_mine, cross_send, gain3, shift3,
+        layer_out, grad_two, grads, lse, delta, up_keep, up_first, up_second, up_both, down_keep,
+        down_away, cross_sum, gain3, shift3,
     ) = feed(
-        side_arr, flat(own_part(part)), own_part(lse_part), flat(swap(other_part(part))),
-        swap(other_part(lse_part)), hidden, cot, cross_out, row(norm3_gain), row(norm3_shift),
-        w_up, w_down, length,
+        part, lse_part, hidden, cot, cross_out, norm3_gain, norm3_shift, w_up, w_down, length, groups
     )
-    early = [
-        split_rows(add_low(mine, exchange(send, "kv", 1, 2)), groups)
-        for mine, send in ((up_mine, up_send), (down_mine, down_send), (cross_mine, cross_send))
+    bits = groups.bit_length() - 1
+    cubes = lambda v, count: v.reshape((2,) * count + (v.shape[0] * v.shape[1] >> count, v.shape[2]))
+    up_terms = [up_keep] + [
+        exchange(away, "dp", flip, groups) for away, flip in ((up_first, 1), (up_second, 2), (up_both, 3))
     ]
-
-    grads = both(grad_att.reshape(captions, length, width))
+    down_terms = [down_keep, exchange(down_away, "dp", 1 << (bits - 2), groups)]
+    early = (
+        [cubes(v, bits - 2) for v in up_terms], [cubes(v, bits - 1) for v in down_terms],
+        cubes(cross_sum, bits),
+    )
+
+    stats = lambda v: v.reshape(caps, GROUPS, LANES)
     back, images_grad, kv_mine, kv_send = cross_back(
-        valid, side_arr, kv, queries, grads, both(lse), both(delta), cross_kv, images, short
+        valid, side_arr, kv, queries, grads.reshape(caps, length, width), stats(lse), stats(delta),
+        cross_kv, images, short
     )
     cut = lambda v: split_rows(v, groups)
     (
         tokens_grad, w_up_grad, down_grad, cross_out_grad, self_qkv_grad, self_out_grad, cross_q_grad,
-        cross_kv_grad, gains,
+        cross_kv_grad, gains, layer_out,
     ) = hand_over(*end(
         back, hidden, grad_two, att, qkv, tok, self_qkv, self_out, cross_q, norm1_gain, norm1_shift,
         norm2_gain, norm2_shift, gain3, shift3, early, cut(kv_mine), cut(kv_send), length, groups,
-    ))
+    ), layer_out)
     return (
         layer_out.reshape(captions, length, width),
         tokens_grad.reshape(captions, length, width),

time: 262 us -> 230 us (0.88)
  other arithmetic: 16.2 us -> 3.08 us
  Pallas kernels: 225 us -> 215 us
  waiting for transfers between devices: 10.2 us -> 1.96 us
  local copies, waits for them, and re-layouts: 5.54 us -> 1.71 us
    pallas_call x1, Pallas kernels: 89.6 us -> 74.4 us  [end(): pl.pallas_call(functools.partial(end_body, plan=plan, bits=bits, length=l...]
    convert_element_type x3 -> x0, other arithmetic: 9.57 us -> none  [add_low(): return (first.astype(F32) + second.astype(F32)).astype(BF16)]
    ppermute x9 -> x5, waiting for transfers between devices: 10.2 us -> 1.96 us  [exchange(): return lax.ppermute(value, axis, [(i, i ^ bit) for i in range(size)])]
    pallas_call x1, Pallas kernels: 34.2 us -> 39.5 us  [feed(): pl.pallas_call(functools.partial(feed_body, length=length, tile=tile, bit...]
    dynamic_slice x2 -> x0, local copies, waits for them, and re-layouts: 3.08 us -> none  [other_part(): return lax.dynamic_slice_in_dim(array, (1 - side) * captions, captions, 0)]
  transfers between devices with their start and end apart: 9 -> 5, of which waited for: 3 -> 1; matrix products, arithmetic and copies ran while one was open for 4% -> 0% of each run, Pallas kernels for 22% -> 24%
where the time goes in v4:
time: 230 us; the launch traced here: 227 us
  Pallas kernels  215 us (93%)
  starting transfers between devices  4.43 us (2%)
  other arithmetic  3.08 us (1%)
    pallas_call x1, Pallas kernels, end(): pl.pallas_call(functools.partial(end_body, plan=plan, bits=bits, length=l...  74.4 us
    pallas_call x1, Pallas kernels, cross_back(): pl.pallas_call(functools.partial(cross_back_body, short=short), grid_spec...  54.2 us
    pallas_call x1, Pallas kernels, feed(): pl.pallas_call(functools.partial(feed_body, length=length, tile=tile, bit...  39.5 us
    pallas_call x1, Pallas kernels, cross_start(): pl.pallas_call(functools.partial(cross_start_body, short=short), grid_spe...  31.1 us
    pallas_call x1, Pallas kernels, token_start(): pl.pallas_call(functools.partial(token_start_body, length=length), grid=(...  12.5 us
  transfers between devices with their start and end apart: 5, of which 1 were waited for; matrix products, arithmetic and copies ran while one was open for 0% of the time, Pallas kernels for 24%

profile of v4, /device:TPU:2, one launch (start us, length us, event | category | flops | bytes accessed | tf_op | source)
XLA Modules:
  0.0 227.0 jit_solution(14590942096075100745)
XLA Ops:
  0.6 0.0 copy-start
  0.7 12.5 %token_start.1 = (bf16[512,2304]{1,0:T(8,128)(2,1)}, bf16[512,768]{1,0:T(8,128)(2,1)}, f32[512,768]{1,0:T(8,128)}, bf16[512,768]{1,0:T(8,128)(2,1)}) custom-call(bf16[512,768]{1,0:T(8,128)(2,1)} %bitcast.22, f32[768]{0:T(1024)} %gain_one.3, f32[768]{0:T(1024)} %shift_one.3, bf16[768,2304]{1,0:T(8,128)(2,1)} %qkv_mat_hbm.1, bf16[768,768]{1,0:T(8,128)(2,1)} %out_mat_hbm.1, ...), custom_call_target="tpu_custom_call" | custom-call | tf_op jit(solution)/shard_map/token_start/pallas_call | solution.py:144
  13.2 0.0 collective-permute-start
  13.2 0.0 copy-done
  13.2 0.5 subtract_clamp_fusion.valid_ref
  13.7 2.0 collective-permute-done
  15.7 1.2 broadcast_select_fusion.1
  16.9 1.3 pad_maximum_fusion.query_ref
  18.2 31.1 %cross_start.1 = (bf16[16,288,1536]{2,1,0:T(8,128)(2,1)}, bf16[16,64,768]{2,1,0:T(8,128)(2,1)}, f32[16,3,256]{2,1,0:T(4,128)}) custom-call(s32[16]{0:T(128)} %subtract_clamp_fusion.valid_ref, bf16[16,288,768]{2,1,0:T(8,128)(2,1)} %img_ref.3, bf16[768,1536]{1,0:T(8,128)(2,1)} %kv_mat.3, bf16[16,64,768]{2,1,0:T(8,128)(2,1)} %pad_maximum_fusion.query_ref), custom_call_target="tpu_custom_call" | custom-call | tf_op jit(solution)/shard_map/cross_start/pallas_call | solution.py:202
  49.3 39.5 %feed.1 = (bf16[512,768]{1,0:T(8,128)(2,1)}, f32[512,768]{1,0:T(8,128)}, bf16[2,512,768]{2,1,0:T(8,128)(2,1)}, f32[2,8,3,256]{3,2,1,0:T(4,128)}, f32[2,8,3,256]{...) custom-call(bf16[2,512,768]{2,1,0:T(8,128)(2,1)} %bitcast.24, ...), custom_call_target="tpu_custom_call" | custom-call | tf_op jit(solution)/shard_map/feed/pallas_call | solution.py:443
  88.8 0.9 collective-permute-start.4
  89.8 0.6 collective-permute-start.1
  90.4 1.5 collective-permute-start.2
  91.8 1.4 collective-permute-start.3
  93.3 54.2 %cross_back.1 = (bf16[16,64,768]{2,1,0:T(8,128)(2,1)}, bf16[16,288,768]{2,1,0:T(8,128)(2,1)}, bf16[768,768]{1,0:T(8,128)(2,1)}, bf16[768,768]{1,0:T(8,128)(2,1)}) custom-call(s32[16]{0:T(128)} %subtract_clamp_fusion.valid_ref, s32[1]{0:T(128)} %bitcast.side_ref, bf16[16,288,1536]{2,1,0:T(8,128)(2,1)} %get-tuple-element.61.kv_ref, ...), custom_call_target="tpu_custom_call" | custom-call | tf_op jit(solution)/shard_map/cross_back/pallas_call | solution.py:559
  147.5 0.0 collective-permute-done.1
  147.5 0.0 collective-permute-done.2
  147.5 0.0 collective-permute-done.3
  147.5 0.0 collective-permute-done.4
  147.5 74.4 %end.1 = (bf16[512,768]{1,0:T(8,128)(2,1)}, f32[48,1536]{1,0:T(8,128)}, f32[192,384]{1,0:T(8,128)}, f32[48,384]{1,0:T(8,128)}, f32[48,1152]{1,0:T(8,128)}, /*ind...) custom-call(bf16[16,64,768]{2,1,0:T(8,128)(2,1)} %get-tuple-element.68.back_hbm, ...), custom_call_target="tpu_custom_call" | custom-call | tf_op jit(solution)/shard_map/end/pallas_call | solution.py:932
  222.0 3.4 %hand_over.1 = (bf16[512,768]{1,0:T(8,128)(2,1)}, f32[48,1536]{1,0:T(8,128)}, f32[192,384]{1,0:T(8,128)}, f32[48,384]{1,0:T(8,128)}, f32[48,1152]{1,0:T(8,128)},...) custom-call(bf16[512,768]{1,0:T(8,128)(2,1)} %get-tuple-element.83.r, ...), custom_call_target="tpu_custom_call" | custom-call | tf_op jit(solution)/shard_map/hand_over/pallas_call | solution.py:969
  225.3 1.7 slice_reduce_fusion
Async XLA Ops:
  0.6 12.6 %copy-start = (s32[16]{0:T(128)S(1)}, s32[16]{0:T(128)}, u32[]{:S(2)}) copy-start(s32[16]{0:T(128)} %param.19) | copy-start | bytes 196
  13.2 2.5 %collective-permute-start = (bf16[8,64,768]{2,1,0:T(8,128)(2,1)}, bf16[8,64,768]{2,1,0:T(8,128)(2,1)S(1)}, u32[]{:S(2)}, u32[]{:S(2)}) collective-permute-start(bf16[8,64,768]{2,1,0:T(8,128)(2,1)} %bitcast.30), channel_id=1, source_target_pairs={{0,1},{1,0},{2,3},{3,2},{4,5},{5,4},{6,7},{7,6},{8,9},{9,8},{10,11... | collective-permute-start | bytes 2359304 | tf_op jit(solution)/shard_map/ppermute | solution.py:979
  88.8 58.7 %collective-permute-start.4 = (bf16[2,768,384]{2,1,0:T(8,128)(2,1)}, bf16[2,768,384]{2,1,0:T(8,128)(2,1)}, u32[]{:S(2)}, u32[]{:S(2)}) collective-permute-start(bf16[2,768,384]{2,1,0:T(8,128)(2,1)} %get-tuple-element.79), channel_id=1, source_target_pairs={{0,8},{2,10},{4,12},{6,14},{8,0},{10,2},{12,4},{14,6},{16,24},{18,... | collective-permute-start | bytes 3538952 | tf_op jit(solution)/shard_map/ppermute | solution.py:979
  89.8 57.7 %collective-permute-start.1 = (bf16[4,48,1536]{2,1,0:T(8,128)(2,1)}, bf16[4,48,1536]{2,1,0:T(8,128)(2,1)}, u32[]{:S(2)}, u32[]{:S(2)}) collective-permute-start(bf16[4,48,1536]{2,1,0:T(8,128)(2,1)} %get-tuple-element.75), channel_id=1, source_target_pairs={{0,2},{2,0},{4,6},{6,4},{8,10},{10,8},{12,14},{14,12},{16,18},{18,... | collective-permute-start | bytes 1769480 | tf_op jit(solution)/shard_map/ppermute | solution.py:979
  90.4 57.1 %collective-permute-start.2 = (bf16[4,48,1536]{2,1,0:T(8,128)(2,1)}, bf16[4,48,1536]{2,1,0:T(8,128)(2,1)}, u32[]{:S(2)}, u32[]{:S(2)}) collective-permute-start(bf16[4,48,1536]{2,1,0:T(8,128)(2,1)} %get-tuple-element.76), channel_id=1, source_target_pairs={{0,4},{2,6},{4,0},{6,2},{8,12},{10,14},{12,8},{14,10},{16,20},{18,... | collective-permute-start | bytes 1769480 | tf_op jit(solution)/shard_map/ppermute | solution.py:979
  91.8 55.7 %collective-permute-start.3 = (bf16[4,48,1536]{2,1,0:T(8,128)(2,1)}, bf16[4,48,1536]{2,1,0:T(8,128)(2,1)}, u32[]{:S(2)}, u32[]{:S(2)}) collective-permute-start(bf16[4,48,1536]{2,1,0:T(8,128)(2,1)} %get-tuple-element.77), channel_id=1, source_target_pairs={{0,6},{2,4},{4,2},{6,0},{8,14},{10,12},{12,10},{14,8},{16,22},{18,... | collective-permute-start | bytes 1769480 | tf_op jit(solution)/shard_map/ppermute | solution.py:979

commit v5 on v4

--- a/solution.py
+++ b/solution.py
@@ -217,23 +217,30 @@
     )(valid, images, kv_mat, queries)
 
 
+def cut_rows(target, value):
+    count, height, _ = target.shape
+    if height % 16 == 0:
+        target[...] = value.astype(BF16).reshape(target.shape)
+    else:
+        for index in range(count):
+            target[index] = value[index * height : (index + 1) * height].astype(BF16)
+
+
 def feed_body(
     part_hbm, lse_hbm, hidden_ref, cot_ref, cross_mat, gain_ref, shift_ref, up_one, up_two, down_ref,
-    out_ref, grad_two_ref, grads_hbm, lse_out, delta_out, up_keep, up_first, up_second, up_both,
-    down_keep, down_away, cross_sum, gain_grad, shift_grad,
+    out_ref, grad_two_ref, grads_hbm, lse_out, delta_out, up_sum, down_sum, cross_sum, gain_grad, shift_grad,
     send_sem, recv_sem, load_sem, att_one, att_two, lse_one, lse_two, att_full, att_low, hidden_two,
     normed_ref, acc_out, acc_grad, grad_att, lse_own, delta_own, up_pair, up_got, down_pair, down_got,
-    cross_pair, cross_got, *, length, tile, bits, steps
+    cross_pair, cross_got, *, length, tile, steps
 ):
     step = pl.program_id(0)
-    me, side = lax.axis_index("dp"), lax.axis_index("kv")
+    side = lax.axis_index("kv")
     rows, width = hidden_ref.shape
     captions = rows // length
     tiles = rows // tile
     half = width // 2
     sub = up_one.shape[1]
     blocks = up_pair.shape[2]
-    own = lambda bit: (me // (1 << bit)) % 2
 
     def remote(src, dst, index):
         return pltpu.make_async_remote_copy(
@@ -257,14 +264,6 @@
         grad_att.at[pl.ds(index * tile, tile)], grads_hbm.at[side, pl.ds(index * tile, tile)], 9 + index
     )
     lse_store = lambda: pltpu.make_async_copy(lse_own, lse_out.at[side], load_sem.at[2])
-
-    def cut(target, value):
-        count, height, _ = target.shape
-        if height % 16 == 0:
-            target[...] = value.astype(BF16).reshape(target.shape)
-        else:
-            for index in range(count):
-                target[index] = value[index * height : (index + 1) * height].astype(BF16)
 
     @pl.when(step == 0)
     def _():
@@ -334,35 +333,15 @@
     grad_down = dot_tn(act, cot).astype(BF16)
     grad_w = dot_tn(normed_ref[...], grad_up)
     for part in range(2):
-        cut(up_pair.at[slot, part], grad_w[:, part * sub : (part + 1) * sub])
+        cut_rows(up_pair.at[slot, part], grad_w[:, part * sub : (part + 1) * sub])
         down_pair[slot, part] = grad_down[:, part * half : (part + 1) * half].reshape(2, sub, half)
 
     def take(chunk, place):
         for copy in chunk_copies(place):
             copy.wait()
-        cols = pl.ds(pl.multiple_of(chunk * sub, sub), sub)
-        for index, target in enumerate((up_keep, up_first, up_second, up_both)):
-            flip = (index % 2, index // 2)
-            low_bit, high_bit = (own(b) + f - 2 * own(b) * f for b, f in zip(bits[:2], flip))
-            near = high_bit * 2 + low_bit
-
-            def one(block, carry):
-                source = block * 4 + near
-                target[block, :, cols] = add_low(up_pair[place, side, source], up_got[place, source])
-                return carry
-
-            lax.fori_loop(0, blocks // 4, one, 0)
-        total = add_low(down_pair[place, side], down_got[place])
-        span = pl.ds(pl.multiple_of(chunk % (steps // 2) * sub, sub), sub)
-        stays = chunk // (steps // 2) == own(bits[-2])
-
-        @pl.when(stays)
-        def _():
-            down_keep[:, span, :] = total
-
-        @pl.when(jnp.logical_not(stays))
-        def _():
-            down_away[:, span, :] = total
+        span = pl.ds(pl.multiple_of(chunk * sub, sub), sub)
+        up_sum[:, :, span] = add_low(up_pair[place, side], up_got[place])
+        down_sum[:, span, :] = add_low(down_pair[place, side], down_got[place])
 
     @pl.when(step > 0)
     def _():
@@ -405,7 +384,7 @@
         delta_store.start()
         grad_cross = dot_tn(att_low[...], normed_ref[...])
         for part in range(2):
-            cut(cross_pair.at[part], grad_cross[:, part * half : (part + 1) * half])
+            cut_rows(cross_pair.at[part], grad_cross[:, part * half : (part + 1) * half])
         cross_copy().start()
         out_ref[...] = acc_out[...].astype(BF16)
         take(steps - 1, (steps - 1) % 2)
@@ -431,7 +410,6 @@
     tile = min(256, rows)
     half = width // 2
     block = width // size
-    bits = list(range(size.bit_length() - 1))
     stat = (captions, GROUPS, LANES)
     sds = jax.ShapeDtypeStruct
     once = lambda shape: pl.BlockSpec(shape, lambda *_: (0,) * len(shape), pipeline_mode=pl.Buffered(1))
@@ -439,9 +417,9 @@
     copies = 9 + rows // tile
     f32_rows = lambda: pltpu.VMEM((rows, width), F32)
     low_rows = lambda: pltpu.VMEM((rows, width), BF16)
-    quarter = (size // 4, block, units // 2)
+    up_shape, down_shape = (size, block, units // 2), (2, units // 2, half)
     return pl.pallas_call(
-        functools.partial(feed_body, length=length, tile=tile, bits=bits, steps=steps),
+        functools.partial(feed_body, length=length, tile=tile, steps=steps),
         grid=(steps,),
         in_specs=[
             hbm, hbm, once((rows, width)), once((rows, width)), once((width, width)),
@@ -452,16 +430,12 @@
         ],
         out_specs=[
             whole((rows, width)), whole((rows, width)), hbm, hbm, hbm,
-            whole(quarter), whole(quarter), whole(quarter), whole(quarter),
-            whole((2, units // 4, half)), whole((2, units // 4, half)),
-            whole((size, block, half)), whole((1, width)), whole((1, width)),
+            whole(up_shape), whole(down_shape), whole((size, block, half)), whole((1, width)), whole((1, width)),
         ],
         out_shape=[
             sds((rows, width), BF16), sds((rows, width), F32), sds((2, rows, width), BF16),
             sds((2,) + stat, F32), sds((2,) + stat, F32),
-            sds(quarter, BF16), sds(quarter, BF16), sds(quarter, BF16), sds(quarter, BF16),
-            sds((2, units // 4, half), BF16), sds((2, units // 4, half), BF16),
-            sds((size, block, half), BF16), sds((1, width), F32), sds((1, width), F32),
+            sds(up_shape, BF16), sds(down_shape, BF16), sds((size, block, half), BF16), sds((1, width), F32), sds((1, width), F32),
         ],
         scratch_shapes=[
             pltpu.SemaphoreType.DMA((copies,)), pltpu.SemaphoreType.DMA((copies,)),
@@ -484,55 +458,81 @@
 
 
 def cross_back_body(
-    valid_ref, side_ref, kv_ref, query_ref, grad_ref, lse_ref, delta_ref, kv_mat, img_ref,
-    grad_query_ref, grad_img_ref, mine_ref, send_ref, grad_kv_ref, acc_ref, *, short
+    valid_ref, kv_ref, query_ref, grad_ref, lse_ref, delta_ref, kv_mat, img_ref, up_ref, down_ref, cross_ref,
+    back_ref, grad_img_ref, mine_ref, send_ref, up_out, down_out, cross_out,
+    send_sem, recv_sem, back_send_sem, back_recv_sem, grad_kv_ref, acc_ref, back_away, back_got,
+    *buffers, plan, bits
 ):
     cap = pl.program_id(0)
+    caps = valid_ref.shape[0]
+    captions, length, width = back_ref.shape
     valid = valid_ref[cap]
-    width = query_ref.shape[2]
     slots = kv_ref.shape[1]
     batch = img_ref.shape[0]
     place = cap % batch
+    buffers = list(buffers)
+    sums = Sums(send_sem, recv_sem)
+    side = sums.side
+    named = dict(up=(up_ref, up_out), down=(down_ref, down_out), cross=(cross_ref, cross_out))
+    pieces = []
+    for name, col, cols, axes, order, _ in plan:
+        source, out = named[name]
+        recvs = [buffers.pop(0) for _ in order]
+        pieces.append(Piece(sums, source, out, col, cols, axes, order, recvs))
+
+    def back_copy(index):
+        return pltpu.make_async_remote_copy(
+            src_ref=back_away.at[index], dst_ref=back_got.at[index], send_sem=back_send_sem.at[index],
+            recv_sem=back_recv_sem.at[index], device_id={"kv": 1 - side},
+            device_id_type=pl.DeviceIdType.MESH,
+        )
 
     @pl.when(cap == 0)
     def _():
+        sums.greet(bits)
+        for piece in pieces:
+            piece.start()
         acc_ref[...] = jnp.zeros_like(acc_ref)
 
-    def work(count):
-        mask = same_head()
-        inside = iota((count, LANES), 0) < valid
-        for group in range(GROUPS):
-            lo = group * LANES
-            key = kv_ref[0, :count, lo : lo + LANES]
-            value = kv_ref[0, :count, width + lo : width + lo + LANES]
-            query = spread(query_ref[0, :, lo : lo + LANES], mask)
-            grad = spread(grad_ref[0, :, lo : lo + LANES], mask)
-            scores = dot_nt(key, query)
-            probs = jnp.where(inside, jnp.exp(scores - lse_ref[0, group : group + 1]), 0.0)
-            grad_probs = dot_nt(value, grad)
-            grad_scores = (probs * (grad_probs - delta_ref[0, group : group + 1])).astype(BF16)
-            back = gather_heads(dot_tn(grad_scores, key)) * SCALE
-            grad_query_ref[0, :, lo : lo + LANES] = back.astype(BF16)
-            grad_kv_ref[place, :count, lo : lo + LANES] = dot(grad_scores, query).astype(BF16)
-            grad_kv_ref[place, :count, width + lo : width + lo + LANES] = dot(
-                probs.astype(BF16), grad
-            ).astype(BF16)
-        grad_img_ref[0, :count] = dot_nt(grad_kv_ref[place, :count], kv_mat[...]).astype(BF16)
-        if count < slots:
-            grad_kv_ref[place, count:] = jnp.zeros((slots - count, 2 * width), BF16)
-            grad_img_ref[0, count:] = jnp.zeros((slots - count, width), BF16)
-
-    @pl.when(valid <= 0)
+    for stage in range(len(bits) - 1):
+
+        @pl.when(cap == caps - 1 - (caps >> (stage + 1)))
+        def _():
+            for piece in pieces:
+                piece.advance()
+
+    mask = same_head()
+    inside = iota((slots, LANES), 0) < valid
+    away = cap // captions != side
+    index = cap % captions
+    for group in range(GROUPS):
+        lo = group * LANES
+        key = kv_ref[0, :, lo : lo + LANES]
+        value = kv_ref[0, :, width + lo : width + lo + LANES]
+        query = spread(query_ref[0, :, lo : lo + LANES], mask)
+        grad = spread(grad_ref[0, :, lo : lo + LANES], mask)
+        scores = dot_nt(key, query)
+        probs = jnp.where(inside, jnp.exp(scores - lse_ref[0, group : group + 1]), 0.0)
+        grad_probs = dot_nt(value, grad)
+        grad_scores = (probs * (grad_probs - delta_ref[0, group : group + 1])).astype(BF16)
+        back = (gather_heads(dot_tn(grad_scores, key)) * SCALE).astype(BF16)
+
+        @pl.when(away)
+        def _():
+            back_away[index, :, lo : lo + LANES] = back
+
+        @pl.when(jnp.logical_not(away))
+        def _():
+            back_ref[index, :, lo : lo + LANES] = back
+
+        grad_kv_ref[place, :, lo : lo + LANES] = dot(grad_scores, query).astype(BF16)
+        grad_kv_ref[place, :, width + lo : width + lo + LANES] = dot(probs.astype(BF16), grad).astype(BF16)
+
+    @pl.when(away)
     def _():
-        grad_query_ref[...] = jnp.zeros_like(grad_query_ref)
-        grad_kv_ref[place] = jnp.zeros((slots, 2 * width), BF16)
-        grad_img_ref[...] = jnp.zeros_like(grad_img_ref)
-
-    if short < slots:
-        pl.when((valid > 0) & (valid <= short))(lambda: work(short))
-        pl.when(valid > short)(lambda: work(slots))
-    else:
-        pl.when(valid > 0)(lambda: work(slots))
+        back_copy(index).start()
+
+    grad_img_ref[0] = dot_nt(grad_kv_ref[place], kv_mat[...]).astype(BF16)
 
     @pl.when(place == batch - 1)
     def _():
@@ -540,50 +540,95 @@
         right = grad_kv_ref[...].reshape(batch * slots, 2 * width)
         acc_ref[...] += dot_tn(left, right)
 
-    @pl.when(cap == pl.num_programs(0) - 1)
+    @pl.when(cap == caps - 1)
     def _():
-        side = side_ref[0]
         own = pl.ds(pl.multiple_of(side * width, width), width)
         other = pl.ds(pl.multiple_of((1 - side) * width, width), width)
         mine_ref[...] = acc_ref[:, own].astype(BF16)
         send_ref[...] = acc_ref[:, other].astype(BF16)
 
-
-def cross_back(valid, side, kv, queries, grads, lse, delta, kv_mat, images, short):
+        def one(i, carry):
+            back_copy(i).wait()
+            back_ref[i] = add_low(back_ref[i], back_got[i])
+            return carry
+
+        lax.fori_loop(0, captions, one, 0)
+        for piece in pieces:
+            piece.advance()
+
+
+def cross_back(valid, kv, queries, grads, lse, delta, kv_mat, images, early, size):
     caps, slots, double = kv.shape
     width = double // 2
     length = queries.shape[1]
+    captions = caps // 2
     batch = 4 if caps % 4 == 0 else 1
+    bits = list(range(size.bit_length() - 1))
+    axes = bits[::-1]
+    up, down, cross = early
+    plan = []
+    for by in range(3):
+        for name, array in (("up", up), ("down", down)):
+            third = array.shape[-1] // 3
+            plan.append((name, by * third, third, axes, turned(bits, by), False))
+    plan.append(("cross", 0, cross.shape[-1], axes, turned(bits, 1), False))
+    heights = dict(up=up.shape[-2], down=down.shape[-2], cross=cross.shape[-2])
+    buffers = [
+        pltpu.VMEM((2,) * count + (heights[name], cols), BF16)
+        for name, _, cols, _, order, _ in plan
+        for count in range(len(order) - 1, -1, -1)
+    ]
     block = lambda *shape: pl.BlockSpec((1,) + shape, lambda i, *_: (i, 0, 0))
+    once = lambda shape: pl.BlockSpec(shape, lambda *_: (0,) * len(shape), pipeline_mode=pl.Buffered(1))
     sds = jax.ShapeDtypeStruct
+    sems = pltpu.SemaphoreType.DMA((len(buffers),))
+    back_sems = pltpu.SemaphoreType.DMA((captions,))
+    swapped = pltpu.VMEM((captions, length, width), BF16)
+    outs = [sds(v.shape[-2:], F32) for v in early]
     return pl.pallas_call(
-        functools.partial(cross_back_body, short=short),
+        functools.partial(cross_back_body, plan=plan, bits=bits),
         grid_spec=pltpu.PrefetchScalarGridSpec(
-            num_scalar_prefetch=2,
+            num_scalar_prefetch=1,
             grid=(caps,),
             in_specs=[
                 block(slots, double), block(length, width), block(length, width),
-                block(GROUPS, LANES), block(GROUPS, LANES), whole(kv_mat.shape),
+                block(GROUPS, LANES), block(GROUPS, LANES), once(kv_mat.shape),
                 pl.BlockSpec((batch, slots, width), lambda i, *_: (i // batch, 0, 0)),
+                once(up.shape), once(down.shape), once(cross.shape),
             ],
             out_specs=[
-                block(length, width), block(slots, width), whole((width, width)), whole((width, width)),
-            ],
+                whole((captions, length, width)), block(slots, width), whole((width, width)),
+                whole((width, width)),
+            ] + [whole(v.shape) for v in outs],
             scratch_shapes=[
-                pltpu.VMEM((batch, slots, double), BF16), pltpu.VMEM((width, double), F32),
-            ],
+                sems, sems, back_sems, back_sems,
+                pltpu.VMEM((batch, slots, double), BF16), pltpu.VMEM((width, double), F32), swapped, swapped,
+            ] + buffers,
         ),
         out_shape=[
-            sds((caps, length, width), BF16), sds((caps, slots, width), BF16),
+            sds((captions, length, width), BF16), sds((caps, slots, width), BF16),
             sds((width, width), BF16), sds((width, width), BF16),
-        ],
-        compiler_params=pltpu.CompilerParams(vmem_limit_bytes=VMEM_LIMIT),
+        ] + outs,
+        compiler_params=pltpu.CompilerParams(
+            vmem_limit_bytes=VMEM_MOST, collective_id=2, has_side_effects=True
+        ),
         name="cross_back",
-    )(valid, side, kv, queries, grads, lse, delta, kv_mat, images)
+    )(valid, kv, queries, grads, lse, delta, kv_mat, images, up, down, cross)
 
 
 def add_low(first, second):
     return (first.astype(F32) + second.astype(F32)).astype(BF16)
+
+
+def cut_blocks(target, value):
+    height = target.shape[-2]
+    count = len(target.shape) - 2
+    if height % 16 == 0:
+        target[...] = value.astype(BF16).reshape(target.shape)
+    else:
+        for i in range(1 << count):
+            lead = tuple((i >> (count - 1 - d)) % 2 for d in range(count))
+            target[lead] = value[i * height : (i + 1) * height].astype(BF16)
 
 
 class Piece:
@@ -598,18 +643,23 @@
 
     def start_kv(self):
         whole_lead = (slice(None),) * len(self.bits)
-        self.pending = self.sums.copy(
-            self.send.at[whole_lead + self.columns(self.send)], self.kv_recv, {"kv": 1 - self.sums.side}
+        index = self.sums.take_index()
+        self.pending = lambda: self.sums.copy(
+            index, self.send.at[whole_lead + self.columns(self.send)], self.kv_recv,
+            {"kv": 1 - self.sums.side},
         )
-        self.pending.start()
+        self.pending().start()
 
     def start(self):
-        bit = self.order[self.now]
-        lead = tuple(1 - self.sums.own(bit) if b == bit else slice(None) for b in self.bits)
-        self.pending = self.sums.copy(
-            self.holds.at[lead + self.columns(self.holds)], self.recvs[self.now], self.sums.partner(bit)
-        )
-        self.pending.start()
+        bit, bits, holds, arrives = self.order[self.now], self.bits, self.holds, self.recvs[self.now]
+        index = self.sums.take_index()
+
+        def make():
+            lead = tuple(1 - self.sums.own(bit) if b == bit else slice(None) for b in bits)
+            return self.sums.copy(index, holds.at[lead + self.columns(holds)], arrives, self.sums.partner(bit))
+
+        self.pending = make
+        make().start()
 
     def add(self, kept, arrived, cols, left, fixed):
         def one(i, carry):
@@ -624,7 +674,7 @@
     def advance(self):
         if self.pending is None:
             return True
-        self.pending.wait()
+        self.pending().wait()
         self.pending = None
         if self.holds is None:
             self.add(self.mine, self.kv_recv, self.columns(self.mine), self.bits, {})
@@ -655,9 +705,11 @@
     def partner(self, bit):
         return {"dp": self.me + (1 - 2 * self.own(bit)) * (1 << bit)}
 
-    def copy(self, src, dst, device):
-        index = self.count
+    def take_index(self):
         self.count += 1
+        return self.count - 1
+
+    def copy(self, index, src, dst, device):
         return pltpu.make_async_remote_copy(
             src_ref=src, dst_ref=dst, send_sem=self.send_sem.at[index], recv_sem=self.recv_sem.at[index],
             device_id=device, device_id_type=pl.DeviceIdType.MESH,
@@ -679,46 +731,40 @@
 def end_body(
     back_hbm, hidden_hbm, grad_two_hbm, att_hbm, qkv_hbm, tok_hbm, qkv_mat_hbm, out_mat_hbm, query_mat_hbm,
     gain_one, shift_one, gain_two, shift_two, gain_three, shift_three,
-    up_keep, up_first, up_second, up_both, down_keep, down_away, cross_ref, kv_mine, kv_send,
-    grad_tok, up_out, down_out, cross_out, qkv_out, out_out, query_out, kv_out, gains_out,
+    kv_mine, kv_send, grad_tok, qkv_out, out_out, query_out, kv_out, gains_out,
     *scratch, plan, bits, length, tile
 ):
     scratch = list(scratch)
     (
-        send_sem, recv_sem, load_sem, back_one, back_two, hidden, grad_two, att, qkv, tok, qkv_mat,
-        out_mat, query_mat, back_sum, normed, low, grad_att, grad_qkv, acc, gains_all, gain_kv,
+        send_sem, recv_sem, load_sem, back_sum, hidden, grad_two, att, qkv, tok, qkv_mat,
+        out_mat, query_mat, normed, low, grad_att, grad_qkv, gains_all, gain_kv,
         gain_buf, gain_recv, qkv_mine, qkv_send, out_mine, out_send, query_mine, query_send,
-        up_ref, down_ref,
-    ) = scratch[:31]
-    rest = scratch[31:]
+    ) = scratch[:26]
+    rest = scratch[26:]
     sums = Sums(send_sem, recv_sem)
     side = sums.side
-    captions = back_one.shape[0]
     rows, width = hidden.shape
+    captions = rows // length
     half = width // 2
     named = dict(
-        up=(up_ref, None, None, up_out), down=(down_ref, None, None, down_out),
-        cross=(cross_ref, None, None, cross_out), qkv=(None, qkv_mine, qkv_send, qkv_out),
+        qkv=(None, qkv_mine, qkv_send, qkv_out),
         out=(None, out_mine, out_send, out_out), query=(None, query_mine, query_send, query_out),
         kv=(None, kv_mine, kv_send, kv_out),
     )
     pieces = {}
     for name, col, cols, axes, order, kv in plan:
         source, mine, send, out = named[name]
-        kv_recv = rest.pop(0) if kv else None
+        kv_recv = rest.pop(0)
         recvs = [rest.pop(0) for _ in order]
         pieces.setdefault(name, []).append(
             Piece(sums, source, out, col, cols, axes, order, recvs, mine, send, kv_recv)
         )
-    early = pieces["up"] + pieces["down"] + pieces["cross"]
     image = pieces["kv"]
     middle = pieces["query"] + pieces["out"]
     late = pieces["qkv"]
 
-    own_caps = pl.ds(pl.multiple_of(side * captions, captions), captions)
-    other_caps = pl.ds(pl.multiple_of((1 - side) * captions, captions), captions)
     pairs = [
-        (back_hbm.at[own_caps], back_one), (hidden_hbm, hidden), (query_mat_hbm, query_mat),
+        (back_hbm, back_sum), (hidden_hbm, hidden), (query_mat_hbm, query_mat),
         (grad_two_hbm, grad_two), (out_mat_hbm, out_mat), (att_hbm, att), (qkv_hbm, qkv),
         (tok_hbm, tok), (qkv_mat_hbm, qkv_mat),
     ]
@@ -726,43 +772,20 @@
     for load in loads:
         load.start()
     sums.greet(bits)
-    swap = sums.copy(back_hbm.at[other_caps], back_two, {"kv": 1 - side})
-    swap.start()
     for piece in image:
         piece.start_kv()
-
-    def sum_terms(target, terms):
-        count = len(target.shape) - 2
-
-        def one(i, carry):
-            lead = tuple((i // (1 << (count - 1 - d))) % 2 for d in range(count))
-            total = terms[0][lead].astype(F32)
-            for term in terms[1:]:
-                total += term[lead].astype(F32)
-            target[lead] = total.astype(BF16)
-            return carry
-
-        lax.fori_loop(0, 1 << count, one, 0)
-
-    sum_terms(up_ref, (up_keep, up_first, up_second, up_both))
-    sum_terms(down_ref, (down_keep, down_away))
-    for piece in early:
-        piece.start()
     gains_all[...] = jnp.zeros_like(gains_all)
     gains_all[4:5] = gain_three[...]
     gains_all[5:6] = shift_three[...]
     for load in loads[:5]:
         load.wait()
-    swap.wait()
 
     def rows_at(index):
         return pl.ds(pl.multiple_of(index * tile, tile), tile)
 
     def query_back(index, carry):
         span = rows_at(index)
-        caps = pl.ds(index * (tile // length), tile // length)
-        back = add_low(back_one[caps], back_two[caps]).reshape(tile, width)
-        back_sum[span, :] = back
+        back = back_sum[span, :]
         unit, inverse = normalize(hidden[span, :])
         normed[span, :] = (unit * as_row(gain_two) + as_row(shift_two)).astype(BF16)
         grad = dot_nt(back, query_mat[...])
@@ -780,21 +803,8 @@
 
     def weight(left, right, target, which):
         cols = target.shape[-1]
-        block = target.shape[-2]
         start = pl.multiple_of(which * cols, 128)
-        acc[:, :cols] = dot_tn(left[...], right[:, pl.ds(start, cols)])
-
-        def one(i, carry):
-            lead = tuple((i // (1 << (len(bits) - 1 - d))) % 2 for d in range(len(bits)))
-            span = pl.ds(i * block, block) if isinstance(i, int) else pl.ds(pl.multiple_of(i * block, 8), block)
-            target[lead] = acc[span, :cols].astype(BF16)
-            return carry
-
-        if block % 8 == 0:
-            lax.fori_loop(0, 1 << len(bits), one, 0)
-        else:
-            for i in range(1 << len(bits)):
-                one(i, 0)
+        cut_blocks(target, dot_tn(left[...], right[:, pl.ds(start, cols)]))
 
     def weights(left, right, mine, send, group):
         weight(left, right, send, 1 - side)
@@ -806,14 +816,14 @@
     loads[5].wait()
     loads[6].wait()
     weights(att, low, out_mine, out_send, pieces["out"])
-    for piece in middle:
+    for piece in image + middle:
         piece.advance()
 
     mask = same_head()
     causal = causal_mask(length)
 
-    def attend(cap, carry):
-        span = pl.ds(pl.multiple_of(cap * length, length), length)
+    def attend(cap):
+        span = pl.ds(cap * length, length)
         for group in range(GROUPS):
             lo = group * LANES
             query = spread(qkv[span, lo : lo + LANES] * SCALE, mask)
@@ -832,12 +842,12 @@
             grad_qkv[span, 2 * width + lo : 2 * width + lo + LANES] = dot(
                 probs.astype(BF16), cot
             ).astype(BF16)
-        return carry
-
-    lax.fori_loop(0, captions // 2, attend, 0)
-    lax.fori_loop(captions // 2, captions, attend, 0)
-    for piece in early:
-        piece.advance()
+
+    for first_cap in range(0, captions, 4):
+        for cap in range(first_cap, min(first_cap + 4, captions)):
+            attend(cap)
+        for piece in middle + image:
+            piece.advance()
     loads[7].wait()
     loads[8].wait()
 
@@ -849,7 +859,7 @@
 
     lax.fori_loop(0, rows // tile, token_norm, 0)
     weights(normed, grad_qkv, qkv_mine, qkv_send, late)
-    for piece in late + image:
+    for piece in late + middle + image:
         piece.advance()
 
     def token_back(index, carry):
@@ -865,10 +875,10 @@
     lax.fori_loop(0, rows // tile, token_back, 0)
     own_cols = pl.ds(pl.multiple_of(side * half, 128), half)
     other_cols = pl.ds(pl.multiple_of((1 - side) * half, 128), half)
-    gain_copy = sums.copy(gains_all.at[:, other_cols], gain_kv, {"kv": 1 - side})
+    gain_copy = sums.copy(sums.take_index(), gains_all.at[:, other_cols], gain_kv, {"kv": 1 - side})
     gain_copy.start()
     stage = -1
-    everything = early + image + middle + late
+    everything = late + image + middle
     while stage < len(bits) or not all(piece.pending is None for piece in everything):
         if stage < len(bits):
             gain_copy.wait()
@@ -878,7 +888,9 @@
                 gain_buf[stage + 1] = gain_buf[stage] + gain_recv[stage]
             stage += 1
             if stage < len(bits):
-                gain_copy = sums.copy(gain_buf.at[stage], gain_recv.at[stage], sums.partner(bits[stage]))
+                gain_copy = sums.copy(
+                    sums.take_index(), gain_buf.at[stage], gain_recv.at[stage], sums.partner(bits[stage])
+                )
                 gain_copy.start()
             else:
                 gains_out[...] = gain_buf[stage]
@@ -888,7 +900,7 @@
 
 def end(
     back, hidden, grad_two, att, qkv, tokens, qkv_mat, out_mat, query_mat, gain_one, shift_one,
-    gain_two, shift_two, gain_three, shift_three, early, kv_mine, kv_send, length, size
+    gain_two, shift_two, gain_three, shift_three, kv_mine, kv_send, length, size
 ):
     bits = list(range(size.bit_length() - 1))
     axes = bits[::-1]
@@ -897,56 +909,48 @@
     tile = min(256, rows)
     block = width // size
     lead = (2,) * len(bits)
-    up_terms, down_terms, cross = early
-    up, down = up_terms[0], down_terms[0]
-    cut_down = down.shape[-1] // 384 * 256
     third = width // 3
-    plan = [("up", 0, up.shape[-1], axes[:-2], bits[2:], False)]
-    down_axes = axes[:1] + axes[2:]
-    for col, cols, by in ((0, cut_down, 0), (cut_down, down.shape[-1] - cut_down, 1)):
-        order = [b for b in turned(bits, by) if b in down_axes]
-        plan.append(("down", col, cols, down_axes, order, False))
-    plan.append(("cross", 0, cross.shape[-1], axes, turned(bits, 2), False))
+    plan = []
     plan.append(("query", 0, width // 2, axes, turned(bits, 0), True))
     plan.append(("out", 0, width // 2, axes, turned(bits, 1), True))
     for by in range(3):
         plan.append(("kv", by * third, third, axes, turned(bits, by), True))
-        plan.append(("qkv", by * (width // 2), width // 2, axes, turned(bits, by), True))
-    heights = dict(up=up.shape[-2], down=down.shape[-2], cross=cross.shape[-2])
+    col = 0
+    for cols in (width // 3, width // 6):
+        for by in range(3):
+            plan.append(("qkv", col, cols, axes, turned(bits, by), True))
+            col += cols
     buffers = []
     copies = 2 + len(bits)
     for name, col, cols, piece_axes, order, kv in plan:
-        shape = (heights.get(name, block), cols)
-        for count in range(len(order) if kv else len(order) - 1, -1, -1):
-            buffers.append(pltpu.VMEM((2,) * count + shape, BF16))
+        for count in range(len(order), -1, -1):
+            buffers.append(pltpu.VMEM((2,) * count + (block, cols), BF16))
             copies += 1
     vmem = pl.BlockSpec(memory_space=pltpu.VMEM)
     hbm = pl.BlockSpec(memory_space=pl.ANY)
     sds = jax.ShapeDtypeStruct
     cut = lambda cols: pltpu.VMEM(lead + (block, cols), BF16)
     outs = [sds((rows, width), BF16)]
-    outs += [sds(v.shape[-2:], F32) for v in (up, down, cross)]
     outs += [sds((block, cols), F32) for cols in (3 * width // 2, width // 2, width // 2, width)]
     outs += [sds((8, width // 2), F32)]
     low_rows = lambda cols: pltpu.VMEM((rows, cols), BF16)
     return pl.pallas_call(
         functools.partial(end_body, plan=plan, bits=bits, length=length, tile=tile),
-        in_specs=[hbm] * 9 + [vmem] * 6 + [vmem] * 8 + [hbm],
+        in_specs=[hbm] * 9 + [vmem] * 7 + [hbm],
         out_specs=[vmem] * len(outs),
         out_shape=outs,
         scratch_shapes=[
             pltpu.SemaphoreType.DMA((copies,)), pltpu.SemaphoreType.DMA((copies,)),
             pltpu.SemaphoreType.DMA((9,)),
-            pltpu.VMEM((captions, length, width), BF16), pltpu.VMEM((captions, length, width), BF16),
-            pltpu.VMEM((rows, width), F32), pltpu.VMEM((rows, width), F32), low_rows(width),
+            low_rows(width), pltpu.VMEM((rows, width), F32), pltpu.VMEM((rows, width), F32), low_rows(width),
             low_rows(3 * width), low_rows(width), pltpu.VMEM(qkv_mat.shape, BF16),
             pltpu.VMEM(out_mat.shape, BF16), pltpu.VMEM(query_mat.shape, BF16),
-            low_rows(width), low_rows(width), low_rows(width), low_rows(width), low_rows(3 * width),
-            pltpu.VMEM((width, 3 * width // 2), F32), pltpu.VMEM((8, width), F32),
+            low_rows(width), low_rows(width), low_rows(width), low_rows(3 * width),
+            pltpu.VMEM((8, width), F32),
             pltpu.VMEM((8, width // 2), F32), pltpu.VMEM((len(bits) + 1, 8, width // 2), F32),
             pltpu.VMEM((len(bits), 8, width // 2), F32),
             cut(3 * width // 2), cut(3 * width // 2), cut(width // 2), cut(width // 2),
-            cut(width // 2), cut(width // 2), pltpu.VMEM(up.shape, BF16), pltpu.VMEM(down.shape, BF16),
+            cut(width // 2), cut(width // 2),
         ] + buffers,
         compiler_params=pltpu.CompilerParams(
             vmem_limit_bytes=VMEM_MOST, collective_id=0, has_side_effects=True
@@ -954,7 +958,7 @@
         name="end",
     )(
         back, hidden, grad_two, att, qkv, tokens, qkv_mat, out_mat, query_mat, gain_one, shift_one,
-        gain_two, shift_two, gain_three, shift_three, *up_terms, *down_terms, cross, kv_mine, kv_send,
+        gain_two, shift_two, gain_three, shift_three, kv_mine, kv_send,
     )
 
 
@@ -993,7 +997,6 @@
     side = lax.axis_index("kv")
     me = lax.axis_index("dp")
     groups = lax.axis_size("dp")
-    side_arr = side.reshape(1)
     tok = tokens.reshape(captions * length, width)
     cot = cotangent.reshape(captions * length, width)
     short = -(-SHORT // 16) * 16
@@ -1013,36 +1016,24 @@
 
     queries = both(query.reshape(captions, length, width))
     kv, part, lse_part = cross_start(valid, images, cross_kv, queries, short)
-    (
-        layer_out, grad_two, grads, lse, delta, up_keep, up_first, up_second, up_both, down_keep,
-        down_away, cross_sum, gain3, shift3,
-    ) = feed(
+    layer_out, grad_two, grads, lse, delta, up_sum, down_sum, cross_sum, gain3, shift3 = feed(
         part, lse_part, hidden, cot, cross_out, norm3_gain, norm3_shift, w_up, w_down, length, groups
     )
-    bits = groups.bit_length() - 1
-    cubes = lambda v, count: v.reshape((2,) * count + (v.shape[0] * v.shape[1] >> count, v.shape[2]))
-    up_terms = [up_keep] + [
-        exchange(away, "dp", flip, groups) for away, flip in ((up_first, 1), (up_second, 2), (up_both, 3))
-    ]
-    down_terms = [down_keep, exchange(down_away, "dp", 1 << (bits - 2), groups)]
-    early = (
-        [cubes(v, bits - 2) for v in up_terms], [cubes(v, bits - 1) for v in down_terms],
-        cubes(cross_sum, bits),
+    cut = lambda v: split_rows(v, groups)
+    early = [cut(v.reshape(-1, v.shape[-1])) for v in (up_sum, down_sum, cross_sum)]
+    stats = lambda v: v.reshape(caps, GROUPS, LANES)
+    back, images_grad, kv_mine, kv_send, w_up_grad, down_grad, cross_out_grad = cross_back(
+        valid, kv, queries, grads.reshape(caps, length, width), stats(lse), stats(delta), cross_kv,
+        images, early, groups
     )
-
-    stats = lambda v: v.reshape(caps, GROUPS, LANES)
-    back, images_grad, kv_mine, kv_send = cross_back(
-        valid, side_arr, kv, queries, grads.reshape(caps, length, width), stats(lse), stats(delta),
-        cross_kv, images, short
-    )
-    cut = lambda v: split_rows(v, groups)
     (
-        tokens_grad, w_up_grad, down_grad, cross_out_grad, self_qkv_grad, self_out_grad, cross_q_grad,
-        cross_kv_grad, gains, layer_out,
+        tokens_grad, self_qkv_grad, self_out_grad, cross_q_grad, cross_kv_grad, gains, layer_out,
+        w_up_grad, down_grad, cross_out_grad,
     ) = hand_over(*end(
-        back, hidden, grad_two, att, qkv, tok, self_qkv, self_out, cross_q, norm1_gain, norm1_shift,
-        norm2_gain, norm2_shift, gain3, shift3, early, cut(kv_mine), cut(kv_send), length, groups,
-    ), layer_out)
+        back.reshape(captions * length, width), hidden, grad_two, att, qkv, tok, self_qkv, self_out,
+        cross_q, norm1_gain, norm1_shift, norm2_gain, norm2_shift, gain3, shift3, cut(kv_mine),
+        cut(kv_send), length, groups,
+    ), layer_out, w_up_grad, down_grad, cross_out_grad)
     return (
         layer_out.reshape(captions, length, width),
         tokens_grad.reshape(captions, length, width),

time: 230 us -> 245 us (1.065)
  Pallas kernels: 215 us -> 229 us
  local copies, waits for them, and re-layouts: 1.71 us -> 7.98 us
  starting transfers between devices: 4.43 us -> 0.01 us
    pallas_call x2, Pallas kernels: 93.7 us -> 123 us  [the longest x1 84.9 us: cross_back(): pl.pallas_call(functools.partial(cross_back_body, plan=plan, bits=bits),...]
    pallas_call x1, Pallas kernels: 74.4 us -> 59.2 us  [end(): pl.pallas_call(functools.partial(end_body, plan=plan, bits=bits, length=l...]
    unnamed x2 -> x3, local copies, waits for them, and re-layouts: 0.01 us -> 6.43 us
    ppermute x5 -> x1, starting transfers between devices: 4.43 us -> 0.01 us  [exchange(): return lax.ppermute(value, axis, [(i, i ^ bit) for i in range(size)])]
  transfers between devices with their start and end apart: 5 -> 1, of which waited for: 1 -> 1; matrix products, arithmetic and copies ran while one was open for 0% -> 0% of each run, Pallas kernels for 24% -> 0%
where the time goes in v5:
time: 245 us; the launch traced here: 243 us
  Pallas kernels  229 us (93%)
  local copies, waits for them, and re-layouts  7.98 us (3%)
  other arithmetic  3.13 us (1%)
    pallas_call x1, Pallas kernels, cross_back(): pl.pallas_call(functools.partial(cross_back_body, plan=plan, bits=bits),...  84.9 us
    pallas_call x1, Pallas kernels, end(): pl.pallas_call(functools.partial(end_body, plan=plan, bits=bits, length=l...  59.2 us
    pallas_call x1, Pallas kernels, feed(): pl.pallas_call(functools.partial(feed_body, length=length, tile=tile, ste...  38.4 us
    pallas_call x1, Pallas kernels, cross_start(): pl.pallas_call(functools.partial(cross_start_body, short=short), grid_spe...  30.5 us
    pallas_call x1, Pallas kernels, token_start(): pl.pallas_call(functools.partial(token_start_body, length=length), grid=(...  12.5 us
    unnamed x3, local copies, waits for them, and re-layouts  6.43 us
  transfers between devices with their start and end apart: 1, of which 1 were waited for; matrix products, arithmetic and copies ran while one was open for 0% of the time, Pallas kernels for 0%

profile of v5, /device:TPU:2, one launch (start us, length us, event | category | flops | bytes accessed | tf_op | source)
XLA Modules:
  0.0 242.7 jit_solution(3320042759808102600)
XLA Ops:
  0.6 0.0 copy-start
  0.7 12.5 %token_start.1 = (bf16[512,2304]{1,0:T(8,128)(2,1)}, bf16[512,768]{1,0:T(8,128)(2,1)}, f32[512,768]{1,0:T(8,128)}, bf16[512,768]{1,0:T(8,128)(2,1)}) custom-call(bf16[512,768]{1,0:T(8,128)(2,1)} %bitcast.18, f32[768]{0:T(1024)} %gain_one.3, f32[768]{0:T(1024)} %shift_one.3, bf16[768,2304]{1,0:T(8,128)(2,1)} %qkv_mat_hbm.1, bf16[768,768]{1,0:T(8,128)(2,1)} %out_mat_hbm.1, ...), custom_call_target="tpu_custom_call" | custom-call | tf_op jit(solution)/shard_map/token_start/pallas_call | solution.py:144
  13.2 0.0 collective-permute-start
  13.2 0.0 copy-done
  13.2 0.5 subtract_clamp_fusion.valid_ref
  13.7 2.0 collective-permute-done
  15.7 1.2 broadcast_select_fusion.1
  16.9 1.4 pad_maximum_fusion.query_ref
  18.3 30.5 %cross_start.1 = (bf16[16,288,1536]{2,1,0:T(8,128)(2,1)}, bf16[16,64,768]{2,1,0:T(8,128)(2,1)}, f32[16,3,256]{2,1,0:T(4,128)}) custom-call(s32[16]{0:T(128)} %subtract_clamp_fusion.valid_ref, bf16[16,288,768]{2,1,0:T(8,128)(2,1)} %img_ref.3, bf16[768,1536]{1,0:T(8,128)(2,1)} %kv_mat.3, bf16[16,64,768]{2,1,0:T(8,128)(2,1)} %pad_maximum_fusion.query_ref), custom_call_target="tpu_custom_call" | custom-call | tf_op jit(solution)/shard_map/cross_start/pallas_call | solution.py:202
  48.8 38.4 %feed.1 = (bf16[512,768]{1,0:T(8,128)(2,1)}, f32[512,768]{1,0:T(8,128)}, bf16[2,512,768]{2,1,0:T(8,128)(2,1)}, f32[2,8,3,256]{3,2,1,0:T(4,128)}, f32[2,8,3,256]{...) custom-call(bf16[2,512,768]{2,1,0:T(8,128)(2,1)} %bitcast.23, ...), custom_call_target="tpu_custom_call" | custom-call | tf_op jit(solution)/shard_map/feed/pallas_call | solution.py:421
  87.2 84.9 %cross_back.1 = (bf16[8,64,768]{2,1,0:T(8,128)(2,1)}, bf16[16,288,768]{2,1,0:T(8,128)(2,1)}, bf16[768,768]{1,0:T(8,128)(2,1)}, bf16[768,768]{1,0:T(8,128)(2,1)},...) custom-call(s32[16]{0:T(128)} %subtract_clamp_fusion.valid_ref, ...), custom_call_target="tpu_custom_call" | custom-call | tf_op jit(solution)/shard_map/cross_back/pallas_call | solution.py:588
  172.1 59.2 %end.1 = (bf16[512,768]{1,0:T(8,128)(2,1)}, f32[48,1152]{1,0:T(8,128)}, f32[48,384]{1,0:T(8,128)}, f32[48,384]{1,0:T(8,128)}, f32[48,768]{1,0:T(8,128)}, /*index=5*/f32[8,384]{1,0:T(8,128)}) custom-call(bf16[512,768]{1,0:T(8,128)(2,1)} %bitcast.27, f32[512,768]{1,0:T(8,128)} %get-tuple-element.60.hidden_ref.hidden_hbm, ...), custom_call_target="tpu_custom_call" | custom-call | tf_op jit(solution)/shard_map/end/pallas_call | solution.py:937
  231.4 3.3 %hand_over.1 = (bf16[512,768]{1,0:T(8,128)(2,1)}, f32[48,1152]{1,0:T(8,128)}, f32[48,384]{1,0:T(8,128)}, f32[48,384]{1,0:T(8,128)}, f32[48,768]{1,0:T(8,128)}, /...) custom-call(bf16[512,768]{1,0:T(8,128)(2,1)} %get-tuple-element.75.r, ...), custom_call_target="tpu_custom_call" | custom-call | tf_op jit(solution)/shard_map/hand_over/pallas_call | solution.py:973
  234.7 1.6 slice_reduce_fusion
  236.2 6.4 %copy.34 = bf16[16,288,768]{2,1,0:T(8,128)(2,1)} copy(bf16[16,288,768]{2,1,0:T(8,128)(2,1)} %get-tuple-element.122) | data formatting | bytes 14155776
Async XLA Ops:
  0.6 12.6 %copy-start = (s32[16]{0:T(128)S(1)}, s32[16]{0:T(128)}, u32[]{:S(2)}) copy-start(s32[16]{0:T(128)} %param.19) | copy-start | bytes 196
  13.2 2.5 %collective-permute-start = (bf16[8,64,768]{2,1,0:T(8,128)(2,1)}, bf16[8,64,768]{2,1,0:T(8,128)(2,1)S(1)}, u32[]{:S(2)}, u32[]{:S(2)}) collective-permute-start(bf16[8,64,768]{2,1,0:T(8,128)(2,1)} %bitcast.28), channel_id=1, source_target_pairs={{0,1},{1,0},{2,3},{3,2},{4,5},{5,4},{6,7},{7,6},{8,9},{9,8},{10,11... | collective-permute-start | bytes 2359304 | tf_op jit(solution)/shard_map/ppermute | solution.py:983

commit v6 on v4

--- a/solution.py
+++ b/solution.py
@@ -104,8 +104,29 @@
 
 def token_start_body(
     tok_ref, gain_one, shift_one, qkv_mat, out_mat, gain_two, shift_two, query_mat,
-    qkv_ref, att_ref, hidden_ref, query_ref, *, length
+    qkv_ref, att_ref, hidden_ref, queries_hbm, send_sem, recv_sem, store_sem, held, *, length
 ):
+    step = pl.program_id(0)
+    side = lax.axis_index("kv")
+    tiles, tile, _ = held.shape
+
+    def copies(index):
+        into = queries_hbm.at[side, pl.ds(pl.multiple_of(index * tile, tile), tile)]
+        return (
+            pltpu.make_async_copy(held.at[index], into, store_sem.at[index]),
+            pltpu.make_async_remote_copy(
+                src_ref=held.at[index], dst_ref=into, send_sem=send_sem.at[index],
+                recv_sem=recv_sem.at[index], device_id={"kv": 1 - side},
+                device_id_type=pl.DeviceIdType.MESH,
+            ),
+        )
+
+    @pl.when(step == 0)
+    def _():
+        barrier = pltpu.get_barrier_semaphore()
+        pl.semaphore_signal(barrier, inc=1, device_id={"kv": 1 - side}, device_id_type=pl.DeviceIdType.MESH)
+        pl.semaphore_wait(barrier, 1)
+
     x = tok_ref[...].astype(F32)
     unit, _ = normalize(x)
     normed = (unit * as_row(gain_one) + as_row(shift_one)).astype(BF16)
@@ -129,7 +150,15 @@
     hidden_ref[...] = hidden
     unit, _ = normalize(hidden)
     normed = (unit * as_row(gain_two) + as_row(shift_two)).astype(BF16)
-    query_ref[...] = (dot(normed, query_mat[...]).astype(BF16).astype(F32) * SCALE).astype(BF16)
+    held[step] = (dot(normed, query_mat[...]).astype(BF16).astype(F32) * SCALE).astype(BF16)
+    for copy in copies(step):
+        copy.start()
+
+    @pl.when(step == tiles - 1)
+    def _():
+        for index in range(tiles):
+            for copy in copies(index):
+                copy.wait()
 
 
 def whole(shape):
@@ -148,62 +177,87 @@
             row_block(width), whole((width,)), whole((width,)), whole(qkv_mat.shape),
             whole(out_mat.shape), whole((width,)), whole((width,)), whole(query_mat.shape),
         ],
-        out_specs=[row_block(3 * width), row_block(width), row_block(width), row_block(width)],
+        out_specs=[
+            row_block(3 * width), row_block(width), row_block(width), pl.BlockSpec(memory_space=pl.ANY),
+        ],
         out_shape=[
             jax.ShapeDtypeStruct((rows, 3 * width), BF16),
             jax.ShapeDtypeStruct((rows, width), BF16),
             jax.ShapeDtypeStruct((rows, width), F32),
-            jax.ShapeDtypeStruct((rows, width), BF16),
+            jax.ShapeDtypeStruct((2, rows, width), BF16),
         ],
-        compiler_params=pltpu.CompilerParams(vmem_limit_bytes=VMEM_LIMIT),
+        scratch_shapes=[pltpu.SemaphoreType.DMA((rows // tile,))] * 3
+        + [pltpu.VMEM((rows // tile, tile, width), BF16)],
+        compiler_params=pltpu.CompilerParams(
+            vmem_limit_bytes=VMEM_LIMIT, collective_id=2, has_side_effects=True
+        ),
         name="token_start",
     )(tokens, gain_one, shift_one, qkv_mat, out_mat, gain_two, shift_two, query_mat)
 
 
+def most(values):
+    return functools.reduce(jnp.maximum, values)
+
+
 def cross_start_body(valid_ref, img_ref, kv_mat, query_ref, kv_ref, att_ref, lse_ref, *, short):
-    cap = pl.program_id(0)
-    valid = valid_ref[cap]
+    batch, slots, _ = img_ref.shape
     width = query_ref.shape[2]
-    slots = img_ref.shape[1]
+    valids = [valid_ref[pl.program_id(0) * batch + cap] for cap in range(batch)]
+    longest = most(valids)
 
     def work(count):
-        kv_ref[0, :count] = dot(img_ref[0, :count], kv_mat[...]).astype(BF16)
         mask = same_head()
-        inside = iota((count, LANES), 0) < valid
-        for group in range(GROUPS):
+        row = iota((count, LANES), 0)
+        units = [(cap, group) for cap in range(batch) for group in range(GROUPS)]
+
+        def project(unit, first):
+            cap, group = unit
+            lo = first + group * LANES
+            columns = dot(img_ref[cap, :count], kv_mat[:, lo : lo + LANES]).astype(BF16)
+            kv_ref[cap, :count, lo : lo + LANES] = columns
+            return columns
+
+        key, value = project(units[0], 0), project(units[0], width)
+        for unit, later in zip(units, units[1:] + [None]):
+            cap, group = unit
             lo = group * LANES
-            key = kv_ref[0, :count, lo : lo + LANES]
-            value = kv_ref[0, :count, width + lo : width + lo + LANES]
-            scores = dot_nt(key, spread(query_ref[0, :, lo : lo + LANES], mask))
+            inside = row < valids[cap]
+            scores = dot_nt(key, spread(query_ref[cap, :, lo : lo + LANES], mask))
+            if later:
+                key = project(later, 0)
             scores = jnp.where(inside, scores, NEG)
             peak = jnp.max(scores, axis=0, keepdims=True)
             exponent = jnp.where(inside, jnp.exp(scores - peak), 0.0)
-            total = jnp.sum(exponent, axis=0, keepdims=True)
+            total = jnp.maximum(jnp.sum(exponent, axis=0, keepdims=True), 1.0)
+            held = value
+            if later:
+                value = project(later, width)
             probs = (exponent * (1.0 / total)).astype(BF16)
-            att_ref[0, :, lo : lo + LANES] = gather_heads(dot_tn(probs, value)).astype(BF16)
-            lse_ref[0, group : group + 1] = peak + jnp.log(total)
-
-    @pl.when(valid <= 0)
+            att_ref[cap, :, lo : lo + LANES] = gather_heads(dot_tn(probs, held)).astype(BF16)
+            lse_ref[cap, group : group + 1] = peak + jnp.log(total)
+
+    @pl.when(longest <= 0)
     def _():
         att_ref[...] = jnp.zeros_like(att_ref)
         lse_ref[...] = jnp.full_like(lse_ref, NEG)
 
-    if short < slots:
-        pl.when((valid > 0) & (valid <= short))(lambda: work(short))
-        pl.when(valid > short)(lambda: work(slots))
+    if short < slots and batch <= 2:
+        pl.when((longest > 0) & (longest <= short))(lambda: work(short))
+        pl.when(longest > short)(lambda: work(slots))
     else:
-        pl.when(valid > 0)(lambda: work(slots))
+        pl.when(longest > 0)(lambda: work(slots))
 
 
 def cross_start(valid, images, kv_mat, queries, short):
     caps, slots, width = images.shape
     length = queries.shape[1]
-    block = lambda *shape: pl.BlockSpec((1,) + shape, lambda i, *_: (i, 0, 0))
+    batch = 4 if caps % 4 == 0 else 1
+    block = lambda *shape: pl.BlockSpec((batch,) + shape, lambda i, *_: (i, 0, 0))
     return pl.pallas_call(
         functools.partial(cross_start_body, short=short),
         grid_spec=pltpu.PrefetchScalarGridSpec(
             num_scalar_prefetch=1,
-            grid=(caps,),
+            grid=(caps // batch,),
             in_specs=[block(slots, width), whole(kv_mat.shape), block(length, width)],
             out_specs=[block(slots, 2 * width), block(length, width), block(GROUPS, LANES)],
         ),
@@ -487,60 +541,75 @@
     valid_ref, side_ref, kv_ref, query_ref, grad_ref, lse_ref, delta_ref, kv_mat, img_ref,
     grad_query_ref, grad_img_ref, mine_ref, send_ref, grad_kv_ref, acc_ref, *, short
 ):
-    cap = pl.program_id(0)
-    valid = valid_ref[cap]
+    step = pl.program_id(0)
+    batch, slots, _ = kv_ref.shape
     width = query_ref.shape[2]
-    slots = kv_ref.shape[1]
-    batch = img_ref.shape[0]
-    place = cap % batch
-
-    @pl.when(cap == 0)
+    held = img_ref.shape[0]
+    base = step % (held // batch) * batch
+    valids = [valid_ref[step * batch + cap] for cap in range(batch)]
+    longest = most(valids)
+
+    @pl.when(step == 0)
     def _():
         acc_ref[...] = jnp.zeros_like(acc_ref)
 
     def work(count):
         mask = same_head()
-        inside = iota((count, LANES), 0) < valid
+        row = iota((count, LANES), 0)
+
+        def image_back(cap, part):
+            place = base + cap if held > batch else cap
+            lo = part * LANES
+            columns = dot_nt(grad_kv_ref[place, :count], kv_mat[lo : lo + LANES, :])
+            grad_img_ref[cap, :count, lo : lo + LANES] = columns.astype(BF16)
+
+        for cap, valid in enumerate(valids):
+            place = base + cap if held > batch else cap
+            inside = row < valid
+            for group in range(GROUPS):
+                lo = group * LANES
+                key = kv_ref[cap, :count, lo : lo + LANES]
+                value = kv_ref[cap, :count, width + lo : width + lo + LANES]
+                query = spread(query_ref[cap, :, lo : lo + LANES], mask)
+                grad = spread(grad_ref[cap, :, lo : lo + LANES], mask)
+                scores = dot_nt(key, query)
+                probs = jnp.where(inside, jnp.exp(scores - lse_ref[cap, group : group + 1]), 0.0)
+                grad_probs = dot_nt(value, grad)
+                if cap > 0:
+                    image_back(cap - 1, group)
+                grad_scores = (probs * (grad_probs - delta_ref[cap, group : group + 1])).astype(BF16)
+                back = gather_heads(dot_tn(grad_scores, key)) * SCALE
+                grad_query_ref[cap, :, lo : lo + LANES] = back.astype(BF16)
+                grad_kv_ref[place, :count, lo : lo + LANES] = dot(grad_scores, query).astype(BF16)
+                grad_kv_ref[place, :count, width + lo : width + lo + LANES] = dot(
+                    probs.astype(BF16), grad
+                ).astype(BF16)
+            if count < slots:
+                grad_kv_ref[place, count:] = jnp.zeros((slots - count, 2 * width), BF16)
+                grad_img_ref[cap, count:] = jnp.zeros((slots - count, width), BF16)
         for group in range(GROUPS):
-            lo = group * LANES
-            key = kv_ref[0, :count, lo : lo + LANES]
-            value = kv_ref[0, :count, width + lo : width + lo + LANES]
-            query = spread(query_ref[0, :, lo : lo + LANES], mask)
-            grad = spread(grad_ref[0, :, lo : lo + LANES], mask)
-            scores = dot_nt(key, query)
-            probs = jnp.where(inside, jnp.exp(scores - lse_ref[0, group : group + 1]), 0.0)
-            grad_probs = dot_nt(value, grad)
-            grad_scores = (probs * (grad_probs - delta_ref[0, group : group + 1])).astype(BF16)
-            back = gather_heads(dot_tn(grad_scores, key)) * SCALE
-            grad_query_ref[0, :, lo : lo + LANES] = back.astype(BF16)
-            grad_kv_ref[place, :count, lo : lo + LANES] = dot(grad_scores, query).astype(BF16)
-            grad_kv_ref[place, :count, width + lo : width + lo + LANES] = dot(
-                probs.astype(BF16), grad
-            ).astype(BF16)
-        grad_img_ref[0, :count] = dot_nt(grad_kv_ref[place, :count], kv_mat[...]).astype(BF16)
-        if count < slots:
-            grad_kv_ref[place, count:] = jnp.zeros((slots - count, 2 * width), BF16)
-            grad_img_ref[0, count:] = jnp.zeros((slots - count, width), BF16)
-
-    @pl.when(valid <= 0)
+            image_back(batch - 1, group)
+
+    @pl.when(longest <= 0)
     def _():
         grad_query_ref[...] = jnp.zeros_like(grad_query_ref)
-        grad_kv_ref[place] = jnp.zeros((slots, 2 * width), BF16)
+        for cap in range(batch):
+            grad_kv_ref[base + cap] = jnp.zeros((slots, 2 * width), BF16)
         grad_img_ref[...] = jnp.zeros_like(grad_img_ref)
 
-    if short < slots:
-        pl.when((valid > 0) & (valid <= short))(lambda: work(short))
-        pl.when(valid > short)(lambda: work(slots))
+    if short < slots and batch <= 2:
+        pl.when((longest > 0) & (longest <= short))(lambda: work(short))
+        pl.when(longest > short)(lambda: work(slots))
     else:
-        pl.when(valid > 0)(lambda: work(slots))
-
-    @pl.when(place == batch - 1)
+        pl.when(longest > 0)(lambda: work(slots))
+
+    @pl.when(base == held - batch)
     def _():
-        left = img_ref[...].reshape(batch * slots, width)
-        right = grad_kv_ref[...].reshape(batch * slots, 2 * width)
+        left = img_ref[...].reshape(held * slots, width)
+        right = grad_kv_ref[...].reshape(held * slots, 2 * width)
         acc_ref[...] += dot_tn(left, right)
 
-    @pl.when(cap == pl.num_programs(0) - 1)
+    @pl.when(step == pl.num_programs(0) - 1)
     def _():
         side = side_ref[0]
         own = pl.ds(pl.multiple_of(side * width, width), width)
@@ -553,24 +622,25 @@
     caps, slots, double = kv.shape
     width = double // 2
     length = queries.shape[1]
-    batch = 4 if caps % 4 == 0 else 1
-    block = lambda *shape: pl.BlockSpec((1,) + shape, lambda i, *_: (i, 0, 0))
+    held = 4 if caps % 4 == 0 else 1
+    batch = min(4, held)
+    block = lambda *shape: pl.BlockSpec((batch,) + shape, lambda i, *_: (i, 0, 0))
     sds = jax.ShapeDtypeStruct
     return pl.pallas_call(
         functools.partial(cross_back_body, short=short),
         grid_spec=pltpu.PrefetchScalarGridSpec(
             num_scalar_prefetch=2,
-            grid=(caps,),
+            grid=(caps // batch,),
             in_specs=[
                 block(slots, double), block(length, width), block(length, width),
                 block(GROUPS, LANES), block(GROUPS, LANES), whole(kv_mat.shape),
-                pl.BlockSpec((batch, slots, width), lambda i, *_: (i // batch, 0, 0)),
+                pl.BlockSpec((held, slots, width), lambda i, *_: (i // (held // batch), 0, 0)),
             ],
             out_specs=[
                 block(length, width), block(slots, width), whole((width, width)), whole((width, width)),
             ],
             scratch_shapes=[
-                pltpu.VMEM((batch, slots, double), BF16), pltpu.VMEM((width, double), F32),
+                pltpu.VMEM((held, slots, double), BF16), pltpu.VMEM((width, double), F32),
             ],
         ),
         out_shape=[
@@ -584,6 +654,17 @@
 
 def add_low(first, second):
     return (first.astype(F32) + second.astype(F32)).astype(BF16)
+
+
+def cut_blocks(target, value):
+    height = target.shape[-2]
+    count = len(target.shape) - 2
+    if height % 16 == 0:
+        target[...] = value.astype(BF16).reshape(target.shape)
+    else:
+        for i in range(1 << count):
+            lead = tuple((i >> (count - 1 - d)) % 2 for d in range(count))
+            target[lead] = value[i * height : (i + 1) * height].astype(BF16)
 
 
 class Piece:
@@ -686,11 +767,11 @@
     scratch = list(scratch)
     (
         send_sem, recv_sem, load_sem, back_one, back_two, hidden, grad_two, att, qkv, tok, qkv_mat,
-        out_mat, query_mat, back_sum, normed, low, grad_att, grad_qkv, acc, gains_all, gain_kv,
+        out_mat, query_mat, back_sum, normed, low, grad_att, grad_qkv, gains_all, gain_kv,
         gain_buf, gain_recv, qkv_mine, qkv_send, out_mine, out_send, query_mine, query_send,
         up_ref, down_ref,
-    ) = scratch[:31]
-    rest = scratch[31:]
+    ) = scratch[:30]
+    rest = scratch[30:]
     sums = Sums(send_sem, recv_sem)
     side = sums.side
     captions = back_one.shape[0]
@@ -780,21 +861,8 @@
 
     def weight(left, right, target, which):
         cols = target.shape[-1]
-        block = target.shape[-2]
         start = pl.multiple_of(which * cols, 128)
-        acc[:, :cols] = dot_tn(left[...], right[:, pl.ds(start, cols)])
-
-        def one(i, carry):
-            lead = tuple((i // (1 << (len(bits) - 1 - d))) % 2 for d in range(len(bits)))
-            span = pl.ds(i * block, block) if isinstance(i, int) else pl.ds(pl.multiple_of(i * block, 8), block)
-            target[lead] = acc[span, :cols].astype(BF16)
-            return carry
-
-        if block % 8 == 0:
-            lax.fori_loop(0, 1 << len(bits), one, 0)
-        else:
-            for i in range(1 << len(bits)):
-                one(i, 0)
+        cut_blocks(target, dot_tn(left[...], right[:, pl.ds(start, cols)]))
 
     def weights(left, right, mine, send, group):
         weight(left, right, send, 1 - side)
@@ -806,13 +874,13 @@
     loads[5].wait()
     loads[6].wait()
     weights(att, low, out_mine, out_send, pieces["out"])
-    for piece in middle:
+    for piece in early + image + middle:
         piece.advance()
 
     mask = same_head()
     causal = causal_mask(length)
 
-    def attend(cap, carry):
+    def attend(cap):
         span = pl.ds(pl.multiple_of(cap * length, length), length)
         for group in range(GROUPS):
             lo = group * LANES
@@ -832,11 +900,16 @@
             grad_qkv[span, 2 * width + lo : 2 * width + lo + LANES] = dot(
                 probs.astype(BF16), cot
             ).astype(BF16)
+
+    together = 2 if captions % 2 == 0 else 1
+
+    def attend_some(index, carry):
+        for cap in range(together):
+            attend(index * together + cap)
         return carry
 
-    lax.fori_loop(0, captions // 2, attend, 0)
-    lax.fori_loop(captions // 2, captions, attend, 0)
-    for piece in early:
+    lax.fori_loop(0, captions // together, attend_some, 0)
+    for piece in early + middle + image:
         piece.advance()
     loads[7].wait()
     loads[8].wait()
@@ -849,7 +922,7 @@
 
     lax.fori_loop(0, rows // tile, token_norm, 0)
     weights(normed, grad_qkv, qkv_mine, qkv_send, late)
-    for piece in late + image:
+    for piece in late + early + middle + image:
         piece.advance()
 
     def token_back(index, carry):
@@ -868,7 +941,7 @@
     gain_copy = sums.copy(gains_all.at[:, other_cols], gain_kv, {"kv": 1 - side})
     gain_copy.start()
     stage = -1
-    everything = early + image + middle + late
+    everything = late + early + image + middle
     while stage < len(bits) or not all(piece.pending is None for piece in everything):
         if stage < len(bits):
             gain_copy.wait()
@@ -911,7 +984,11 @@
     plan.append(("out", 0, width // 2, axes, turned(bits, 1), True))
     for by in range(3):
         plan.append(("kv", by * third, third, axes, turned(bits, by), True))
-        plan.append(("qkv", by * (width // 2), width // 2, axes, turned(bits, by), True))
+    col = 0
+    for cols in (width // 3, width // 6):
+        for by in range(3):
+            plan.append(("qkv", col, cols, axes, turned(bits, by), True))
+            col += cols
     heights = dict(up=up.shape[-2], down=down.shape[-2], cross=cross.shape[-2])
     buffers = []
     copies = 2 + len(bits)
@@ -942,7 +1019,7 @@
             low_rows(3 * width), low_rows(width), pltpu.VMEM(qkv_mat.shape, BF16),
             pltpu.VMEM(out_mat.shape, BF16), pltpu.VMEM(query_mat.shape, BF16),
             low_rows(width), low_rows(width), low_rows(width), low_rows(width), low_rows(3 * width),
-            pltpu.VMEM((width, 3 * width // 2), F32), pltpu.VMEM((8, width), F32),
+            pltpu.VMEM((8, width), F32),
             pltpu.VMEM((8, width // 2), F32), pltpu.VMEM((len(bits) + 1, 8, width // 2), F32),
             pltpu.VMEM((len(bits), 8, width // 2), F32),
             cut(3 * width // 2), cut(3 * width // 2), cut(width // 2), cut(width // 2),
@@ -958,21 +1035,25 @@
     )
 
 
-def hand_over_body(*refs):
-    count = len(refs) // 2
-    for source, target in zip(refs[:count], refs[count:]):
+def hand_over_body(gains_ref, *refs):
+    count = len(refs) // 2 - 3
+    for source, target in zip(refs[:count], refs[count : 2 * count]):
         target[...] = source[...]
-
-
-def hand_over(*arrays):
+    for index, target in enumerate(refs[2 * count :]):
+        target[...] = gains_ref[index : index + 1, :].reshape(target.shape)
+
+
+def hand_over(gains, *arrays):
     vmem = pl.BlockSpec(memory_space=pltpu.VMEM)
+    shapes = [jax.ShapeDtypeStruct(v.shape, v.dtype) for v in arrays]
+    shapes += [jax.ShapeDtypeStruct(gains.shape[1:], gains.dtype)] * 6
     return pl.pallas_call(
         hand_over_body,
-        in_specs=[vmem] * len(arrays),
-        out_specs=[vmem] * len(arrays),
-        out_shape=[jax.ShapeDtypeStruct(v.shape, v.dtype) for v in arrays],
+        in_specs=[vmem] * (1 + len(arrays)),
+        out_specs=[vmem] * len(shapes),
+        out_shape=shapes,
         name="hand_over",
-    )(*arrays)
+    )(gains, *arrays)
 
 
 def exchange(value, axis, bit, size):
@@ -998,20 +1079,13 @@
     cot = cotangent.reshape(captions * length, width)
     short = -(-SHORT // 16) * 16
     valid = jnp.clip(image_counts - side * slots, 0, slots)
-    swap = lambda v: exchange(v, "kv", 1, 2)
-
-    qkv, att, hidden, query = token_start(
+
+    qkv, att, hidden, queries = token_start(
         tok, norm1_gain, norm1_shift, self_qkv, self_out, norm2_gain,
         norm2_shift, cross_q, length,
     )
 
-    def both(own):
-        other = swap(own)
-        first = jnp.where(side == 0, own, other)
-        second = jnp.where(side == 0, other, own)
-        return jnp.concatenate([first, second], axis=0)
-
-    queries = both(query.reshape(captions, length, width))
+    queries = queries.reshape(caps, length, width)
     kv, part, lse_part = cross_start(valid, images, cross_kv, queries, short)
     (
         layer_out, grad_two, grads, lse, delta, up_keep, up_first, up_second, up_both, down_keep,
@@ -1036,13 +1110,14 @@
         cross_kv, images, short
     )
     cut = lambda v: split_rows(v, groups)
+    *sums, gains = end(
+        back, hidden, grad_two, att, qkv, tok, self_qkv, self_out, cross_q, norm1_gain, norm1_shift,
+        norm2_gain, norm2_shift, gain3, shift3, early, cut(kv_mine), cut(kv_send), length, groups,
+    )
     (
         tokens_grad, w_up_grad, down_grad, cross_out_grad, self_qkv_grad, self_out_grad, cross_q_grad,
-        cross_kv_grad, gains, layer_out,
-    ) = hand_over(*end(
-        back, hidden, grad_two, att, qkv, tok, self_qkv, self_out, cross_q, norm1_gain, norm1_shift,
-        norm2_gain, norm2_shift, gain3, shift3, early, cut(kv_mine), cut(kv_send), length, groups,
-    ), layer_out)
+        cross_kv_grad, layer_out, *gains,
+    ) = hand_over(gains, *sums, layer_out)
     return (
         layer_out.reshape(captions, length, width),
         tokens_grad.reshape(captions, length, width),

time: 230 us -> 215 us (0.935)
  Pallas kernels: 215 us -> 206 us
    pallas_call x1, Pallas kernels: 31.1 us -> 24.7 us  [cross_start(): pl.pallas_call(functools.partial(cross_start_body, short=short), grid_spe...]
    pallas_call x1, Pallas kernels: 54.2 us -> 50.8 us  [cross_back(): pl.pallas_call(functools.partial(cross_back_body, short=short), grid_spec...]
    pallas_call x1, Pallas kernels: 12.5 us -> 15 us  [token_start(): pl.pallas_call(functools.partial(token_start_body, length=length), grid=(...]
    ppermute x5 -> x4, starting transfers between devices: 4.43 us -> 5.16 us  [exchange(): return lax.ppermute(value, axis, [(i, i ^ bit) for i in range(size)])]
  transfers between devices with their start and end apart: 5 -> 4, of which waited for: 1 -> 0; matrix products, arithmetic and copies ran while one was open for 0% -> 0% of each run, Pallas kernels for 24% -> 24%
where the time goes in v6:
time: 215 us; the launch traced here: 213 us
  Pallas kernels  206 us (96%)
  starting transfers between devices  5.16 us (2%)
    pallas_call x1, Pallas kernels, end(): pl.pallas_call(functools.partial(end_body, plan=plan, bits=bits, length=l...  72.3 us
    pallas_call x1, Pallas kernels, cross_back(): pl.pallas_call(functools.partial(cross_back_body, short=short), grid_spec...  50.8 us
    pallas_call x1, Pallas kernels, feed(): pl.pallas_call(functools.partial(feed_body, length=length, tile=tile, bit...  39.6 us
    pallas_call x1, Pallas kernels, cross_start(): pl.pallas_call(functools.partial(cross_start_body, short=short), grid_spe...  24.7 us
    pallas_call x1, Pallas kernels, token_start(): pl.pallas_call(functools.partial(token_start_body, length=length), grid=(...  15 us
    ppermute x4, starting transfers between devices, exchange(): return lax.ppermute(value, axis, [(i, i ^ bit) for i in range(size)])  5.16 us
  transfers between devices with their start and end apart: 4, of which 0 were waited for; matrix products, arithmetic and copies ran while one was open for 0% of the time, Pallas kernels for 24%

profile of v6, /device:TPU:2, one launch (start us, length us, event | category | flops | bytes accessed | tf_op | source)
XLA Modules:
  0.0 213.1 jit_solution(4434423441589950291)
XLA Ops:
  0.6 1.2 subtract_clamp_fusion.valid_ref
  1.8 15.0 %token_start.1 = (bf16[512,2304]{1,0:T(8,128)(2,1)}, bf16[512,768]{1,0:T(8,128)(2,1)}, f32[512,768]{1,0:T(8,128)}, bf16[2,512,768]{2,1,0:T(8,128)(2,1)}) custom-call(bf16[512,768]{1,0:T(8,128)(2,1)} %bitcast.24, f32[768]{0:T(1024)} %gain_one.3, f32[768]{0:T(1024)} %shift_one.3, bf16[768,2304]{1,0:T(8,128)(2,1)} %qkv_mat_hbm.1, bf16[768,768]{1,0:T(8,128)(2,1)} %out_mat_hbm.1, ...), custom_call_target="tpu_custom_call" | custom-call | tf_op jit(solution)/shard_map/token_start/pallas_call | solution.py:173
  16.8 24.7 %cross_start.1 = (bf16[16,288,1536]{2,1,0:T(8,128)(2,1)}, bf16[16,64,768]{2,1,0:T(8,128)(2,1)}, f32[16,3,256]{2,1,0:T(4,128)}) custom-call(s32[16]{0:T(128)} %subtract_clamp_fusion.valid_ref, bf16[16,288,768]{2,1,0:T(8,128)(2,1)} %img_ref.3, bf16[768,1536]{1,0:T(8,128)(2,1)} %kv_mat.3, bf16[16,64,768]{2,1,0:T(8,128)(2,1)} %bitcast.21), custom_call_target="tpu_custom_call" | custom-call | tf_op jit(solution)/shard_map/cross_start/pallas_call | solution.py:256
  41.6 39.6 %feed.1 = (bf16[512,768]{1,0:T(8,128)(2,1)}, f32[512,768]{1,0:T(8,128)}, bf16[2,512,768]{2,1,0:T(8,128)(2,1)}, f32[2,8,3,256]{3,2,1,0:T(4,128)}, f32[2,8,3,256]{...) custom-call(bf16[2,512,768]{2,1,0:T(8,128)(2,1)} %bitcast.26, ...), custom_call_target="tpu_custom_call" | custom-call | tf_op jit(solution)/shard_map/feed/pallas_call | solution.py:497
  81.2 1.7 collective-permute-start.3
  82.9 0.5 collective-permute-start
  83.4 1.5 collective-permute-start.1
  84.9 1.4 collective-permute-start.2
  86.4 50.8 %cross_back.1 = (bf16[16,64,768]{2,1,0:T(8,128)(2,1)}, bf16[16,288,768]{2,1,0:T(8,128)(2,1)}, bf16[768,768]{1,0:T(8,128)(2,1)}, bf16[768,768]{1,0:T(8,128)(2,1)}) custom-call(s32[16]{0:T(128)} %subtract_clamp_fusion.valid_ref, s32[1]{0:T(128)} %bitcast.side_ref, bf16[16,288,1536]{2,1,0:T(8,128)(2,1)} %get-tuple-element.66.kv_ref, ...), custom_call_target="tpu_custom_call" | custom-call | tf_op jit(solution)/shard_map/cross_back/pallas_call | solution.py:629
  137.2 0.0 collective-permute-done
  137.2 0.0 collective-permute-done.1
  137.2 0.0 collective-permute-done.2
  137.2 0.0 collective-permute-done.3
  137.3 72.3 %end.1 = (bf16[512,768]{1,0:T(8,128)(2,1)}, f32[48,1536]{1,0:T(8,128)}, f32[192,384]{1,0:T(8,128)}, f32[48,384]{1,0:T(8,128)}, f32[48,1152]{1,0:T(8,128)}, /*ind...) custom-call(bf16[16,64,768]{2,1,0:T(8,128)(2,1)} %get-tuple-element.73.back_hbm, ...), custom_call_target="tpu_custom_call" | custom-call | tf_op jit(solution)/shard_map/end/pallas_call | solution.py:1009
  209.6 3.3 %hand_over.1 = (bf16[512,768]{1,0:T(8,128)(2,1)}, f32[48,1536]{1,0:T(8,128)}, f32[192,384]{1,0:T(8,128)}, f32[48,384]{1,0:T(8,128)}, f32[48,1152]{1,0:T(8,128)},...) custom-call(f32[8,384]{1,0:T(8,128)} %get-tuple-element.88.gains_ref, ...), custom_call_target="tpu_custom_call" | custom-call | tf_op jit(solution)/shard_map/hand_over/pallas_call | solution.py:1050
Async XLA Ops:
  81.2 56.0 %collective-permute-start.3 = (bf16[2,768,384]{2,1,0:T(8,128)(2,1)}, bf16[2,768,384]{2,1,0:T(8,128)(2,1)}, u32[]{:S(2)}, u32[]{:S(2)}) collective-permute-start(bf16[2,768,384]{2,1,0:T(8,128)(2,1)} %get-tuple-element.84), channel_id=1, source_target_pairs={{0,8},{2,10},{4,12},{6,14},{8,0},{10,2},{12,4},{14,6},{16,24},{18,... | collective-permute-start | bytes 3538952 | tf_op jit(solution)/shard_map/ppermute | solution.py:1060
  82.9 54.3 %collective-permute-start = (bf16[4,48,1536]{2,1,0:T(8,128)(2,1)}, bf16[4,48,1536]{2,1,0:T(8,128)(2,1)}, u32[]{:S(2)}, u32[]{:S(2)}) collective-permute-start(bf16[4,48,1536]{2,1,0:T(8,128)(2,1)} %get-tuple-element.80), channel_id=1, source_target_pairs={{0,2},{2,0},{4,6},{6,4},{8,10},{10,8},{12,14},{14,12},{16,18},{18,... | collective-permute-start | bytes 1769480 | tf_op jit(solution)/shard_map/ppermute | solution.py:1060
  83.4 53.8 %collective-permute-start.1 = (bf16[4,48,1536]{2,1,0:T(8,128)(2,1)}, bf16[4,48,1536]{2,1,0:T(8,128)(2,1)}, u32[]{:S(2)}, u32[]{:S(2)}) collective-permute-start(bf16[4,48,1536]{2,1,0:T(8,128)(2,1)} %get-tuple-element.81), channel_id=1, source_target_pairs={{0,4},{2,6},{4,0},{6,2},{8,12},{10,14},{12,8},{14,10},{16,20},{18,... | collective-permute-start | bytes 1769480 | tf_op jit(solution)/shard_map/ppermute | solution.py:1060
  84.9 52.3 %collective-permute-start.2 = (bf16[4,48,1536]{2,1,0:T(8,128)(2,1)}, bf16[4,48,1536]{2,1,0:T(8,128)(2,1)}, u32[]{:S(2)}, u32[]{:S(2)}) collective-permute-start(bf16[4,48,1536]{2,1,0:T(8,128)(2,1)} %get-tuple-element.82), channel_id=1, source_target_pairs={{0,6},{2,4},{4,2},{6,0},{8,14},{10,12},{12,10},{14,8},{16,22},{18,... | collective-permute-start | bytes 1769480 | tf_op jit(solution)/shard_map/ppermute | solution.py:1060

commit v7 on v6

--- a/solution.py
+++ b/solution.py
@@ -653,7 +653,7 @@
 
 
 def add_low(first, second):
-    return (first.astype(F32) + second.astype(F32)).astype(BF16)
+    return first + second
 
 
 def cut_blocks(target, value):
@@ -874,7 +874,7 @@
     loads[5].wait()
     loads[6].wait()
     weights(att, low, out_mine, out_send, pieces["out"])
-    for piece in early + image + middle:
+    for piece in middle + pieces["cross"] + pieces["up"]:
         piece.advance()
 
     mask = same_head()
@@ -908,8 +908,12 @@
             attend(index * together + cap)
         return carry
 
-    lax.fori_loop(0, captions // together, attend_some, 0)
-    for piece in early + middle + image:
+    rounds = captions // together
+    lax.fori_loop(0, rounds // 2, attend_some, 0)
+    for piece in image + pieces["down"]:
+        piece.advance()
+    lax.fori_loop(rounds // 2, rounds, attend_some, 0)
+    for piece in early + image + middle:
         piece.advance()
     loads[7].wait()
     loads[8].wait()
@@ -972,23 +976,17 @@
     lead = (2,) * len(bits)
     up_terms, down_terms, cross = early
     up, down = up_terms[0], down_terms[0]
-    cut_down = down.shape[-1] // 384 * 256
     third = width // 3
     plan = [("up", 0, up.shape[-1], axes[:-2], bits[2:], False)]
     down_axes = axes[:1] + axes[2:]
-    for col, cols, by in ((0, cut_down, 0), (cut_down, down.shape[-1] - cut_down, 1)):
-        order = [b for b in turned(bits, by) if b in down_axes]
-        plan.append(("down", col, cols, down_axes, order, False))
-    plan.append(("cross", 0, cross.shape[-1], axes, turned(bits, 2), False))
+    plan.append(("down", 0, down.shape[-1], down_axes, [b for b in bits if b in down_axes], False))
+    plan.append(("cross", 0, cross.shape[-1], axes, bits[1:2] + bits[:1] + bits[2:], False))
     plan.append(("query", 0, width // 2, axes, turned(bits, 0), True))
     plan.append(("out", 0, width // 2, axes, turned(bits, 1), True))
     for by in range(3):
         plan.append(("kv", by * third, third, axes, turned(bits, by), True))
-    col = 0
-    for cols in (width // 3, width // 6):
-        for by in range(3):
-            plan.append(("qkv", col, cols, axes, turned(bits, by), True))
-            col += cols
+    for by in range(3):
+        plan.append(("qkv", by * (width // 2), width // 2, axes, turned(bits, by), True))
     heights = dict(up=up.shape[-2], down=down.shape[-2], cross=cross.shape[-2])
     buffers = []
     copies = 2 + len(bits)

time: 215 us -> 213 us (level)
  Pallas kernels: 206 us -> 203 us
    pallas_call x1, Pallas kernels: 72.3 us -> 70 us  [end(): pl.pallas_call(functools.partial(end_body, plan=plan, bits=bits, length=l...]
where the time goes in v7:
time: 213 us; the launch traced here: 210 us
  Pallas kernels  203 us (95%)
  starting transfers between devices  5.17 us (2%)
    pallas_call x1, Pallas kernels, end(): pl.pallas_call(functools.partial(end_body, plan=plan, bits=bits, length=l...  70 us
    pallas_call x1, Pallas kernels, cross_back(): pl.pallas_call(functools.partial(cross_back_body, short=short), grid_spec...  50.8 us
    pallas_call x1, Pallas kernels, feed(): pl.pallas_call(functools.partial(feed_body, length=length, tile=tile, bit...  38.7 us
    pallas_call x1, Pallas kernels, cross_start(): pl.pallas_call(functools.partial(cross_start_body, short=short), grid_spe...  24.7 us
    pallas_call x1, Pallas kernels, token_start(): pl.pallas_call(functools.partial(token_start_body, length=length), grid=(...  15 us
    ppermute x4, starting transfers between devices, exchange(): return lax.ppermute(value, axis, [(i, i ^ bit) for i in range(size)])  5.17 us
  transfers between devices with their start and end apart: 4, of which 0 were waited for; matrix products, arithmetic and copies ran while one was open for 0% of the time, Pallas kernels for 24%

profile of v7, /device:TPU:2, one launch (start us, length us, event | category | flops | bytes accessed | tf_op | source)
XLA Modules:
  0.0 209.9 jit_solution(16232328327620442054)
XLA Ops:
  0.6 1.2 subtract_clamp_fusion.valid_ref
  1.8 15.0 %token_start.1 = (bf16[512,2304]{1,0:T(8,128)(2,1)}, bf16[512,768]{1,0:T(8,128)(2,1)}, f32[512,768]{1,0:T(8,128)}, bf16[2,512,768]{2,1,0:T(8,128)(2,1)}) custom-call(bf16[512,768]{1,0:T(8,128)(2,1)} %bitcast.24, f32[768]{0:T(1024)} %gain_one.3, f32[768]{0:T(1024)} %shift_one.3, bf16[768,2304]{1,0:T(8,128)(2,1)} %qkv_mat_hbm.1, bf16[768,768]{1,0:T(8,128)(2,1)} %out_mat_hbm.1, ...), custom_call_target="tpu_custom_call" | custom-call | tf_op jit(solution)/shard_map/token_start/pallas_call | solution.py:173
  16.8 24.7 %cross_start.1 = (bf16[16,288,1536]{2,1,0:T(8,128)(2,1)}, bf16[16,64,768]{2,1,0:T(8,128)(2,1)}, f32[16,3,256]{2,1,0:T(4,128)}) custom-call(s32[16]{0:T(128)} %subtract_clamp_fusion.valid_ref, bf16[16,288,768]{2,1,0:T(8,128)(2,1)} %img_ref.3, bf16[768,1536]{1,0:T(8,128)(2,1)} %kv_mat.3, bf16[16,64,768]{2,1,0:T(8,128)(2,1)} %bitcast.21), custom_call_target="tpu_custom_call" | custom-call | tf_op jit(solution)/shard_map/cross_start/pallas_call | solution.py:256
  41.6 38.7 %feed.1 = (bf16[512,768]{1,0:T(8,128)(2,1)}, f32[512,768]{1,0:T(8,128)}, bf16[2,512,768]{2,1,0:T(8,128)(2,1)}, f32[2,8,3,256]{3,2,1,0:T(4,128)}, f32[2,8,3,256]{...) custom-call(bf16[2,512,768]{2,1,0:T(8,128)(2,1)} %bitcast.26, ...), custom_call_target="tpu_custom_call" | custom-call | tf_op jit(solution)/shard_map/feed/pallas_call | solution.py:497
  80.2 1.7 collective-permute-start.3
  81.9 0.5 collective-permute-start
  82.4 1.5 collective-permute-start.1
  84.0 1.4 collective-permute-start.2
  85.4 50.8 %cross_back.1 = (bf16[16,64,768]{2,1,0:T(8,128)(2,1)}, bf16[16,288,768]{2,1,0:T(8,128)(2,1)}, bf16[768,768]{1,0:T(8,128)(2,1)}, bf16[768,768]{1,0:T(8,128)(2,1)}) custom-call(s32[16]{0:T(128)} %subtract_clamp_fusion.valid_ref, s32[1]{0:T(128)} %bitcast.side_ref, bf16[16,288,1536]{2,1,0:T(8,128)(2,1)} %get-tuple-element.66.kv_ref, ...), custom_call_target="tpu_custom_call" | custom-call | tf_op jit(solution)/shard_map/cross_back/pallas_call | solution.py:629
  136.2 0.0 collective-permute-done
  136.3 0.0 collective-permute-done.1
  136.3 0.0 collective-permute-done.2
  136.3 0.0 collective-permute-done.3
  136.3 70.0 %end.1 = (bf16[512,768]{1,0:T(8,128)(2,1)}, f32[48,1536]{1,0:T(8,128)}, f32[192,384]{1,0:T(8,128)}, f32[48,384]{1,0:T(8,128)}, f32[48,1152]{1,0:T(8,128)}, /*ind...) custom-call(bf16[16,64,768]{2,1,0:T(8,128)(2,1)} %get-tuple-element.73.back_hbm, ...), custom_call_target="tpu_custom_call" | custom-call | tf_op jit(solution)/shard_map/end/pallas_call | solution.py:1007
  206.3 3.3 %hand_over.1 = (bf16[512,768]{1,0:T(8,128)(2,1)}, f32[48,1536]{1,0:T(8,128)}, f32[192,384]{1,0:T(8,128)}, f32[48,384]{1,0:T(8,128)}, f32[48,1152]{1,0:T(8,128)},...) custom-call(f32[8,384]{1,0:T(8,128)} %get-tuple-element.88.gains_ref, ...), custom_call_target="tpu_custom_call" | custom-call | tf_op jit(solution)/shard_map/hand_over/pallas_call | solution.py:1048
Async XLA Ops:
  80.2 56.1 %collective-permute-start.3 = (bf16[2,768,384]{2,1,0:T(8,128)(2,1)}, bf16[2,768,384]{2,1,0:T(8,128)(2,1)}, u32[]{:S(2)}, u32[]{:S(2)}) collective-permute-start(bf16[2,768,384]{2,1,0:T(8,128)(2,1)} %get-tuple-element.84), channel_id=1, source_target_pairs={{0,8},{2,10},{4,12},{6,14},{8,0},{10,2},{12,4},{14,6},{16,24},{18,... | collective-permute-start | bytes 3538952 | tf_op jit(solution)/shard_map/ppermute | solution.py:1058
  81.9 54.3 %collective-permute-start = (bf16[4,48,1536]{2,1,0:T(8,128)(2,1)}, bf16[4,48,1536]{2,1,0:T(8,128)(2,1)}, u32[]{:S(2)}, u32[]{:S(2)}) collective-permute-start(bf16[4,48,1536]{2,1,0:T(8,128)(2,1)} %get-tuple-element.80), channel_id=1, source_target_pairs={{0,2},{2,0},{4,6},{6,4},{8,10},{10,8},{12,14},{14,12},{16,18},{18,... | collective-permute-start | bytes 1769480 | tf_op jit(solution)/shard_map/ppermute | solution.py:1058
  82.4 53.8 %collective-permute-start.1 = (bf16[4,48,1536]{2,1,0:T(8,128)(2,1)}, bf16[4,48,1536]{2,1,0:T(8,128)(2,1)}, u32[]{:S(2)}, u32[]{:S(2)}) collective-permute-start(bf16[4,48,1536]{2,1,0:T(8,128)(2,1)} %get-tuple-element.81), channel_id=1, source_target_pairs={{0,4},{2,6},{4,0},{6,2},{8,12},{10,14},{12,8},{14,10},{16,20},{18,... | collective-permute-start | bytes 1769480 | tf_op jit(solution)/shard_map/ppermute | solution.py:1058
  84.0 52.3 %collective-permute-start.2 = (bf16[4,48,1536]{2,1,0:T(8,128)(2,1)}, bf16[4,48,1536]{2,1,0:T(8,128)(2,1)}, u32[]{:S(2)}, u32[]{:S(2)}) collective-permute-start(bf16[4,48,1536]{2,1,0:T(8,128)(2,1)} %get-tuple-element.82), channel_id=1, source_target_pairs={{0,6},{2,4},{4,2},{6,0},{8,14},{10,12},{12,10},{14,8},{16,22},{18,... | collective-permute-start | bytes 1769480 | tf_op jit(solution)/shard_map/ppermute | solution.py:1058

commit v8 on v7

--- a/solution.py
+++ b/solution.py
@@ -375,21 +375,24 @@
         lax.fori_loop(0, tiles, one_tile, 0)
 
     slot = step % 2
-    up_mat = jnp.concatenate([up_one[...], up_two[...]], axis=1)
-    down_mat = down_ref[...].reshape(2 * sub, width)
-    pre = dot(normed_ref[...], up_mat)
-    cdf = 0.5 * (1.0 + lax.erf(pre * 0.7071067811865476))
-    act = (pre * cdf).astype(BF16)
-    acc_out[...] += dot(act, down_mat)
     cot = cot_ref[...]
-    density = jnp.exp(-0.5 * pre * pre) * 0.3989422804014327
-    grad_up = (dot_nt(cot, down_mat) * (cdf + pre * density)).astype(BF16)
-    acc_grad[...] += dot_nt(grad_up, up_mat)
-    grad_down = dot_tn(act, cot).astype(BF16)
-    grad_w = dot_tn(normed_ref[...], grad_up)
-    for part in range(2):
-        cut(up_pair.at[slot, part], grad_w[:, part * sub : (part + 1) * sub])
-        down_pair[slot, part] = grad_down[:, part * half : (part + 1) * half].reshape(2, sub, half)
+    pre = dot(normed_ref[...], up_one[...])
+    arrived = dot_nt(cot, down_ref[0])
+    for part, up_part in enumerate((up_one, up_two)):
+        now, came = pre, arrived
+        if part == 0:
+            pre = dot(normed_ref[...], up_two[...])
+            arrived = dot_nt(cot, down_ref[1])
+        cdf = 0.5 * (1.0 + lax.erf(now * 0.7071067811865476))
+        density = jnp.exp(-0.5 * now * now) * 0.3989422804014327
+        act = (now * cdf).astype(BF16)
+        grad_up = (came * (cdf + now * density)).astype(BF16)
+        acc_out[...] += dot(act, down_ref[part])
+        acc_grad[...] += dot_nt(grad_up, up_part[...])
+        grad_down = dot_tn(act, cot).astype(BF16)
+        cut(up_pair.at[slot, part], dot_tn(normed_ref[...], grad_up))
+        for side_part in range(2):
+            down_pair[slot, side_part, part] = grad_down[:, side_part * half : (side_part + 1) * half]
 
     def take(chunk, place):
         for copy in chunk_copies(place):

time: 213 us -> 212 us (level)
  no operation moved by 1% of the time
where the time goes in v8:
time: 212 us; the launch traced here: 209 us
  Pallas kernels  202 us (95%)
  starting transfers between devices  5.17 us (2%)
    pallas_call x1, Pallas kernels, end(): pl.pallas_call(functools.partial(end_body, plan=plan, bits=bits, length=l...  70 us
    pallas_call x1, Pallas kernels, cross_back(): pl.pallas_call(functools.partial(cross_back_body, short=short), grid_spec...  50.8 us
    pallas_call x1, Pallas kernels, feed(): pl.pallas_call(functools.partial(feed_body, length=length, tile=tile, bit...  38 us
    pallas_call x1, Pallas kernels, cross_start(): pl.pallas_call(functools.partial(cross_start_body, short=short), grid_spe...  24.7 us
    pallas_call x1, Pallas kernels, token_start(): pl.pallas_call(functools.partial(token_start_body, length=length), grid=(...  15 us
    ppermute x4, starting transfers between devices, exchange(): return lax.ppermute(value, axis, [(i, i ^ bit) for i in range(size)])  5.17 us
  transfers between devices with their start and end apart: 4, of which 0 were waited for; matrix products, arithmetic and copies ran while one was open for 0% of the time, Pallas kernels for 24%

profile of v8, /device:TPU:2, one launch (start us, length us, event | category | flops | bytes accessed | tf_op | source)
XLA Modules:
  0.0 209.2 jit_solution(1719081696488379299)
XLA Ops:
  0.6 1.2 subtract_clamp_fusion.valid_ref
  1.8 15.0 %token_start.1 = (bf16[512,2304]{1,0:T(8,128)(2,1)}, bf16[512,768]{1,0:T(8,128)(2,1)}, f32[512,768]{1,0:T(8,128)}, bf16[2,512,768]{2,1,0:T(8,128)(2,1)}) custom-call(bf16[512,768]{1,0:T(8,128)(2,1)} %bitcast.24, f32[768]{0:T(1024)} %gain_one.3, f32[768]{0:T(1024)} %shift_one.3, bf16[768,2304]{1,0:T(8,128)(2,1)} %qkv_mat_hbm.1, bf16[768,768]{1,0:T(8,128)(2,1)} %out_mat_hbm.1, ...), custom_call_target="tpu_custom_call" | custom-call | tf_op jit(solution)/shard_map/token_start/pallas_call | solution.py:173
  16.8 24.7 %cross_start.1 = (bf16[16,288,1536]{2,1,0:T(8,128)(2,1)}, bf16[16,64,768]{2,1,0:T(8,128)(2,1)}, f32[16,3,256]{2,1,0:T(4,128)}) custom-call(s32[16]{0:T(128)} %subtract_clamp_fusion.valid_ref, bf16[16,288,768]{2,1,0:T(8,128)(2,1)} %img_ref.3, bf16[768,1536]{1,0:T(8,128)(2,1)} %kv_mat.3, bf16[16,64,768]{2,1,0:T(8,128)(2,1)} %bitcast.21), custom_call_target="tpu_custom_call" | custom-call | tf_op jit(solution)/shard_map/cross_start/pallas_call | solution.py:256
  41.6 38.0 %feed.1 = (bf16[512,768]{1,0:T(8,128)(2,1)}, f32[512,768]{1,0:T(8,128)}, bf16[2,512,768]{2,1,0:T(8,128)(2,1)}, f32[2,8,3,256]{3,2,1,0:T(4,128)}, f32[2,8,3,256]{...) custom-call(bf16[2,512,768]{2,1,0:T(8,128)(2,1)} %bitcast.26, ...), custom_call_target="tpu_custom_call" | custom-call | tf_op jit(solution)/shard_map/feed/pallas_call | solution.py:500
  79.6 1.7 collective-permute-start.3
  81.2 0.5 collective-permute-start
  81.8 1.5 collective-permute-start.1
  83.3 1.4 collective-permute-start.2
  84.7 50.8 %cross_back.1 = (bf16[16,64,768]{2,1,0:T(8,128)(2,1)}, bf16[16,288,768]{2,1,0:T(8,128)(2,1)}, bf16[768,768]{1,0:T(8,128)(2,1)}, bf16[768,768]{1,0:T(8,128)(2,1)}) custom-call(s32[16]{0:T(128)} %subtract_clamp_fusion.valid_ref, s32[1]{0:T(128)} %bitcast.side_ref, bf16[16,288,1536]{2,1,0:T(8,128)(2,1)} %get-tuple-element.66.kv_ref, ...), custom_call_target="tpu_custom_call" | custom-call | tf_op jit(solution)/shard_map/cross_back/pallas_call | solution.py:632
  135.6 0.0 collective-permute-done
  135.6 0.0 collective-permute-done.1
  135.6 0.0 collective-permute-done.2
  135.6 0.0 collective-permute-done.3
  135.6 70.0 %end.1 = (bf16[512,768]{1,0:T(8,128)(2,1)}, f32[48,1536]{1,0:T(8,128)}, f32[192,384]{1,0:T(8,128)}, f32[48,384]{1,0:T(8,128)}, f32[48,1152]{1,0:T(8,128)}, /*ind...) custom-call(bf16[16,64,768]{2,1,0:T(8,128)(2,1)} %get-tuple-element.73.back_hbm, ...), custom_call_target="tpu_custom_call" | custom-call | tf_op jit(solution)/shard_map/end/pallas_call | solution.py:1010
  205.7 3.3 %hand_over.1 = (bf16[512,768]{1,0:T(8,128)(2,1)}, f32[48,1536]{1,0:T(8,128)}, f32[192,384]{1,0:T(8,128)}, f32[48,384]{1,0:T(8,128)}, f32[48,1152]{1,0:T(8,128)},...) custom-call(f32[8,384]{1,0:T(8,128)} %get-tuple-element.88.gains_ref, ...), custom_call_target="tpu_custom_call" | custom-call | tf_op jit(solution)/shard_map/hand_over/pallas_call | solution.py:1051
Async XLA Ops:
  79.6 56.0 %collective-permute-start.3 = (bf16[2,768,384]{2,1,0:T(8,128)(2,1)}, bf16[2,768,384]{2,1,0:T(8,128)(2,1)}, u32[]{:S(2)}, u32[]{:S(2)}) collective-permute-start(bf16[2,768,384]{2,1,0:T(8,128)(2,1)} %get-tuple-element.84), channel_id=1, source_target_pairs={{0,8},{2,10},{4,12},{6,14},{8,0},{10,2},{12,4},{14,6},{16,24},{18,... | collective-permute-start | bytes 3538952 | tf_op jit(solution)/shard_map/ppermute | solution.py:1061
  81.2 54.3 %collective-permute-start = (bf16[4,48,1536]{2,1,0:T(8,128)(2,1)}, bf16[4,48,1536]{2,1,0:T(8,128)(2,1)}, u32[]{:S(2)}, u32[]{:S(2)}) collective-permute-start(bf16[4,48,1536]{2,1,0:T(8,128)(2,1)} %get-tuple-element.80), channel_id=1, source_target_pairs={{0,2},{2,0},{4,6},{6,4},{8,10},{10,8},{12,14},{14,12},{16,18},{18,... | collective-permute-start | bytes 1769480 | tf_op jit(solution)/shard_map/ppermute | solution.py:1061
  81.8 53.8 %collective-permute-start.1 = (bf16[4,48,1536]{2,1,0:T(8,128)(2,1)}, bf16[4,48,1536]{2,1,0:T(8,128)(2,1)}, u32[]{:S(2)}, u32[]{:S(2)}) collective-permute-start(bf16[4,48,1536]{2,1,0:T(8,128)(2,1)} %get-tuple-element.81), channel_id=1, source_target_pairs={{0,4},{2,6},{4,0},{6,2},{8,12},{10,14},{12,8},{14,10},{16,20},{18,... | collective-permute-start | bytes 1769480 | tf_op jit(solution)/shard_map/ppermute | solution.py:1061
  83.3 52.3 %collective-permute-start.2 = (bf16[4,48,1536]{2,1,0:T(8,128)(2,1)}, bf16[4,48,1536]{2,1,0:T(8,128)(2,1)}, u32[]{:S(2)}, u32[]{:S(2)}) collective-permute-start(bf16[4,48,1536]{2,1,0:T(8,128)(2,1)} %get-tuple-element.82), channel_id=1, source_target_pairs={{0,6},{2,4},{4,2},{6,0},{8,14},{10,12},{12,10},{14,8},{16,22},{18,... | collective-permute-start | bytes 1769480 | tf_op jit(solution)/shard_map/ppermute | solution.py:1061
